TPU v7x, 32 devices: a whole 2x2x4 slice. The times are simulated.
32 devices in a mesh: dp: 16 (over z, x, core), tensor: 2 (over y).
Axes of the slice: x: 2, y: 2, z: 4, core: 2. Of those that a mesh axis runs over, the one named last changes fastest.
Arguments:
- inputs: bfloat16 [6272, 512], P('dp'), may hold values from -6 to 6
- ln1_gain: float32 [512], replicated, may hold values from 0.5 to 1.5
- ln1_shift: float32 [512], replicated, may hold values from -3 to 3
- w_qkv: bfloat16 [512, 3, 512], P(None, None, 'tensor'), may hold values from -0.25 to 0.25
- qv_bias: float32 [2, 512], P(None, 'tensor'), may hold values from -3 to 3
- bias_table: float32 [169, 16], P(None, 'tensor'), may hold values from -6 to 320
- rel_index: int32 [49, 49], replicated, may hold values from 0 to 168
- regions: int32 [196], replicated, may hold values from 0 to 8
- w_proj: bfloat16 [512, 512], P('tensor'), may hold values from -0.5 to 0.5
- proj_bias: float32 [512], replicated, may hold values from -3 to 3
- ln2_gain: float32 [512], replicated, may hold values from 0.5 to 1.5
- ln2_shift: float32 [512], replicated, may hold values from -3 to 3
- w_fc1: bfloat16 [512, 2048], P(None, 'tensor'), may hold values from -0.25 to 0.25
- fc1_bias: float32 [2048], P('tensor'), may hold values from -3 to 3
- w_fc2: bfloat16 [2048, 512], P('tensor'), may hold values from -0.1875 to 0.1875
- fc2_bias: float32 [512], replicated, may hold values from -3 to 3
- grad_output: bfloat16 [6272, 512], P('dp'), may hold values from -12 to 12
Outputs:
- output: bfloat16 [6272, 512], P('dp')
- grad_input: float32 [6272, 512], P('dp')
- grad_ln1_gain: float32 [512], replicated
- grad_ln1_shift: float32 [512], replicated
- grad_qkv: float32 [512, 3, 512], P(None, None, 'tensor')
- grad_qv_bias: float32 [2, 512], P(None, 'tensor')
- grad_table: float32 [169, 16], P(None, 'tensor')
- grad_proj: float32 [512, 512], P('tensor')
- grad_proj_bias: float32 [512], replicated
- grad_ln2_gain: float32 [512], replicated
- grad_ln2_shift: float32 [512], replicated
- grad_fc1: float32 [512, 2048], P(None, 'tensor')
- grad_fc1_bias: float32 [2048], P('tensor')
- grad_fc2: float32 [2048, 512], P('tensor')
- grad_fc2_bias: float32 [512], replicated
All inputs are finite; a program needn't handle non-finite values.
Results may differ from a plain program's by a relative error of at most 0.017.
Values may be sent and summed in bfloat16 or wider, within the bound.
No kernel may reach another device: no remote copies, remote signals or barrier semaphores. Data moves between devices by JAX's collectives and lax.ppermute only.
A program may use at most 64 MiB of HBM per device.

v0:
```python
import jax
import jax.numpy as jnp
from jax import lax
from jax.sharding import PartitionSpec as P

HEAD_DIM = 32
SIDE = 14
WIN = 7
SHIFT = 3


NORM_EPS = 1e-05
MASKED = -1e30


def layer_norm(values, norm_gain, norm_shift):
    centered = values - jnp.mean(values, axis=-1, keepdims=True)
    inverse = lax.rsqrt(jnp.mean(centered * centered, axis=-1, keepdims=True) + NORM_EPS)
    normed = centered * inverse
    return (normed * norm_gain + norm_shift, normed, inverse)


def norm_backward(upstream, normed, inverse, norm_gain):
    weighted = upstream * norm_gain
    return inverse * (
        weighted
        - jnp.mean(weighted, axis=-1, keepdims=True)
        - normed * jnp.mean(weighted * normed, axis=-1, keepdims=True)
    )


def gelu_exact(hidden):
    return 0.5 * hidden * (1.0 + jax.scipy.special.erf(hidden * 0.7071067811865476))


def gelu_slope(hidden):
    return (
        0.5 * (1.0 + jax.scipy.special.erf(hidden * 0.7071067811865476))
        + hidden * jnp.exp(-0.5 * hidden * hidden) * 0.3989422804014327
    )


def to_windows(tensor, images):
    heads_here = tensor.shape[1]
    head_depth = tensor.shape[2]
    across = SIDE // WIN
    layout = tensor.reshape(images, SIDE, SIDE, heads_here, head_depth)
    layout = jnp.roll(layout, (-SHIFT, -SHIFT), axis=(1, 2))
    layout = layout.reshape(images, across, WIN, across, WIN, heads_here, head_depth).transpose(
        0, 1, 3, 5, 2, 4, 6
    )
    return layout.reshape(images * across * across, heads_here, WIN * WIN, head_depth)


def from_windows(tensor, images):
    heads_here = tensor.shape[1]
    head_depth = tensor.shape[3]
    across = SIDE // WIN
    layout = tensor.reshape(images, across, across, heads_here, WIN, WIN, head_depth).transpose(
        0, 1, 4, 2, 5, 3, 6
    )
    layout = jnp.roll(
        layout.reshape(images, SIDE, SIDE, heads_here, head_depth), (SHIFT, SHIFT), axis=(1, 2)
    )
    return layout.reshape(images * SIDE * SIDE, heads_here * head_depth)


def window_scores(queries, keys_win, rel_bias, allowed, images):
    raw_scores = jnp.einsum(
        "whie,whje->whij", queries, keys_win, preferred_element_type=jnp.float32
    )
    layout = (
        raw_scores.reshape((images, allowed.shape[0]) + raw_scores.shape[1:]) + rel_bias[None, None]
    )
    return jnp.where(allowed[None, :, None], layout, MASKED)


def local(
    inputs,
    ln1_gain,
    ln1_shift,
    w_qkv,
    qv_bias,
    bias_table,
    rel_index,
    regions,
    w_proj,
    proj_bias,
    ln2_gain,
    ln2_shift,
    w_fc1,
    fc1_bias,
    w_fc2,
    fc2_bias,
    grad_output,
):
    tokens_here = inputs.shape[0]
    width = inputs.shape[1]
    images = tokens_here // (SIDE * SIDE)
    inner = w_qkv.shape[2]
    heads_here = inner // HEAD_DIM
    q_factor = HEAD_DIM ** (-0.5)
    across = SIDE // WIN
    positions = WIN * WIN
    residual_in = inputs.astype(jnp.float32)
    normed_one, unit_one, inverse_one = layer_norm(residual_in, ln1_gain, ln1_shift)
    normed_one_b = normed_one.astype(jnp.bfloat16)
    qkv_weight = w_qkv.reshape(width, 3 * inner)
    projected = jnp.dot(normed_one_b, qkv_weight, preferred_element_type=jnp.float32).reshape(
        tokens_here, 3, inner
    )
    queries = ((projected[:, 0] + qv_bias[0]) * q_factor).astype(jnp.bfloat16)
    keys_tok = projected[:, 1].astype(jnp.bfloat16)
    values_tok = (projected[:, 2] + qv_bias[1]).astype(jnp.bfloat16)
    query_win = to_windows(queries.reshape(tokens_here, heads_here, HEAD_DIM), images)
    key_win = to_windows(keys_tok.reshape(tokens_here, heads_here, HEAD_DIM), images)
    value_win = to_windows(values_tok.reshape(tokens_here, heads_here, HEAD_DIM), images)
    region_win = (
        regions.reshape(across, WIN, across, WIN)
        .transpose(0, 2, 1, 3)
        .reshape(across * across, positions)
    )
    allowed = region_win[:, :, None] == region_win[:, None, :]
    one_hot = (
        rel_index.reshape(-1)[:, None] == jnp.arange(bias_table.shape[0], dtype=jnp.int32)[None, :]
    ).astype(jnp.float32)
    rel_bias = jnp.dot(one_hot, bias_table, precision=lax.Precision.HIGHEST).T.reshape(
        heads_here, positions, positions
    )
    scores = window_scores(query_win, key_win, rel_bias, allowed, images)
    top_score = jnp.max(scores, axis=-1, keepdims=True)
    log_total = top_score + jnp.log(jnp.sum(jnp.exp(scores - top_score), axis=-1, keepdims=True))
    prob_b = (
        jnp.exp(scores - log_total)
        .astype(jnp.bfloat16)
        .reshape(-1, heads_here, positions, positions)
    )
    mixed = jnp.einsum("whij,whje->whie", prob_b, value_win, preferred_element_type=jnp.float32)
    mixed_tok = from_windows(mixed.astype(jnp.bfloat16), images)
    attn_part = jnp.dot(mixed_tok, w_proj, preferred_element_type=jnp.float32)
    attn_total = lax.psum(attn_part.astype(jnp.bfloat16), "tensor").astype(jnp.float32)
    hidden_res = residual_in + attn_total + proj_bias
    normed_two, unit_two, inverse_two = layer_norm(hidden_res, ln2_gain, ln2_shift)
    normed_two_b = normed_two.astype(jnp.bfloat16)
    pre_act = jnp.dot(normed_two_b, w_fc1, preferred_element_type=jnp.float32) + fc1_bias
    activ_b = gelu_exact(pre_act).astype(jnp.bfloat16)
    mlp_part = jnp.dot(activ_b, w_fc2, preferred_element_type=jnp.float32)
    mlp_total = lax.psum(mlp_part.astype(jnp.bfloat16), "tensor").astype(jnp.float32)
    output = (hidden_res + mlp_total + fc2_bias).astype(jnp.bfloat16)
    upstream = grad_output.astype(jnp.float32)
    grad_fc2_bias = jnp.sum(upstream, axis=0)
    grad_fc2 = jnp.dot(activ_b.T, grad_output, preferred_element_type=jnp.float32)
    grad_act = jnp.dot(grad_output, w_fc2.T, preferred_element_type=jnp.float32)
    grad_pre = grad_act * gelu_slope(pre_act)
    grad_pre_b = grad_pre.astype(jnp.bfloat16)
    grad_fc1_bias = jnp.sum(grad_pre, axis=0)
    grad_fc1 = jnp.dot(normed_two_b.T, grad_pre_b, preferred_element_type=jnp.float32)
    back_two_part = jnp.dot(grad_pre_b, w_fc1.T, preferred_element_type=jnp.float32)
    back_two = lax.psum(back_two_part.astype(jnp.bfloat16), "tensor").astype(jnp.float32)
    grad_ln2_gain = jnp.sum(back_two * unit_two, axis=0)
    grad_ln2_shift = jnp.sum(back_two, axis=0)
    mlp_sums = (grad_ln2_gain, grad_ln2_shift, grad_fc1, grad_fc1_bias, grad_fc2, grad_fc2_bias)
    grad_hidden = upstream + norm_backward(back_two, unit_two, inverse_two, ln2_gain)
    grad_hidden_b = grad_hidden.astype(jnp.bfloat16)
    grad_proj_bias = jnp.sum(grad_hidden, axis=0)
    grad_proj = jnp.dot(mixed_tok.T, grad_hidden_b, preferred_element_type=jnp.float32)
    grad_mixed = jnp.dot(grad_hidden_b, w_proj.T, preferred_element_type=jnp.float32).astype(
        jnp.bfloat16
    )
    grad_mixed_win = to_windows(grad_mixed.reshape(tokens_here, heads_here, HEAD_DIM), images)
    scores_again = window_scores(query_win, key_win, rel_bias, allowed, images)
    prob_again = jnp.exp(scores_again - log_total)
    prob_again_b = prob_again.astype(jnp.bfloat16).reshape(-1, heads_here, positions, positions)
    grad_prob = jnp.einsum(
        "whie,whje->whij", grad_mixed_win, value_win, preferred_element_type=jnp.float32
    ).reshape(prob_again.shape)
    row_dot = jnp.sum(prob_again * grad_prob, axis=-1, keepdims=True)
    grad_score = prob_again * (grad_prob - row_dot)
    summed_scores = jnp.sum(grad_score, axis=(0, 1)).reshape(heads_here, positions * positions)
    grad_table = jnp.dot(one_hot.T, summed_scores.T, precision=lax.Precision.HIGHEST)
    grad_score_b = grad_score.astype(jnp.bfloat16).reshape(-1, heads_here, positions, positions)
    grad_query_win = (
        jnp.einsum("whij,whje->whie", grad_score_b, key_win, preferred_element_type=jnp.float32)
        * q_factor
    )
    grad_key_win = jnp.einsum(
        "whij,whie->whje", grad_score_b, query_win, preferred_element_type=jnp.float32
    )
    grad_value_win = jnp.einsum(
        "whij,whie->whje", prob_again_b, grad_mixed_win, preferred_element_type=jnp.float32
    )
    grad_query = from_windows(grad_query_win, images)
    grad_key = from_windows(grad_key_win, images)
    grad_value = from_windows(grad_value_win, images)
    grad_qv_bias = jnp.stack([jnp.sum(grad_query, axis=0), jnp.sum(grad_value, axis=0)])
    grad_three = (
        jnp.stack([grad_query, grad_key, grad_value], axis=1)
        .astype(jnp.bfloat16)
        .reshape(tokens_here, 3 * inner)
    )
    grad_qkv = jnp.dot(normed_one_b.T, grad_three, preferred_element_type=jnp.float32).reshape(
        width, 3, inner
    )
    back_one_part = jnp.dot(grad_three, qkv_weight.T, preferred_element_type=jnp.float32)
    back_one = lax.psum(back_one_part.astype(jnp.bfloat16), "tensor").astype(jnp.float32)
    grad_ln1_gain = jnp.sum(back_one * unit_one, axis=0)
    grad_ln1_shift = jnp.sum(back_one, axis=0)
    grad_input = grad_hidden + norm_backward(back_one, unit_one, inverse_one, ln1_gain)
    total_grads = tuple(
        lax.psum(
            (
                grad_ln1_gain,
                grad_ln1_shift,
                grad_qkv,
                grad_qv_bias,
                grad_table,
                grad_proj,
                grad_proj_bias,
                mlp_sums[0],
                mlp_sums[1],
                mlp_sums[2],
                mlp_sums[3],
                mlp_sums[4],
                mlp_sums[5],
            ),
            "dp",
        )
    )
    return (output, grad_input) + total_grads


def solution(mesh):
    return jax.shard_map(
        local,
        mesh=mesh,
        in_specs=(
            P("dp", None),
            P(),
            P(),
            P(None, None, "tensor"),
            P(None, "tensor"),
            P(None, "tensor"),
            P(),
            P(),
            P("tensor", None),
            P(),
            P(),
            P(),
            P(None, "tensor"),
            P("tensor"),
            P("tensor", None),
            P(),
            P("dp", None),
        ),
        out_specs=(
            P("dp", None),
            P("dp", None),
            P(),
            P(),
            P(None, None, "tensor"),
            P(None, "tensor"),
            P(None, "tensor"),
            P("tensor", None),
            P(),
            P(),
            P(),
            P(None, "tensor"),
            P("tensor"),
            P("tensor", None),
            P(),
        ),
        check_vma=False,
    )
```

profile of v0, /device:TPU:0, one launch (start us, length us, event | category | flops | bytes accessed | tf_op | source)
XLA Modules:
  0.0 338.9 jit_solution(2142861799854349741)
XLA Ops:
  9.8 1.4 copy.96
  14.7 1.4 squeeze.7
  24.2 1.4 copy.99
  25.6 2.0 fusion.72
  29.9 2.4 copy.104
  32.3 2.2 convolution_convert_fusion
  34.5 2.4 copy.105
  39.3 1.7 reshape.250
  41.1 2.0 convolution_convert_fusion.3
  43.4 28.6 %all-reduce.8.cloned.1.call-done = bf16[392,512]{1,0:T(8,128)(2,1)} async-done(((bf16[392,512]{1,0:T(8,128)(2,1)}), bf16[392,512]{1,0:T(8,128)(2,1)}) %all-reduce.8.cloned.1.call-update) | async-done | bytes 401424 | tf_op jit(solution)/shard_map/psum | solution.py:141
  74.7 1.8 multiply_convert_fusion
  76.5 1.6 fusion.73
  78.9 1.4 convolution_convert_fusion.1
  80.4 2.9 convolution_convert_fusion.2
  83.3 2.2 fusion.52
  85.6 21.0 %all-reduce.10.cloned.1.call-done = bf16[392,512]{1,0:T(8,128)(2,1)} async-done(((bf16[392,512]{1,0:T(8,128)(2,1)}), bf16[392,512]{1,0:T(8,128)(2,1)}) %all-reduce.10.cloned.1.call-update) | async-done | bytes 401424 | tf_op jit(solution)/shard_map/psum | solution.py:159
  106.6 2.2 fusion.32
  108.8 2.3 fusion.65
  116.0 2.4 copy.108
  118.4 2.6 fusion.56
  121.0 3.0 copy.120
  124.1 1.5 copy.121
  133.5 1.9 copy.112
  142.6 2.5 fusion.8
  145.5 2.1 fusion.74
  148.7 1.9 fusion.45
  152.9 27.3 %all-reduce.14.cloned.1.call-done = (bf16[392,512]{1,0:T(8,128)(2,1)}, bf16[392,512]{1,0:T(8,128)(2,1)}) async-done(((bf16[392,512]{1,0:T(8,128)(2,1)}, bf16[392,512]{1,0:T(8,128)(2,1)}), (bf16[392,512]{1,0:T(8,128)(2,1)}, bf16[392,512]{1,0:T(8,128)(2,1)})) %all-reduce.14.cloned.1.call-update) | async-done | bytes 802832 | tf_op jit(solution)/shard_map/psum | solution.py:148
  180.2 1.5 fusion.33
  181.8 63.3 %all-reduce = (f32[512]{0:T(512)}, f32[512]{0:T(512)}, f32[2,256]{1,0:T(2,128)}, f32[169,8]{0,1:T(8,128)}, f32[512]{0:T(512)}, /*index=5*/f32[512]{0:T(512)}, f32[512]{0:T(512)}, f32[1024]{0:T(1024)}, f32[512]{0:T(512)}) all-reduce(f32[512]{0:T(512)S(1)} %get-tuple-element.17, ...), channel_id=1, replica_groups=mesh['dp'=16,'tensor'=2] {'dp'}, use_global_device_ids=true, to_apply=%region_16.17 | all-reduce | flops 5960 | bytes 47680 | tf_op jit(solution)/shard_map/psum | solution.py:210
  245.1 2.6 fusion.25
  247.7 77.4 %all-reduce.12.cloned.1.call-done = (f32[512,3,256]{2,0,1:T(8,128)}, f32[256,512]{1,0:T(8,128)}, f32[512,1024]{1,0:T(8,128)}, f32[1024,512]{1,0:T(8,128)}) async-done(((f32[512,3,256]{2,0,1:T(8,128)}, f32[256,512]{1,0:T(8,128)}, f32[512,1024]{1,0:T(8,128)}, f32[1024,512]{1,0:T(8,128)}), (f32[512,3,256]{2,0,1:T(8,128)}, f32[256,512]{1,0:T(8,128)}, f32[512,1024]{1,0:T(8,128)}, ...) | async-done | bytes 6291472 | tf_op jit(solution)/shard_map/psum | solution.py:210
  325.1 2.8 copy.146
  (221 shorter events, 50.3 us)
Async XLA Ops:
  7.2 67.4 %copy-start = (bf16[512,1024]{1,0:T(8,128)(2,1)S(1)}, bf16[512,1024]{1,0:T(8,128)(2,1)}, u32[]{:S(2)}) copy-start(bf16[512,1024]{1,0:T(8,128)(2,1)} %param.29) | copy-start | bytes 3145732
  7.2 4.0 %copy-start.2 = (bf16[392,512]{1,0:T(8,128)(2,1)S(1)}, bf16[392,512]{1,0:T(8,128)(2,1)}, u32[]{:S(2)}) copy-start(bf16[392,512]{1,0:T(8,128)(2,1)} %param.17) | copy-start | bytes 1204228
  7.2 4.0 %copy-start.42 = (f32[512]{0:T(512)S(1)}, f32[512]{0:T(512)}, u32[]{:S(2)}) copy-start(f32[512]{0:T(512)} %param.18) | copy-start | bytes 6148
  7.2 4.0 %copy-start.56 = (f32[512]{0:T(512)S(1)}, f32[512]{0:T(512)}, u32[]{:S(2)}) copy-start(f32[512]{0:T(512)} %param.19) | copy-start | bytes 6148
  7.2 64.8 %all-reduce.8.cloned.1.call-start = ((), (), s32[]{:S(2)}) async-start(), calls=%async_computation | async-start | bytes 802816 | tf_op jit(solution)/shard_map/psum | solution.py:141
  18.4 3.6 %copy-start.8 = (bf16[2,11,14,8,32]{4,3,2,1,0:T(8,128)(2,1)S(1)}, bf16[2,11,14,8,32]{4,3,2,1,0:T(8,128)(2,1)}, u32[]{:S(2)}) copy-start(bf16[2,11,14,8,32]{4,3,2,1,0:T(8,128)(2,1)} %slice.167) | copy-start | bytes 473092
  18.4 3.6 %copy-start.22 = (bf16[2,3,14,8,32]{4,3,2,1,0:T(8,128)(2,1)S(1)}, bf16[2,3,14,8,32]{4,3,2,1,0:T(8,128)(2,1)}, u32[]{:S(2)}) copy-start(bf16[2,3,14,8,32]{4,3,2,1,0:T(8,128)(2,1)} %slice.168) | copy-start | bytes 129028
  28.6 3.7 %copy-start.26 = (f32[8,8,49]{2,1,0:T(8,128)}, f32[8,8,49]{2,1,0:T(8,128)S(1)}, u32[]{:S(2)}) copy-start(f32[8,8,49]{2,1,0:T(8,128)S(1)} %log_add_fusion) | copy-start | bytes 37636
  38.2 33.8 %copy-start.32 = (f32[512]{0:T(512)S(1)}, f32[512]{0:T(512)}, u32[]{:S(2)}) copy-start(f32[512]{0:T(512)} %param.26) | copy-start | bytes 6148
  41.0 35.4 %copy-start.18 = (bf16[392,256]{1,0:T(8,128)(2,1)}, bf16[392,256]{1,0:T(8,128)(2,1)S(1)}, u32[]{:S(2)}) copy-start(bf16[392,256]{1,0:T(8,128)(2,1)S(1)} %reshape.250) | copy-start | bytes 602116
  41.1 33.6 %copy-start.40 = (f32[512]{0:T(512)S(1)}, f32[512]{0:T(512)}, u32[]{:S(2)}) copy-start(f32[512]{0:T(512)} %param.27) | copy-start | bytes 6148
  41.1 33.6 %copy-start.54 = (f32[1024]{0:T(1024)S(1)}, f32[1024]{0:T(1024)}, u32[]{:S(2)}) copy-start(f32[1024]{0:T(1024)} %param.30) | copy-start | bytes 12292
  41.1 33.6 %copy-start.55 = (f32[512]{0:T(512)S(1)}, f32[512]{0:T(512)}, u32[]{:S(2)}) copy-start(f32[512]{0:T(512)} %param.28) | copy-start | bytes 6148
  43.2 63.4 %all-reduce.10.cloned.1.call-start = ((), (), s32[]{:S(2)}) async-start(), calls=%async_computation.1 | async-start | bytes 802816 | tf_op jit(solution)/shard_map/psum | solution.py:159
  73.3 10.0 %copy-start.33 = (f32[392]{0:T(512)}, f32[392]{0:T(512)S(1)}, u32[]{:S(2)}) copy-start(f32[392]{0:T(512)S(1)} %broadcast_multiply_fusion.4) | copy-start | bytes 4708
  74.7 8.6 %copy-start.37 = (f32[392]{0:T(512)}, f32[392]{0:T(512)S(1)}, u32[]{:S(2)}) copy-start(f32[392]{0:T(512)S(1)} %add_rsqrt_fusion) | copy-start | bytes 4708
  80.3 99.9 %all-reduce.14.cloned.1.call-start = ((), (), s32[]{:S(2)}) async-start(), calls=%async_computation.3 | async-start | bytes 1605632 | tf_op jit(solution)/shard_map/psum | solution.py:148
  83.3 23.3 %copy-start.41 = (f32[512]{0:T(512)S(1)}, f32[512]{0:T(512)}, u32[]{:S(2)}) copy-start(f32[512]{0:T(512)} %param.27) | copy-start | bytes 6148
  85.6 25.5 %copy-start.24 = (bf16[256,512]{1,0:T(8,128)(2,1)S(1)}, bf16[256,512]{1,0:T(8,128)(2,1)}, u32[]{:S(2)}) copy-start(bf16[256,512]{1,0:T(8,128)(2,1)} %param.25) | copy-start | bytes 786436
  145.2 3.5 %copy-start.36 = (f32[392]{0:T(512)S(1)}, f32[392]{0:T(512)}, u32[]{:S(2)}) copy-start(f32[392]{0:T(512)} %copy-done.35) | copy-start | bytes 4708
  145.2 3.5 %copy-start.43 = (f32[512]{0:T(512)S(1)}, f32[512]{0:T(512)}, u32[]{:S(2)}) copy-start(f32[512]{0:T(512)} %param.18) | copy-start | bytes 6148
  145.2 3.5 %copy-start.57 = (f32[512]{0:T(512)S(1)}, f32[512]{0:T(512)}, u32[]{:S(2)}) copy-start(f32[512]{0:T(512)} %param.19) | copy-start | bytes 6148
  145.2 179.9 %all-reduce.12.cloned.1.call-start = ((), (), s32[]{:S(2)}) async-start(), calls=%async_computation.2 | async-start | bytes 12582912 | tf_op jit(solution)/shard_map/psum | solution.py:210
  150.7 31.1 %copy-start.44 = (f32[512]{0:T(512)S(1)}, f32[512]{0:T(512)}, u32[]{:S(2)}) copy-start(f32[512]{0:T(512)} %get-tuple-element.15) | copy-start | bytes 6148
  150.7 31.1 %copy-start.45 = (f32[512]{0:T(512)S(1)}, f32[512]{0:T(512)}, u32[]{:S(2)}) copy-start(f32[512]{0:T(512)} %get-tuple-element.21) | copy-start | bytes 6148
  150.7 31.1 %copy-start.46 = (f32[512]{0:T(512)S(1)}, f32[512]{0:T(512)}, u32[]{:S(2)}) copy-start(f32[512]{0:T(512)} %get-tuple-element.40) | copy-start | bytes 6148
  150.7 31.1 %copy-start.47 = (f32[512]{0:T(512)S(1)}, f32[512]{0:T(512)}, u32[]{:S(2)}) copy-start(f32[512]{0:T(512)} %get-tuple-element.54) | copy-start | bytes 6148
  150.7 31.1 %copy-start.48 = (f32[1024]{0:T(1024)S(1)}, f32[1024]{0:T(1024)}, u32[]{:S(2)}) copy-start(f32[1024]{0:T(1024)} %get-tuple-element.63) | copy-start | bytes 12292
  150.7 94.4 %copy-start.6 = (bf16[392,512]{1,0:T(8,128)(2,1)S(1)}, bf16[392,512]{1,0:T(8,128)(2,1)}, u32[]{:S(2)}) copy-start(bf16[392,512]{1,0:T(8,128)(2,1)} %all-reduce.8.cloned.1.call-done) | copy-start | bytes 1204228
  150.7 94.4 %copy-start.49 = (f32[512]{0:T(512)S(1)}, f32[512]{0:T(512)}, u32[]{:S(2)}) copy-start(f32[512]{0:T(512)} %param.32) | copy-start | bytes 6148
  325.1 3.6 %copy-start.17 = (f32[512,1024]{1,0:T(8,128)S(1)}, f32[512,1024]{1,0:T(8,128)}, u32[]{:S(2)}) copy-start(f32[512,1024]{1,0:T(8,128)} %get-tuple-element.92) | copy-start | bytes 6291460
  328.7 3.7 %copy-start.1 = (bf16[512,1024]{1,0:T(8,128)(2,1)S(1)}, bf16[512,1024]{1,0:T(8,128)(2,1)}, u32[]{:S(2)}) copy-start(bf16[512,1024]{1,0:T(8,128)(2,1)} %param.29) | copy-start | bytes 3145732
  (32 other events, 60.7 us)
Sparse Core Ops, SparseCore 0:
  43.3 28.6 all-reduce.7
  80.5 26.1 all-reduce.9
  145.3 34.8 all-reduce.13
  185.2 139.8 all-reduce.11
where the time goes:
time: 340 us; the launch traced here: 339 us
  waiting for transfers between devices  154 us (45%)
  blocking collectives  63.3 us (19%)
  local copies, waits for them, and re-layouts  53.2 us (16%)
  matrix products  32 us (9%)
  other arithmetic  20.7 us (6%)
  between operations  14.7 us (4%)
    psum x1, waiting for transfers between devices, local(): lax.psum((grad_ln1_gain, grad_ln1_shift, grad_qkv, grad_qv_bias, grad_tab...  77.4 us
    psum x1, blocking collectives, local(): lax.psum((grad_ln1_gain, grad_ln1_shift, grad_qkv, grad_qv_bias, grad_tab...  63.3 us
    psum x1, waiting for transfers between devices, local(): lax.psum(attn_part.astype(jnp.bfloat16), 'tensor').astype(jnp.float32)  28.6 us
    psum x1, waiting for transfers between devices, local(): lax.psum(mlp_part.astype(jnp.bfloat16), 'tensor').astype(jnp.float32)  27.3 us
    psum x1, waiting for transfers between devices, local(): lax.psum(back_two_part.astype(jnp.bfloat16), 'tensor').astype(jnp.float32)  21 us
    unnamed x125, local copies, waits for them, and re-layouts  13.7 us
    reshape x4, local copies, waits for them, and re-layouts, to_windows(): layout.reshape(images * across * across, heads_here, WIN * WIN, head_depth)  7.54 us
  transfers between devices with their start and end apart: 4, of which 4 were waited for; matrix products, arithmetic and copies ran while one was open for 5% of the time, Pallas kernels for 0%

commit v1 on v0

v1 whole, which is shorter than its diff:
```python
import functools

import numpy as np
import jax
import jax.numpy as jnp
from jax import lax
from jax.experimental import pallas as pl
from jax.experimental.pallas import tpu as pltpu
from jax.sharding import PartitionSpec as P

HEAD_DIM = 32
SIDE = 14
WIN = 7
SHIFT = 3
ACROSS = SIDE // WIN
POSITIONS = WIN * WIN
PAD = 64
WINDOWS = ACROSS * ACROSS

NORM_EPS = 1e-05
MASKED = -1e30
F32 = jnp.float32
BF16 = jnp.bfloat16
HIDDEN_BLOCK = 256


def dot(a, b, dims=((1,), (0,)), precision=None):
    return lax.dot_general(a, b, (dims, ((), ())), preferred_element_type=F32, precision=precision)


NN = ((1,), (0,))
NT = ((1,), (1,))
TN = ((0,), (0,))


def normed(values):
    centered = values - jnp.mean(values, axis=-1, keepdims=True)
    inverse = lax.rsqrt(jnp.mean(centered * centered, axis=-1, keepdims=True) + NORM_EPS)
    return centered * inverse, inverse


def norm_backward(upstream, unit, inverse, gain):
    weighted = upstream * gain
    return inverse * (
        weighted
        - jnp.mean(weighted, axis=-1, keepdims=True)
        - unit * jnp.mean(weighted * unit, axis=-1, keepdims=True)
    )


def window_order():
    order = np.zeros((WINDOWS * PAD, SIDE * SIDE), np.float32)
    for a in range(ACROSS):
        for b in range(ACROSS):
            for i in range(POSITIONS):
                row = (a * WIN + i // WIN + SHIFT) % SIDE
                col = (b * WIN + i % WIN + SHIFT) % SIDE
                order[(a * ACROSS + b) * PAD + i, row * SIDE + col] = 1.0
    return order


def spread_heads(tile, mask):
    heads = mask.shape[0] // tile.shape[0]
    return jnp.concatenate([tile] * heads, axis=0) * mask


def gather_heads(full, mask, heads):
    total = None
    for h in range(heads):
        rows = slice(h * PAD, (h + 1) * PAD)
        part = full[rows, :] * mask[rows, :].astype(F32)
        total = part if total is None else total + part
    return total


def attn_forward_kernel(
    x_ref, gain_ref, shift_ref, wqkv_ref, qvb_ref, table_ref, rel_ref, creg_ref, rreg_ref,
    perm_ref, hmask_ref, wproj_ref,
    part_ref, n1_ref, qkvw_ref, prob_ref, otok_ref,
    bm_ref, ow_ref,
):
    inner = wproj_ref.shape[0]
    heads = inner // HEAD_DIM
    lanes = heads * PAD
    unit, _ = normed(x_ref[...].astype(F32))
    n1 = (unit * gain_ref[...] + shift_ref[...]).astype(BF16)
    n1_ref[...] = n1
    proj = dot(n1, wqkv_ref[...])
    q = ((proj[:, :inner] + qvb_ref[0:1, :]) * (HEAD_DIM ** (-0.5))).astype(BF16)
    k = proj[:, inner : 2 * inner].astype(BF16)
    v = (proj[:, 2 * inner :] + qvb_ref[1:2, :]).astype(BF16)
    perm = perm_ref[...]
    qkvw_ref[:, :inner] = dot(perm, q).astype(BF16)
    qkvw_ref[:, inner : 2 * inner] = dot(perm, k).astype(BF16)
    qkvw_ref[:, 2 * inner :] = dot(perm, v).astype(BF16)

    rel = rel_ref[...]
    pairs = lanes // rel.shape[1]
    width = rel.shape[1]

    def pick(t, acc):
        hit = rel == t
        row = table_ref[pl.ds(t, 1), :]
        return tuple(
            jnp.where(hit, row[:, p * width : (p + 1) * width], acc[p]) for p in range(pairs)
        )

    zero = jnp.zeros(rel.shape, F32)
    picked = lax.fori_loop(0, table_ref.shape[0], pick, (zero,) * pairs)
    bias = jnp.concatenate(picked, axis=1)
    for w in range(WINDOWS):
        hit = creg_ref[:, w : w + 1] == rreg_ref[w : w + 1, :]
        bm_ref[w * PAD : (w + 1) * PAD, :] = jnp.where(hit, bias, MASKED)

    def window(i, carry):
        rows = pl.ds(pl.multiple_of(i * PAD, PAD), PAD)
        hmask = hmask_ref[...]
        qw = qkvw_ref[rows, :inner]
        kw = qkvw_ref[rows, inner : 2 * inner]
        vw = qkvw_ref[rows, 2 * inner :]
        brows = pl.ds(pl.multiple_of(lax.rem(i, WINDOWS) * PAD, PAD), PAD)
        s = dot(kw, spread_heads(qw, hmask), NT) + bm_ref[brows, :]
        e = jnp.exp(s - jnp.max(s, axis=0, keepdims=True))
        p = e * (1.0 / jnp.sum(e, axis=0, keepdims=True))
        prob_ref[rows, :] = p
        full = dot(p.astype(BF16), vw, TN)
        ow_ref[rows, :] = gather_heads(full, hmask, heads).astype(BF16)
        return carry

    lax.fori_loop(0, qkvw_ref.shape[0] // PAD, window, 0)
    otok = dot(perm, ow_ref[...], TN).astype(BF16)
    otok_ref[...] = otok
    part_ref[...] = dot(otok, wproj_ref[...]).astype(BF16)


def mlp_kernel(
    x_ref, own_ref, recv_ref, pbias_ref, gain_ref, shift_ref, w1_ref, b1_ref, w2_ref, dy_ref,
    back_ref, h1_ref, n2_ref, act_ref, dub_ref, gb1_ref, gb2_ref,
    acc_ref,
):
    step = pl.program_id(0)

    @pl.when(step == 0)
    def _():
        h1 = (
            x_ref[...].astype(F32)
            + (own_ref[...].astype(F32) + recv_ref[...].astype(F32))
            + pbias_ref[...]
        )
        h1_ref[...] = h1
        unit, _ = normed(h1)
        n2_ref[...] = (unit * gain_ref[...] + shift_ref[...]).astype(BF16)
        gb2_ref[...] = jnp.sum(dy_ref[...].astype(F32), axis=0, keepdims=True)
        acc_ref[...] = jnp.zeros_like(acc_ref)

    u = dot(n2_ref[...], w1_ref[...]) + b1_ref[...]
    cdf = 0.5 * (1.0 + lax.erf(u * 0.7071067811865476))
    act_ref[...] = (u * cdf).astype(BF16)
    slope = cdf + u * jnp.exp(-0.5 * u * u) * 0.3989422804014327
    du = dot(dy_ref[...], w2_ref[...], NT) * slope
    gb1_ref[...] = jnp.sum(du, axis=0, keepdims=True)
    dub = du.astype(BF16)
    dub_ref[...] = dub
    acc_ref[...] += dot(dub, w1_ref[...], NT)

    @pl.when(step == pl.num_programs(0) - 1)
    def _():
        back_ref[...] = acc_ref[...].astype(BF16)


def half(ref, which, size):
    return ref[:, pl.ds(pl.multiple_of(which * size, size), size)]


def mlp_grad_kernel(bit_ref, act_ref, dub_ref, n2_ref, dy_ref, w2_ref, keep_ref, send_ref, part_ref):
    bit = bit_ref[0]
    size = act_ref.shape[1] // 2
    for out, which in ((send_ref, 1 - bit), (keep_ref, bit)):
        out[:size, :] = dot(half(act_ref, which, size), dy_ref[...], TN).astype(BF16)
        out[size:, :] = dot(n2_ref[...], half(dub_ref, which, size), TN).astype(BF16)
    part_ref[...] = dot(act_ref[...], w2_ref[...]).astype(BF16)


def attn_backward_kernel(
    dy_ref, own_ref, recv_ref, h1_ref, gain_ref, wproj_ref, qkvw_ref, prob_ref, perm_ref,
    hmask_ref, wqkv_ref,
    part_ref, dh_ref, dhb_ref, dp_ref, sums_ref, dsum_ref,
    dow_ref, dqkv_ref,
):
    inner = wproj_ref.shape[0]
    heads = inner // HEAD_DIM
    dn2 = own_ref[...].astype(F32) + recv_ref[...].astype(F32)
    unit, inverse = normed(h1_ref[...])
    sums_ref[0:1, :] = jnp.sum(dn2 * unit, axis=0, keepdims=True)
    sums_ref[1:2, :] = jnp.sum(dn2, axis=0, keepdims=True)
    dh = dy_ref[...].astype(F32) + norm_backward(dn2, unit, inverse, gain_ref[...])
    dh_ref[...] = dh
    sums_ref[2:3, :] = jnp.sum(dh, axis=0, keepdims=True)
    dhb = dh.astype(BF16)
    dhb_ref[...] = dhb
    perm = perm_ref[...]
    dow_ref[...] = dot(perm, dot(dhb, wproj_ref[...], NT).astype(BF16)).astype(BF16)
    dsum_ref[...] = jnp.zeros_like(dsum_ref)

    def window(i, carry):
        qsum, vsum = carry
        rows = pl.ds(pl.multiple_of(i * PAD, PAD), PAD)
        hmask = hmask_ref[...]
        qblk = spread_heads(qkvw_ref[rows, :inner], hmask)
        kw = qkvw_ref[rows, inner : 2 * inner]
        vw = qkvw_ref[rows, 2 * inner :]
        oblk = spread_heads(dow_ref[rows, :], hmask)
        p = prob_ref[rows, :]
        dp = dot(vw, oblk, NT)
        ds = p * (dp - jnp.sum(p * dp, axis=0, keepdims=True))
        dsum_ref[...] += ds
        dsb = ds.astype(BF16)
        dq = gather_heads(dot(dsb, kw, TN), hmask, heads) * (HEAD_DIM ** (-0.5))
        dk = dot(dsb, qblk)
        dv = dot(p.astype(BF16), oblk)
        dqkv_ref[rows, :inner] = dq.astype(BF16)
        dqkv_ref[rows, inner : 2 * inner] = dk.astype(BF16)
        dqkv_ref[rows, 2 * inner :] = dv.astype(BF16)
        return (
            qsum + jnp.sum(dq, axis=0, keepdims=True),
            vsum + jnp.sum(dv, axis=0, keepdims=True),
        )

    zero = jnp.zeros((1, inner), F32)
    qsum, vsum = lax.fori_loop(0, qkvw_ref.shape[0] // PAD, window, (zero, zero))
    sums_ref[3:4, :inner] = qsum
    sums_ref[3:4, inner:] = vsum
    dp_tok = dot(perm, dqkv_ref[...], TN).astype(BF16)
    dp_ref[...] = dp_tok
    part_ref[...] = dot(dp_tok, wqkv_ref[...], NT).astype(BF16)


def attn_grad_kernel(bit_ref, n1_ref, dp_ref, otok_ref, dhb_ref, keep_ref, send_ref):
    bit = bit_ref[0]
    wide = dp_ref.shape[1]
    rows = n1_ref.shape[1] // 2
    for out, which in ((send_ref, 1 - bit), (keep_ref, bit)):
        out[:, :wide] = dot(half(n1_ref, which, rows), dp_ref[...], TN).astype(BF16)
        out[:, wide:] = dot(otok_ref[...], half(dhb_ref, which, rows), TN).astype(BF16)


def table_kernel(dsum_ref, rel_ref, group_ref, out_ref, tab_ref):
    rel = rel_ref[...]
    width = rel.shape[1]
    pairs = dsum_ref.shape[1] // width

    def eight(n, carry):
        for p in range(pairs):
            cols = slice(p * width, (p + 1) * width)
            part = dsum_ref[:, cols]
            found = [
                jnp.sum(jnp.where(rel == n * 8 + t, part, 0.0), axis=0, keepdims=True)
                for t in range(8)
            ]
            tab_ref[pl.ds(pl.multiple_of(n * 8, 8), 8), cols] = jnp.concatenate(found, axis=0)
        return carry

    lax.fori_loop(0, tab_ref.shape[0] // 8, eight, 0)
    out_ref[...] = dot(group_ref[...], tab_ref[...], NT, lax.Precision.HIGHEST)


def input_grad_kernel(x_ref, own_ref, recv_ref, dh_ref, gain_ref, gin_ref, sums_ref):
    unit, inverse = normed(x_ref[...].astype(F32))
    dn1 = own_ref[...].astype(F32) + recv_ref[...].astype(F32)
    sums_ref[0:1, :] = jnp.sum(dn1 * unit, axis=0, keepdims=True)
    sums_ref[1:2, :] = jnp.sum(dn1, axis=0, keepdims=True)
    gin_ref[...] = dh_ref[...] + norm_backward(dn1, unit, inverse, gain_ref[...])


def output_kernel(h1_ref, own_ref, recv_ref, bias_ref, out_ref):
    total = own_ref[...].astype(F32) + recv_ref[...].astype(F32)
    out_ref[...] = (h1_ref[...] + total + bias_ref[...]).astype(BF16)


def shape(dims, dtype):
    return jax.ShapeDtypeStruct(dims, dtype)


VMEM = functools.partial(pl.BlockSpec, memory_space=pltpu.VMEM)
SMEM = functools.partial(pl.BlockSpec, memory_space=pltpu.SMEM)


def swap(value, axis, size, bit):
    return lax.ppermute(value, axis, [(i, i ^ bit) for i in range(size)])


def add_pair(left, right):
    return left.astype(F32) + right.astype(F32)


def reduce_scatter(keep, send, bits, size):
    index = lax.axis_index("dp")
    for n, bit in enumerate(bits):
        keep = add_pair(keep, swap(send, "dp", size, bit)).astype(BF16)
        if n + 1 < len(bits):
            rows = keep.shape[0] // 2
            low, high = keep[:rows], keep[rows:]
            upper = (index & bits[n + 1]) != 0
            keep, send = jnp.where(upper, high, low), jnp.where(upper, low, high)
    return keep


def gather_back(value, bits, size):
    index = lax.axis_index("dp")
    for bit in reversed(bits[1:]):
        other = swap(value, "dp", size, bit)
        upper = (index & bit) != 0
        value = jnp.concatenate(
            [jnp.where(upper, other, value), jnp.where(upper, value, other)], axis=0
        )
    other = swap(value, "dp", size, bits[0])
    upper = (index & bits[0]) != 0
    return jnp.where(upper, other, value), jnp.where(upper, value, other)


def local(
    dp_size,
    inputs,
    ln1_gain,
    ln1_shift,
    w_qkv,
    qv_bias,
    bias_table,
    rel_index,
    regions,
    w_proj,
    proj_bias,
    ln2_gain,
    ln2_shift,
    w_fc1,
    fc1_bias,
    w_fc2,
    fc2_bias,
    grad_output,
):
    tokens, width = inputs.shape
    images = tokens // (SIDE * SIDE)
    inner = w_qkv.shape[2]
    heads = inner // HEAD_DIM
    lanes = heads * PAD
    wrows = images * WINDOWS * PAD
    hidden = w_fc1.shape[1]
    table_rows = bias_table.shape[0]
    table_pad = -(-table_rows // 8) * 8
    row = lambda v: v.reshape(1, -1)
    tensor_swap = lambda v: swap(v, "tensor", 2, 1)
    bits = [1 << n for n in range(dp_size.bit_length() - 1)]
    core_bit = (lax.axis_index("dp") & 1).astype(jnp.int32).reshape(1)

    perm = jnp.asarray(np.kron(np.eye(images, dtype=np.float32), window_order()), BF16)
    hmask = jnp.asarray(
        np.kron(np.eye(heads, dtype=np.float32), np.ones((PAD, HEAD_DIM), np.float32)), BF16
    )
    group = jnp.asarray(np.kron(np.eye(heads, dtype=np.float32), np.ones((1, PAD), np.float32)))
    rel = jnp.pad(rel_index.T, ((0, PAD - POSITIONS),) * 2, constant_values=-1)
    rel = jnp.concatenate([rel, rel], axis=1)
    region_win = (
        regions.reshape(ACROSS, WIN, ACROSS, WIN).transpose(0, 2, 1, 3).reshape(WINDOWS, POSITIONS)
    )
    pad = ((0, 0), (0, PAD - POSITIONS))
    creg = jnp.pad(region_win, pad, constant_values=-1).T
    rreg = jnp.tile(jnp.pad(region_win, pad, constant_values=-2), (1, heads))
    table = jnp.repeat(bias_table, PAD, axis=1)
    qkv_weight = w_qkv.reshape(width, 3 * inner)

    attn_part, n1, qkvw, prob, otok = pl.pallas_call(
        attn_forward_kernel,
        out_shape=(
            shape((tokens, width), BF16),
            shape((tokens, width), BF16),
            shape((wrows, 3 * inner), BF16),
            shape((wrows, lanes), F32),
            shape((tokens, inner), BF16),
        ),
        scratch_shapes=[
            pltpu.VMEM((WINDOWS * PAD, lanes), F32),
            pltpu.VMEM((wrows, inner), BF16),
        ],
        name="attn_forward",
    )(
        inputs, row(ln1_gain), row(ln1_shift), qkv_weight, qv_bias, table, rel, creg, rreg,
        perm, hmask, w_proj,
    )
    attn_recv = tensor_swap(attn_part)

    steps = hidden // HIDDEN_BLOCK
    full = lambda dims: pl.BlockSpec(dims, lambda j: (0, 0))
    cols = lambda rows: pl.BlockSpec((rows, HIDDEN_BLOCK), lambda j: (0, j))
    back_two_part, h1, n2, act, dub, grad_b1, grad_b2 = pl.pallas_call(
        mlp_kernel,
        grid=(steps,),
        in_specs=[
            full((tokens, width)), full((tokens, width)), full((tokens, width)), full((1, width)),
            full((1, width)), full((1, width)), cols(width), cols(1),
            pl.BlockSpec((HIDDEN_BLOCK, width), lambda j: (j, 0)), full((tokens, width)),
        ],
        out_specs=(
            full((tokens, width)), full((tokens, width)), full((tokens, width)), cols(tokens),
            cols(tokens), cols(1), full((1, width)),
        ),
        out_shape=(
            shape((tokens, width), BF16),
            shape((tokens, width), F32),
            shape((tokens, width), BF16),
            shape((tokens, hidden), BF16),
            shape((tokens, hidden), BF16),
            shape((1, hidden), F32),
            shape((1, width), F32),
        ),
        scratch_shapes=[pltpu.VMEM((tokens, width), F32)],
        name="mlp",
    )(
        inputs, attn_part, attn_recv, row(proj_bias), row(ln2_gain), row(ln2_shift), w_fc1,
        row(fc1_bias), w_fc2, grad_output,
    )
    back_two_recv = tensor_swap(back_two_part)

    keep, send, mlp_part = pl.pallas_call(
        mlp_grad_kernel,
        in_specs=[SMEM()] + [VMEM()] * 5,
        out_shape=(
            shape((hidden // 2 + width, width), BF16),
            shape((hidden // 2 + width, width), BF16),
            shape((tokens, width), BF16),
        ),
        cost_estimate=pl.CostEstimate(
            flops=6 * tokens * hidden * width, bytes_accessed=8 << 20, transcendentals=0
        ),
        name="mlp_grad",
    )(core_bit, act, dub, n2, grad_output, w_fc2)
    mlp_shard = reduce_scatter(keep, send, bits, dp_size)

    back_one_part, dh, dhb, dproj, sums, dsum = pl.pallas_call(
        attn_backward_kernel,
        out_shape=(
            shape((tokens, width), BF16),
            shape((tokens, width), F32),
            shape((tokens, width), BF16),
            shape((tokens, 3 * inner), BF16),
            shape((4, width), F32),
            shape((PAD, lanes), F32),
        ),
        scratch_shapes=[
            pltpu.VMEM((wrows, inner), BF16),
            pltpu.VMEM((wrows, 3 * inner), BF16),
        ],
        name="attn_backward",
    )(
        grad_output, back_two_part, back_two_recv, h1, row(ln2_gain), w_proj, qkvw, prob, perm,
        hmask, qkv_weight,
    )
    back_one_recv = tensor_swap(back_one_part)

    keep, send = pl.pallas_call(
        attn_grad_kernel,
        in_specs=[SMEM()] + [VMEM()] * 4,
        out_shape=(
            shape((width // 2, 3 * inner + inner), BF16),
            shape((width // 2, 3 * inner + inner), BF16),
        ),
        cost_estimate=pl.CostEstimate(
            flops=8 * tokens * inner * width, bytes_accessed=4 << 20, transcendentals=0
        ),
        name="attn_grad",
    )(core_bit, n1, dproj, otok, dhb)
    attn_shard = reduce_scatter(keep, send, bits, dp_size)

    table_sum = pl.pallas_call(
        table_kernel,
        out_shape=shape((heads, table_pad), F32),
        scratch_shapes=[pltpu.VMEM((table_pad, lanes), F32)],
        name="table",
    )(dsum, rel, group)

    mlp_recv = tensor_swap(mlp_part)
    output = pl.pallas_call(
        output_kernel, out_shape=shape((tokens, width), BF16), name="output"
    )(h1, mlp_part, mlp_recv, row(fc2_bias))

    grad_input, ln1_sums = pl.pallas_call(
        input_grad_kernel,
        out_shape=(shape((tokens, width), F32), shape((2, width), F32)),
        name="input_grad",
    )(inputs, back_one_part, back_one_recv, dh, row(ln1_gain))

    small = jnp.concatenate(
        [
            sums.reshape(-1),
            ln1_sums.reshape(-1),
            grad_b2.reshape(-1),
            grad_b1.reshape(-1),
            table_sum.reshape(-1),
        ]
    )
    for bit in bits:
        small = small + swap(small, "dp", dp_size, bit)
    s = small[: 4 * width].reshape(4, width)
    rest = small[4 * width :]
    grad_ln1_gain, grad_ln1_shift, grad_fc2_bias = rest[: 3 * width].reshape(3, width)
    grad_fc1_bias = rest[3 * width : 3 * width + hidden]
    grad_table = rest[3 * width + hidden :].reshape(heads, table_pad)[:, :table_rows].T
    grad_qv_bias = s[3].reshape(2, inner)

    low, high = gather_back(mlp_shard, bits, dp_size)
    mid = hidden // 2
    grad_fc2 = jnp.concatenate([low[:mid], high[:mid]], axis=0).astype(F32)
    grad_fc1 = jnp.concatenate([low[mid:], high[mid:]], axis=1).astype(F32)
    low, high = gather_back(attn_shard, bits, dp_size)
    grad_qkv = (
        jnp.concatenate([low[:, : 3 * inner], high[:, : 3 * inner]], axis=0)
        .astype(F32)
        .reshape(width, 3, inner)
    )
    grad_proj = jnp.concatenate([low[:, 3 * inner :], high[:, 3 * inner :]], axis=1).astype(F32)

    return (
        output, grad_input, grad_ln1_gain, grad_ln1_shift, grad_qkv, grad_qv_bias, grad_table,
        grad_proj, s[2], s[0], s[1], grad_fc1, grad_fc1_bias, grad_fc2, grad_fc2_bias,
    )


def solution(mesh):
    return jax.shard_map(
        functools.partial(local, mesh.shape["dp"]),
        mesh=mesh,
        in_specs=(
            P("dp", None),
            P(),
            P(),
            P(None, None, "tensor"),
            P(None, "tensor"),
            P(None, "tensor"),
            P(),
            P(),
            P("tensor", None),
            P(),
            P(),
            P(),
            P(None, "tensor"),
            P("tensor"),
            P("tensor", None),
            P(),
            P("dp", None),
        ),
        out_specs=(
            P("dp", None),
            P("dp", None),
            P(),
            P(),
            P(None, None, "tensor"),
            P(None, "tensor"),
            P(None, "tensor"),
            P("tensor", None),
            P(),
            P(),
            P(),
            P(None, "tensor"),
            P("tensor"),
            P("tensor", None),
            P(),
        ),
        check_vma=False,
    )
```

time: 340 us -> 168 us (0.49)
  waiting for transfers between devices: 154 us -> 61.5 us
  blocking collectives: 63.3 us -> 0 us
  Pallas kernels: 0 us -> 45.5 us
  local copies, waits for them, and re-layouts: 53.2 us -> 17.3 us
  matrix products: 32 us -> 0 us
  starting transfers between devices: 0.56 us -> 31.3 us
  between operations: 14.7 us -> 1.02 us
  other arithmetic: 20.7 us -> 10.5 us
    psum x4 -> x0, waiting for transfers between devices: 154 us -> none  [the longest x1 77.4 us: local(): lax.psum((grad_ln1_gain, grad_ln1_shift, grad_qkv, grad_qv_bias, grad_tab...]
    psum x1 -> x0, blocking collectives: 63.3 us -> none  [local(): lax.psum((grad_ln1_gain, grad_ln1_shift, grad_qkv, grad_qv_bias, grad_tab...]
    ppermute x0 -> x24, waiting for transfers between devices: none -> 61.5 us  [swap(): return lax.ppermute(value, axis, [(i, i ^ bit) for i in range(size)])]
    pallas_call x0 -> x8, Pallas kernels: none -> 45.5 us  [the longest x1 11.2 us: local(): pl.pallas_call(attn_forward_kernel, out_shape=(shape((tokens, width), BF1...]
    dot_general x20 -> x0, matrix products: 32 us -> none  [the longest x1 2.9 us: local(): mlp_part = jnp.dot(activ_b, w_fc2, preferred_element_type=jnp.float32)]
    ppermute x0 -> x24, starting transfers between devices: none -> 31.3 us  [swap(): return lax.ppermute(value, axis, [(i, i ^ bit) for i in range(size)])]
    reduce_sum x13 -> x0, other arithmetic: 14 us -> none  [the longest x2 2.52 us: layer_norm(): jnp.mean(centered * centered, axis=-1, keepdims=True) + NORM_EPS]
    slice x19 -> x10, local copies, waits for them, and re-layouts: 9.81 us -> 2.43 us  [the longest x1 0.67 us: local(): high[:, 3 * inner:]]
  transfers between devices with their start and end apart: 4 -> 24, of which waited for: 4 -> 13; matrix products, arithmetic and copies ran while one was open for 5% -> 8% of each run, Pallas kernels for 0% -> 17%
where the time goes in v1:
time: 168 us; the launch traced here: 167 us
  waiting for transfers between devices  61.5 us (37%)
  Pallas kernels  45.5 us (27%)
  starting transfers between devices  31.3 us (19%)
  local copies, waits for them, and re-layouts  17.3 us (10%)
  other arithmetic  10.5 us (6%)
    ppermute x24, waiting for transfers between devices, swap(): return lax.ppermute(value, axis, [(i, i ^ bit) for i in range(size)])  61.5 us
    ppermute x24, starting transfers between devices, swap(): return lax.ppermute(value, axis, [(i, i ^ bit) for i in range(size)])  31.3 us
    pallas_call x1, Pallas kernels, local(): pl.pallas_call(attn_forward_kernel, out_shape=(shape((tokens, width), BF1...  11.2 us
    pallas_call x1, Pallas kernels, local(): pl.pallas_call(attn_backward_kernel, out_shape=(shape((tokens, width), BF...  9.88 us
    unnamed x31, local copies, waits for them, and re-layouts  7.6 us
    pallas_call x1, Pallas kernels, local(): pl.pallas_call(mlp_kernel, grid=(steps,), in_specs=[full((tokens, width))...  6.65 us
    pallas_call x1, Pallas kernels, local(): pl.pallas_call(table_kernel, out_shape=shape((heads, table_pad), F32), sc...  5.03 us
    pallas_call x1, Pallas kernels, local(): pl.pallas_call(mlp_grad_kernel, in_specs=[SMEM()] + [VMEM()] * 5, out_sha...  4.41 us
  transfers between devices with their start and end apart: 24, of which 13 were waited for; matrix products, arithmetic and copies ran while one was open for 8% of the time, Pallas kernels for 17%

profile of v1, /device:TPU:0, one launch (start us, length us, event | category | flops | bytes accessed | tf_op | source)
XLA Modules:
  0.0 167.1 jit_solution(6817685906419202978)
XLA Ops:
  7.7 11.2 %attn_forward.1 = (bf16[392,512]{1,0:T(8,128)(2,1)}, bf16[392,512]{1,0:T(8,128)(2,1)}, bf16[512,768]{1,0:T(8,128)(2,1)}, f32[512,512]{1,0:T(8,128)}, bf16[392,256]{1,0:T(8,128)(2,1)}) custom-call(bf16[392,512]{1,0:T(8,128)(2,1)} %x_ref.5, f32[1,512]{1,0:T(1,128)} %bitcast.34, f32[1,512]{1,0:T(1,128)} %bitcast.40, bf16[512,768]{1,0:T(8,128)(2,1)} %copy.45.wqkv_ref, ...), custom_call_target="tpu_custom_call" | custom-call | tf_op jit(solution)/shard_map/attn_forward/pallas_call | solution.py:371
  18.9 3.0 %collective-permute-start = (bf16[392,512]{1,0:T(8,128)(2,1)}, bf16[392,512]{1,0:T(8,128)(2,1)S(1)}, u32[]{:S(2)}, u32[]{:S(2)}) collective-permute-start(bf16[392,512]{1,0:T(8,128)(2,1)} %get-tuple-element.40.own_ref), channel_id=1, source_target_pairs={{0,1},{1,0},{2,3},{3,2},{4,5},{5,4},{6,7},{7,6},{8,9},{9,8},{10,11... | collective-permute-start | bytes 1204232 | tf_op jit(solution)/shard_map/ppermute | solution.py:289
  21.9 9.5 %collective-permute-done.recv_ref = bf16[392,512]{1,0:T(8,128)(2,1)S(1)} collective-permute-done((bf16[392,512]{1,0:T(8,128)(2,1)}, bf16[392,512]{1,0:T(8,128)(2,1)S(1)}, u32[]{:S(2)}, u32[]{:S(2)}) %collective-permute-start) | collective-permute-done | bytes 401440 | tf_op jit(solution)/shard_map/ppermute | solution.py:289
  32.2 6.6 %mlp.1 = (bf16[392,512]{1,0:T(8,128)(2,1)}, f32[392,512]{1,0:T(8,128)}, bf16[392,512]{1,0:T(8,128)(2,1)}, bf16[392,1024]{1,0:T(8,128)(2,1)}, bf16[392,1024]{1,0:...) custom-call(bf16[392,512]{1,0:T(8,128)(2,1)} %x_ref.5, bf16[392,512]{1,0:T(8,128)(2,1)} %get-tuple-element.40.own_ref, ...), custom_call_target="tpu_custom_call" | custom-call | tf_op jit(solution)/shard_map/mlp/pallas_call | solution.py:394
  38.8 1.8 %collective-permute-start.2 = (bf16[392,512]{1,0:T(8,128)(2,1)}, bf16[392,512]{1,0:T(8,128)(2,1)S(1)}, u32[]{:S(2)}, u32[]{:S(2)}) collective-permute-start(bf16[392,512]{1,0:T(8,128)(2,1)} %get-tuple-element.46.own_ref), channel_id=1, source_target_pairs={{0,1},{1,0},{2,3},{3,2},{4,5},{5,4},{6,7},{7,6},{8,9},{9,8},{10,11... | collective-permute-start | bytes 1204232 | tf_op jit(solution)/shard_map/ppermute | solution.py:289
  40.6 4.4 %mlp_grad.1 = (bf16[1024,512]{1,0:T(8,128)(2,1)}, bf16[1024,512]{1,0:T(8,128)(2,1)}, bf16[392,512]{1,0:T(8,128)(2,1)}) custom-call(s32[1]{0:T(128)} %bitcast.11.bit_ref, bf16[392,1024]{1,0:T(8,128)(2,1)} %get-tuple-element.42.act_ref, bf16[392,1024]{1,0:T(8,128)(2,1)} %get-tuple-element.43.dub_ref, bf16[392,512]{1,0:T(8,128)(2,1)} %get-tuple-element.44.n2_ref, ...), custom_call_target="tpu_custom_call" | custom-call | flops 1233125376 | bytes 8388608 | tf_op jit(solution)/shard_map/mlp_grad/pallas_call | solution.py:423
  45.1 4.5 %collective-permute-done.2.recv_ref = bf16[392,512]{1,0:T(8,128)(2,1)S(1)} collective-permute-done((bf16[392,512]{1,0:T(8,128)(2,1)}, bf16[392,512]{1,0:T(8,128)(2,1)S(1)}, u32[]{:S(2)}, u32[]{:S(2)}) %collective-permute-start.2) | collective-permute-done | bytes 401440 | tf_op jit(solution)/shard_map/ppermute | solution.py:289
  50.3 9.9 %attn_backward.1 = (bf16[392,512]{1,0:T(8,128)(2,1)}, f32[392,512]{1,0:T(8,128)}, bf16[392,512]{1,0:T(8,128)(2,1)}, bf16[392,768]{1,0:T(8,128)(2,1)}, f32[4,512]{1,0:T(4,128)}, /*index=5*/f32[64,512]{1,0:T(8,128)}) custom-call(bf16[392,512]{1,0:T(8,128)(2,1)} %dy_ref.5, bf16[392,512]{1,0:T(8,128)(2,1)} %get-tuple-element.46.own_ref, ...), custom_call_target="tpu_custom_call" | custom-call | tf_op jit(solution)/shard_map/attn_backward/pallas_call | solution.py:438
  60.2 2.9 %attn_grad.1 = (bf16[256,1024]{1,0:T(8,128)(2,1)}, bf16[256,1024]{1,0:T(8,128)(2,1)}) custom-call(s32[1]{0:T(128)} %bitcast.11.bit_ref, bf16[392,512]{1,0:T(8,128)(2,1)} %get-tuple-element.57.n1_ref, bf16[392,768]{1,0:T(8,128)(2,1)} %get-tuple-element.58.dp_ref, bf16[392,256]{1,0:T(8,128)(2,1)} %get-tuple-element.59.otok_ref, ...), custom_call_target="tpu_custom_call" | custom-call | flops 411041792 | bytes 4194304 | tf_op jit(solution)/shard_map/attn_grad/pallas_call | solution.py:459
  64.6 5.0 %table.1 = f32[8,176]{1,0:T(8,128)} custom-call(f32[64,512]{1,0:T(8,128)} %get-tuple-element.56.dsum_ref, s32[64,128]{1,0:T(8,128)} %pad_add_fusion.rel_ref, f32[8,512]{1,0:T(8,128)} %constant.28.clone.group_ref), custom_call_target="tpu_custom_call" | custom-call | tf_op jit(solution)/shard_map/table/pallas_call | solution.py:473
  71.7 3.3 %collective-permute-done.3.recv_ref = bf16[392,512]{1,0:T(8,128)(2,1)S(1)} collective-permute-done((bf16[392,512]{1,0:T(8,128)(2,1)}, bf16[392,512]{1,0:T(8,128)(2,1)S(1)}, u32[]{:S(2)}, u32[]{:S(2)}) %collective-permute-start.3) | collective-permute-done | bytes 401440 | tf_op jit(solution)/shard_map/ppermute | solution.py:289
  75.8 3.1 %input_grad.1 = (f32[392,512]{1,0:T(8,128)}, f32[2,512]{1,0:T(2,128)}) custom-call(bf16[392,512]{1,0:T(8,128)(2,1)} %x_ref.5, bf16[392,512]{1,0:T(8,128)(2,1)} %get-tuple-element.49.own_ref, bf16[392,512]{1,0:T(8,128)(2,1)} %copy-done.6, f32[392,512]{1,0:T(8,128)} %get-tuple-element.50.dh_ref, f32[1,512]{1,0:T(1,128)} %bitcast.35), custom_call_target="tpu_custom_call" | custom-call | tf_op jit(solution)/shard_map/input_grad/pallas_call | solution.py:485
  83.0 6.7 %collective-permute-done.9 = bf16[128,1024]{1,0:T(8,128)(2,1)S(1)} collective-permute-done((bf16[128,1024]{1,0:T(8,128)(2,1)S(1)}, bf16[128,1024]{1,0:T(8,128)(2,1)S(1)}, u32[]{:S(2)}, u32[]{:S(2)}) %collective-permute-start.9) | collective-permute-done | bytes 262176 | tf_op jit(solution)/shard_map/ppermute | solution.py:289
  89.8 1.6 collective-permute-start.10
  91.4 8.1 %collective-permute-done.17 = bf16[512,512]{1,0:T(8,128)(2,1)S(1)} collective-permute-done((bf16[512,512]{1,0:T(8,128)(2,1)S(1)}, bf16[512,512]{1,0:T(8,128)(2,1)S(1)}, u32[]{:S(2)}, u32[]{:S(2)}) %collective-permute-start.17) | collective-permute-done | bytes 524320 | tf_op jit(solution)/shard_map/ppermute | solution.py:289
  99.8 1.6 collective-permute-start.18
  101.4 2.7 %collective-permute-start.11 = (bf16[32,1024]{1,0:T(8,128)(2,1)S(1)}, bf16[32,1024]{1,0:T(8,128)(2,1)S(1)}, u32[]{:S(2)}, u32[]{:S(2)}) collective-permute-start(bf16[32,1024]{1,0:T(8,128)(2,1)S(1)} %broadcast_select_fusion.21), channel_id=1, source_target_pairs={{0,16},{2,18},{4,20},{6,22},{8,24},{10,26},{12,28},{14,30},{16,0},... | collective-permute-start | bytes 196616 | tf_op jit(solution)/shard_map/ppermute | solution.py:289
  104.1 4.1 %collective-permute-done.18 = bf16[256,512]{1,0:T(8,128)(2,1)S(1)} collective-permute-done((bf16[256,512]{1,0:T(8,128)(2,1)S(1)}, bf16[256,512]{1,0:T(8,128)(2,1)S(1)}, u32[]{:S(2)}, u32[]{:S(2)}) %collective-permute-start.18) | collective-permute-done | bytes 262176 | tf_op jit(solution)/shard_map/ppermute | solution.py:289
  108.3 1.9 %collective-permute-start.19 = (bf16[128,512]{1,0:T(8,128)(2,1)S(1)}, bf16[128,512]{1,0:T(8,128)(2,1)S(1)}, u32[]{:S(2)}, u32[]{:S(2)}) collective-permute-start(bf16[128,512]{1,0:T(8,128)(2,1)S(1)} %broadcast_select_fusion.15), channel_id=1, source_target_pairs={{0,16},{2,18},{4,20},{6,22},{8,24},{10,26},{12,28},{14,30},{16,0},... | collective-permute-start | bytes 393224 | tf_op jit(solution)/shard_map/ppermute | solution.py:289
  111.4 7.1 %collective-permute-done.19 = bf16[128,512]{1,0:T(8,128)(2,1)S(1)} collective-permute-done((bf16[128,512]{1,0:T(8,128)(2,1)S(1)}, bf16[128,512]{1,0:T(8,128)(2,1)S(1)}, u32[]{:S(2)}, u32[]{:S(2)}) %collective-permute-start.19) | collective-permute-done | bytes 131104 | tf_op jit(solution)/shard_map/ppermute | solution.py:289
  119.9 2.9 %collective-permute-start.13 = (bf16[64,1024]{1,0:T(8,128)(2,1)S(1)}, bf16[64,1024]{1,0:T(8,128)(2,1)S(1)}, u32[]{:S(2)}, u32[]{:S(2)}) collective-permute-start(bf16[64,1024]{1,0:T(8,128)(2,1)S(1)} %pad_maximum_fusion.5), channel_id=1, source_target_pairs={{0,8},{2,10},{4,12},{6,14},{8,0},{10,2},{12,4},{14,6},{16,24},{18,... | collective-permute-start | bytes 393224 | tf_op jit(solution)/shard_map/ppermute | solution.py:289
  122.7 2.5 %collective-permute-done.20 = bf16[128,512]{1,0:T(8,128)(2,1)S(1)} collective-permute-done((bf16[128,512]{1,0:T(8,128)(2,1)S(1)}, bf16[128,512]{1,0:T(8,128)(2,1)S(1)}, u32[]{:S(2)}, u32[]{:S(2)}) %collective-permute-start.20) | collective-permute-done | bytes 131104 | tf_op jit(solution)/shard_map/ppermute | solution.py:289
  128.7 3.1 %collective-permute-done.21 = bf16[256,512]{1,0:T(8,128)(2,1)S(1)} collective-permute-done((bf16[256,512]{1,0:T(8,128)(2,1)S(1)}, bf16[256,512]{1,0:T(8,128)(2,1)S(1)}, u32[]{:S(2)}, u32[]{:S(2)}) %collective-permute-start.21) | collective-permute-done | bytes 262176 | tf_op jit(solution)/shard_map/ppermute | solution.py:289
  133.6 1.6 collective-permute-start.1
  136.8 8.3 %collective-permute-done.22 = bf16[512,512]{1,0:T(8,128)(2,1)S(1)} collective-permute-done((bf16[512,512]{1,0:T(8,128)(2,1)S(1)}, bf16[512,512]{1,0:T(8,128)(2,1)S(1)}, u32[]{:S(2)}, u32[]{:S(2)}) %collective-permute-start.22) | collective-permute-done | bytes 524320 | tf_op jit(solution)/shard_map/ppermute | solution.py:289
  147.7 2.6 %collective-permute-done.6 = f32[6016]{0:T(1024)S(1)} collective-permute-done((f32[6016]{0:T(1024)S(1)}, f32[6016]{0:T(1024)S(1)}, u32[]{:S(2)}, u32[]{:S(2)}) %collective-permute-start.6) | collective-permute-done | bytes 24096 | tf_op jit(solution)/shard_map/ppermute | solution.py:289
  150.2 3.0 %collective-permute-start.7 = (f32[6016]{0:T(1024)S(1)}, f32[6016]{0:T(1024)S(1)}, u32[]{:S(2)}, u32[]{:S(2)}) collective-permute-start(f32[6016]{0:T(1024)S(1)} %add.44), channel_id=1, source_target_pairs={{0,16},{2,18},{4,20},{6,22},{8,24},{10,26},{12,28},{14,30},{16,0},... | collective-permute-start | bytes 72200 | tf_op jit(solution)/shard_map/ppermute | solution.py:289
  153.3 2.3 %output.1 = bf16[392,512]{1,0:T(8,128)(2,1)} custom-call(f32[392,512]{1,0:T(8,128)} %get-tuple-element.41.h1_ref, bf16[392,512]{1,0:T(8,128)(2,1)} %get-tuple-element.45.own_ref, bf16[392,512]{1,0:T(8,128)(2,1)} %collective-permute-done.1.recv_ref, f32[1,512]{1,0:T(1,128)} %bitcast.43), custom_call_target="tpu_custom_call" | custom-call | tf_op jit(solution)/shard_map/output/pallas_call | solution.py:481
  159.7 1.6 copy.50
  162.1 1.6 broadcast_select_fusion.1
  163.9 1.6 maximum_convert_fusion.1
  165.5 1.6 maximum_convert_fusion
  (119 shorter events, 34.4 us)
Async XLA Ops:
  0.6 5.6 %copy-start.1 = (bf16[512,3,256]{2,0,1:T(8,128)(2,1)S(1)}, bf16[512,3,256]{2,0,1:T(8,128)(2,1)}, u32[]{:S(2)}) copy-start(bf16[512,3,256]{2,0,1:T(8,128)(2,1)} %param.23) | copy-start | bytes 2359300
  18.9 12.5 %collective-permute-start = (bf16[392,512]{1,0:T(8,128)(2,1)}, bf16[392,512]{1,0:T(8,128)(2,1)S(1)}, u32[]{:S(2)}, u32[]{:S(2)}) collective-permute-start(bf16[392,512]{1,0:T(8,128)(2,1)} %get-tuple-element.40.own_ref), channel_id=1, source_target_pairs={{0,1},{1,0},{2,3},{3,2},{4,5},{5,4},{6,7},{7,6},{8,9},{9,8},{10,11... | collective-permute-start | bytes 1204232 | tf_op jit(solution)/shard_map/ppermute | solution.py:289
  38.8 10.7 %collective-permute-start.2 = (bf16[392,512]{1,0:T(8,128)(2,1)}, bf16[392,512]{1,0:T(8,128)(2,1)S(1)}, u32[]{:S(2)}, u32[]{:S(2)}) collective-permute-start(bf16[392,512]{1,0:T(8,128)(2,1)} %get-tuple-element.46.own_ref), channel_id=1, source_target_pairs={{0,1},{1,0},{2,3},{3,2},{4,5},{5,4},{6,7},{7,6},{8,9},{9,8},{10,11... | collective-permute-start | bytes 1204232 | tf_op jit(solution)/shard_map/ppermute | solution.py:289
  45.0 36.9 %collective-permute-start.16 = (bf16[1024,512]{1,0:T(8,128)(2,1)}, bf16[1024,512]{1,0:T(8,128)(2,1)S(1)}, u32[]{:S(2)}, u32[]{:S(2)}) collective-permute-start(bf16[1024,512]{1,0:T(8,128)(2,1)} %get-tuple-element.64), channel_id=1, source_target_pairs={{0,2},{2,0},{4,6},{6,4},{8,10},{10,8},{12,14},{14,12},{16,18},{18,... | collective-permute-start | bytes 3145736 | tf_op jit(solution)/shard_map/ppermute | solution.py:289
  63.1 17.1 %copy-start.2 = (bf16[256,1024]{1,0:T(8,128)(2,1)S(1)}, bf16[256,1024]{1,0:T(8,128)(2,1)}, u32[]{:S(2)}) copy-start(bf16[256,1024]{1,0:T(8,128)(2,1)} %get-tuple-element.61) | copy-start | bytes 1572868
  63.1 17.1 %collective-permute-start.8 = (bf16[256,1024]{1,0:T(8,128)(2,1)}, bf16[256,1024]{1,0:T(8,128)(2,1)S(1)}, u32[]{:S(2)}, u32[]{:S(2)}) collective-permute-start(bf16[256,1024]{1,0:T(8,128)(2,1)} %get-tuple-element.62), channel_id=1, source_target_pairs={{0,2},{2,0},{4,6},{6,4},{8,10},{10,8},{12,14},{14,12},{16,18},{18,... | collective-permute-start | bytes 1572872 | tf_op jit(solution)/shard_map/ppermute | solution.py:289
  63.1 11.9 %collective-permute-start.3 = (bf16[392,512]{1,0:T(8,128)(2,1)}, bf16[392,512]{1,0:T(8,128)(2,1)S(1)}, u32[]{:S(2)}, u32[]{:S(2)}) collective-permute-start(bf16[392,512]{1,0:T(8,128)(2,1)} %get-tuple-element.49.own_ref), channel_id=1, source_target_pairs={{0,1},{1,0},{2,3},{3,2},{4,5},{5,4},{6,7},{7,6},{8,9},{9,8},{10,11... | collective-permute-start | bytes 1204232 | tf_op jit(solution)/shard_map/ppermute | solution.py:289
  75.8 6.2 %copy-start = (bf16[1024,512]{1,0:T(8,128)(2,1)S(1)}, bf16[1024,512]{1,0:T(8,128)(2,1)}, u32[]{:S(2)}) copy-start(bf16[1024,512]{1,0:T(8,128)(2,1)} %get-tuple-element.63) | copy-start | bytes 3145732
  80.4 9.2 %collective-permute-start.9 = (bf16[128,1024]{1,0:T(8,128)(2,1)S(1)}, bf16[128,1024]{1,0:T(8,128)(2,1)S(1)}, u32[]{:S(2)}, u32[]{:S(2)}) collective-permute-start(bf16[128,1024]{1,0:T(8,128)(2,1)S(1)} %broadcast_select_fusion.12), channel_id=1, source_target_pairs={{0,4},{2,6},{4,0},{6,2},{8,12},{10,14},{12,8},{14,10},{16,20},{18,... | collective-permute-start | bytes 786440 | tf_op jit(solution)/shard_map/ppermute | solution.py:289
  81.9 1.0 copy-start.8
  81.9 1.0 copy-start.10
  82.3 17.2 %collective-permute-start.17 = (bf16[512,512]{1,0:T(8,128)(2,1)S(1)}, bf16[512,512]{1,0:T(8,128)(2,1)S(1)}, u32[]{:S(2)}, u32[]{:S(2)}) collective-permute-start(bf16[512,512]{1,0:T(8,128)(2,1)S(1)} %broadcast_select_fusion.4), channel_id=1, source_target_pairs={{0,4},{2,6},{4,0},{6,2},{8,12},{10,14},{12,8},{14,10},{16,20},{18,... | collective-permute-start | bytes 1572872 | tf_op jit(solution)/shard_map/ppermute | solution.py:289
  89.8 11.5 %collective-permute-start.10 = (bf16[64,1024]{1,0:T(8,128)(2,1)S(1)}, bf16[64,1024]{1,0:T(8,128)(2,1)S(1)}, u32[]{:S(2)}, u32[]{:S(2)}) collective-permute-start(bf16[64,1024]{1,0:T(8,128)(2,1)S(1)} %broadcast_select_fusion.18), channel_id=1, source_target_pairs={{0,8},{2,10},{4,12},{6,14},{8,0},{10,2},{12,4},{14,6},{16,24},{18,... | collective-permute-start | bytes 393224 | tf_op jit(solution)/shard_map/ppermute | solution.py:289
  99.8 8.4 %collective-permute-start.18 = (bf16[256,512]{1,0:T(8,128)(2,1)S(1)}, bf16[256,512]{1,0:T(8,128)(2,1)S(1)}, u32[]{:S(2)}, u32[]{:S(2)}) collective-permute-start(bf16[256,512]{1,0:T(8,128)(2,1)S(1)} %broadcast_select_fusion.9), channel_id=1, source_target_pairs={{0,8},{2,10},{4,12},{6,14},{8,0},{10,2},{12,4},{14,6},{16,24},{18,... | collective-permute-start | bytes 786440 | tf_op jit(solution)/shard_map/ppermute | solution.py:289
  101.4 8.8 %collective-permute-start.11 = (bf16[32,1024]{1,0:T(8,128)(2,1)S(1)}, bf16[32,1024]{1,0:T(8,128)(2,1)S(1)}, u32[]{:S(2)}, u32[]{:S(2)}) collective-permute-start(bf16[32,1024]{1,0:T(8,128)(2,1)S(1)} %broadcast_select_fusion.21), channel_id=1, source_target_pairs={{0,16},{2,18},{4,20},{6,22},{8,24},{10,26},{12,28},{14,30},{16,0},... | collective-permute-start | bytes 196616 | tf_op jit(solution)/shard_map/ppermute | solution.py:289
  108.3 10.1 %collective-permute-start.19 = (bf16[128,512]{1,0:T(8,128)(2,1)S(1)}, bf16[128,512]{1,0:T(8,128)(2,1)S(1)}, u32[]{:S(2)}, u32[]{:S(2)}) collective-permute-start(bf16[128,512]{1,0:T(8,128)(2,1)S(1)} %broadcast_select_fusion.15), channel_id=1, source_target_pairs={{0,16},{2,18},{4,20},{6,22},{8,24},{10,26},{12,28},{14,30},{16,0},... | collective-permute-start | bytes 393224 | tf_op jit(solution)/shard_map/ppermute | solution.py:289
  110.2 9.6 %collective-permute-start.12 = (bf16[32,1024]{1,0:T(8,128)(2,1)S(1)}, bf16[32,1024]{1,0:T(8,128)(2,1)S(1)}, u32[]{:S(2)}, u32[]{:S(2)}) collective-permute-start(bf16[32,1024]{1,0:T(8,128)(2,1)S(1)} %add_convert_fusion.7), channel_id=1, source_target_pairs={{0,16},{2,18},{4,20},{6,22},{8,24},{10,26},{12,28},{14,30},{16,0},... | collective-permute-start | bytes 196616 | tf_op jit(solution)/shard_map/ppermute | solution.py:289
  118.5 6.7 %collective-permute-start.20 = (bf16[128,512]{1,0:T(8,128)(2,1)S(1)}, bf16[128,512]{1,0:T(8,128)(2,1)S(1)}, u32[]{:S(2)}, u32[]{:S(2)}) collective-permute-start(bf16[128,512]{1,0:T(8,128)(2,1)S(1)} %add_convert_fusion.5), channel_id=1, source_target_pairs={{0,16},{2,18},{4,20},{6,22},{8,24},{10,26},{12,28},{14,30},{16,0},... | collective-permute-start | bytes 393224 | tf_op jit(solution)/shard_map/ppermute | solution.py:289
  119.8 13.7 %copy-start.9 = (f32[1,1024]{1,0:T(1,128)S(1)}, f32[1,1024]{1,0:T(1,128)}, u32[]{:S(2)}) copy-start(f32[1,1024]{1,0:T(1,128)} %get-tuple-element.55) | copy-start | bytes 12292
  119.8 13.8 %copy-start.5 = (bf16[392,512]{1,0:T(8,128)(2,1)S(1)}, bf16[392,512]{1,0:T(8,128)(2,1)}, u32[]{:S(2)}) copy-start(bf16[392,512]{1,0:T(8,128)(2,1)} %get-tuple-element.45.own_ref) | copy-start | bytes 1204228
  119.9 7.2 %collective-permute-start.13 = (bf16[64,1024]{1,0:T(8,128)(2,1)S(1)}, bf16[64,1024]{1,0:T(8,128)(2,1)S(1)}, u32[]{:S(2)}, u32[]{:S(2)}) collective-permute-start(bf16[64,1024]{1,0:T(8,128)(2,1)S(1)} %pad_maximum_fusion.5), channel_id=1, source_target_pairs={{0,8},{2,10},{4,12},{6,14},{8,0},{10,2},{12,4},{14,6},{16,24},{18,... | collective-permute-start | bytes 393224 | tf_op jit(solution)/shard_map/ppermute | solution.py:289
  125.3 6.5 %collective-permute-start.21 = (bf16[256,512]{1,0:T(8,128)(2,1)S(1)}, bf16[256,512]{1,0:T(8,128)(2,1)S(1)}, u32[]{:S(2)}, u32[]{:S(2)}) collective-permute-start(bf16[256,512]{1,0:T(8,128)(2,1)S(1)} %pad_maximum_fusion.4), channel_id=1, source_target_pairs={{0,8},{2,10},{4,12},{6,14},{8,0},{10,2},{12,4},{14,6},{16,24},{18,... | collective-permute-start | bytes 786440 | tf_op jit(solution)/shard_map/ppermute | solution.py:289
  127.2 8.7 %collective-permute-start.14 = (bf16[128,1024]{1,0:T(8,128)(2,1)S(1)}, bf16[128,1024]{1,0:T(8,128)(2,1)S(1)}, u32[]{:S(2)}, u32[]{:S(2)}) collective-permute-start(bf16[128,1024]{1,0:T(8,128)(2,1)S(1)} %pad_maximum_fusion.3), channel_id=1, source_target_pairs={{0,4},{2,6},{4,0},{6,2},{8,12},{10,14},{12,8},{14,10},{16,20},{18,... | collective-permute-start | bytes 786440 | tf_op jit(solution)/shard_map/ppermute | solution.py:289
  132.0 13.1 %collective-permute-start.22 = (bf16[512,512]{1,0:T(8,128)(2,1)S(1)}, bf16[512,512]{1,0:T(8,128)(2,1)S(1)}, u32[]{:S(2)}, u32[]{:S(2)}) collective-permute-start(bf16[512,512]{1,0:T(8,128)(2,1)S(1)} %pad_maximum_fusion.2), channel_id=1, source_target_pairs={{0,4},{2,6},{4,0},{6,2},{8,12},{10,14},{12,8},{14,10},{16,20},{18,... | collective-permute-start | bytes 1572872 | tf_op jit(solution)/shard_map/ppermute | solution.py:289
  133.5 1.7 collective-permute-start.4
  133.6 19.7 %collective-permute-start.1 = (bf16[392,512]{1,0:T(8,128)(2,1)S(1)}, bf16[392,512]{1,0:T(8,128)(2,1)}, u32[]{:S(2)}, u32[]{:S(2)}) collective-permute-start(bf16[392,512]{1,0:T(8,128)(2,1)S(1)} %copy-done.5), channel_id=1, source_target_pairs={{0,1},{1,0},{2,3},{3,2},{4,5},{5,4},{6,7},{7,6},{8,9},{9,8},{10,11... | collective-permute-start | bytes 1204232 | tf_op jit(solution)/shard_map/ppermute | solution.py:289
  135.2 11.1 %collective-permute-start.5 = (f32[6016]{0:T(1024)S(1)}, f32[6016]{0:T(1024)S(1)}, u32[]{:S(2)}, u32[]{:S(2)}) collective-permute-start(f32[6016]{0:T(1024)S(1)} %add.42), channel_id=1, source_target_pairs={{0,4},{2,6},{4,0},{6,2},{8,12},{10,14},{12,8},{14,10},{16,20},{18,... | collective-permute-start | bytes 72200 | tf_op jit(solution)/shard_map/ppermute | solution.py:289
  136.8 21.3 %collective-permute-start.15 = (bf16[256,1024]{1,0:T(8,128)(2,1)}, bf16[256,1024]{1,0:T(8,128)(2,1)S(1)}, u32[]{:S(2)}, u32[]{:S(2)}) collective-permute-start(bf16[256,1024]{1,0:T(8,128)(2,1)} %pad_maximum_fusion.1), channel_id=1, source_target_pairs={{0,2},{2,0},{4,6},{6,4},{8,10},{10,8},{12,14},{14,12},{16,18},{18,... | collective-permute-start | bytes 1572872 | tf_op jit(solution)/shard_map/ppermute | solution.py:289
  146.3 15.8 %collective-permute-start.23 = (bf16[1024,512]{1,0:T(8,128)(2,1)}, bf16[1024,512]{1,0:T(8,128)(2,1)}, u32[]{:S(2)}, u32[]{:S(2)}) collective-permute-start(bf16[1024,512]{1,0:T(8,128)(2,1)} %pad_maximum_fusion), channel_id=1, source_target_pairs={{0,2},{2,0},{4,6},{6,4},{8,10},{10,8},{12,14},{14,12},{16,18},{18,... | collective-permute-start | bytes 3145736 | tf_op jit(solution)/shard_map/ppermute | solution.py:289
  146.3 3.9 %collective-permute-start.6 = (f32[6016]{0:T(1024)S(1)}, f32[6016]{0:T(1024)S(1)}, u32[]{:S(2)}, u32[]{:S(2)}) collective-permute-start(f32[6016]{0:T(1024)S(1)} %add.43), channel_id=1, source_target_pairs={{0,8},{2,10},{4,12},{6,14},{8,0},{10,2},{12,4},{14,6},{16,24},{18,... | collective-permute-start | bytes 72200 | tf_op jit(solution)/shard_map/ppermute | solution.py:289
  150.2 5.3 %collective-permute-start.7 = (f32[6016]{0:T(1024)S(1)}, f32[6016]{0:T(1024)S(1)}, u32[]{:S(2)}, u32[]{:S(2)}) collective-permute-start(f32[6016]{0:T(1024)S(1)} %add.44), channel_id=1, source_target_pairs={{0,16},{2,18},{4,20},{6,22},{8,24},{10,26},{12,28},{14,30},{16,0},... | collective-permute-start | bytes 72200 | tf_op jit(solution)/shard_map/ppermute | solution.py:289
  159.6 1.6 copy-start.3
  (3 other events, 2.2 us)

commit v2 on v1

--- a/solution.py
+++ b/solution.py
@@ -28,7 +28,6 @@
     return lax.dot_general(a, b, (dims, ((), ())), preferred_element_type=F32, precision=precision)
 
 
-NN = ((1,), (0,))
 NT = ((1,), (1,))
 TN = ((0,), (0,))
 
@@ -48,13 +47,13 @@
     )
 
 
-def window_order():
+def window_order(shift=SHIFT):
     order = np.zeros((WINDOWS * PAD, SIDE * SIDE), np.float32)
     for a in range(ACROSS):
         for b in range(ACROSS):
             for i in range(POSITIONS):
-                row = (a * WIN + i // WIN + SHIFT) % SIDE
-                col = (b * WIN + i % WIN + SHIFT) % SIDE
+                row = (a * WIN + i // WIN + shift) % SIDE
+                col = (b * WIN + i % WIN + shift) % SIDE
                 order[(a * ACROSS + b) * PAD + i, row * SIDE + col] = 1.0
     return order
 
@@ -73,11 +72,20 @@
     return total
 
 
+def pair_index(rel_ref):
+    lane = lax.broadcasted_iota(jnp.int32, (POSITIONS, 2 * PAD), 1)
+    sub = lax.broadcasted_iota(jnp.int32, (POSITIONS, 2 * PAD), 0)
+    same = (lax.rem(lane, PAD) == sub).astype(BF16)
+    spread = dot((rel_ref[...] + 1).astype(F32).astype(BF16), same, TN)
+    zero = jnp.zeros((PAD - POSITIONS, 2 * PAD), F32)
+    return jnp.concatenate([spread, zero], axis=0).astype(jnp.int32)
+
+
 def attn_forward_kernel(
-    x_ref, gain_ref, shift_ref, wqkv_ref, qvb_ref, table_ref, rel_ref, creg_ref, rreg_ref,
-    perm_ref, hmask_ref, wproj_ref,
+    x_ref, gain_ref, shift_ref, wqkv_ref, qvb_ref, table_ref, rel_ref, reg_ref, order_ref,
+    group_ref, perm_ref, hmask_ref, wproj_ref,
     part_ref, n1_ref, qkvw_ref, prob_ref, otok_ref,
-    bm_ref, ow_ref,
+    bm_ref, ow_ref, tab_ref,
 ):
     inner = wproj_ref.shape[0]
     heads = inner // HEAD_DIM
@@ -85,32 +93,37 @@
     unit, _ = normed(x_ref[...].astype(F32))
     n1 = (unit * gain_ref[...] + shift_ref[...]).astype(BF16)
     n1_ref[...] = n1
-    proj = dot(n1, wqkv_ref[...])
-    q = ((proj[:, :inner] + qvb_ref[0:1, :]) * (HEAD_DIM ** (-0.5))).astype(BF16)
-    k = proj[:, inner : 2 * inner].astype(BF16)
-    v = (proj[:, 2 * inner :] + qvb_ref[1:2, :]).astype(BF16)
+    q = ((dot(n1, wqkv_ref[0]) + qvb_ref[0:1, :]) * (HEAD_DIM ** (-0.5))).astype(BF16)
+    k = dot(n1, wqkv_ref[1]).astype(BF16)
+    v = (dot(n1, wqkv_ref[2]) + qvb_ref[1:2, :]).astype(BF16)
     perm = perm_ref[...]
     qkvw_ref[:, :inner] = dot(perm, q).astype(BF16)
     qkvw_ref[:, inner : 2 * inner] = dot(perm, k).astype(BF16)
     qkvw_ref[:, 2 * inner :] = dot(perm, v).astype(BF16)
 
-    rel = rel_ref[...]
-    pairs = lanes // rel.shape[1]
+    rel = pair_index(rel_ref)
     width = rel.shape[1]
+    pairs = lanes // width
+    tab_ref[...] = dot(table_ref[...], group_ref[...], TN, lax.Precision.HIGHEST)
 
     def pick(t, acc):
-        hit = rel == t
-        row = table_ref[pl.ds(t, 1), :]
+        hit = rel == t + 1
+        row = tab_ref[pl.ds(t, 1), :]
         return tuple(
             jnp.where(hit, row[:, p * width : (p + 1) * width], acc[p]) for p in range(pairs)
         )
 
     zero = jnp.zeros(rel.shape, F32)
-    picked = lax.fori_loop(0, table_ref.shape[0], pick, (zero,) * pairs)
+    picked = lax.fori_loop(0, tab_ref.shape[0], pick, (zero,) * pairs)
     bias = jnp.concatenate(picked, axis=1)
+    region = jnp.broadcast_to((reg_ref[...] + 1).astype(F32), (16, reg_ref.shape[1])).astype(BF16)
+    order = order_ref[...]
+    across = dot(region, order, NT)
+    down = dot(order, region, NT)
     for w in range(WINDOWS):
-        hit = creg_ref[:, w : w + 1] == rreg_ref[w : w + 1, :]
-        bm_ref[w * PAD : (w + 1) * PAD, :] = jnp.where(hit, bias, MASKED)
+        rows = slice(w * PAD, (w + 1) * PAD)
+        hit = down[rows, 0:1] == jnp.concatenate([across[0:1, rows]] * heads, axis=1)
+        bm_ref[rows, :] = jnp.where(hit, bias, MASKED)
 
     def window(i, carry):
         rows = pl.ds(pl.multiple_of(i * PAD, PAD), PAD)
@@ -232,7 +245,9 @@
     sums_ref[3:4, inner:] = vsum
     dp_tok = dot(perm, dqkv_ref[...], TN).astype(BF16)
     dp_ref[...] = dp_tok
-    part_ref[...] = dot(dp_tok, wqkv_ref[...], NT).astype(BF16)
+    part = dot(dp_tok[:, :inner], wqkv_ref[0], NT)
+    part = part + dot(dp_tok[:, inner : 2 * inner], wqkv_ref[1], NT)
+    part_ref[...] = (part + dot(dp_tok[:, 2 * inner :], wqkv_ref[2], NT)).astype(BF16)
 
 
 def attn_grad_kernel(bit_ref, n1_ref, dp_ref, otok_ref, dhb_ref, keep_ref, send_ref):
@@ -245,7 +260,7 @@
 
 
 def table_kernel(dsum_ref, rel_ref, group_ref, out_ref, tab_ref):
-    rel = rel_ref[...]
+    rel = pair_index(rel_ref)
     width = rel.shape[1]
     pairs = dsum_ref.shape[1] // width
 
@@ -254,7 +269,7 @@
             cols = slice(p * width, (p + 1) * width)
             part = dsum_ref[:, cols]
             found = [
-                jnp.sum(jnp.where(rel == n * 8 + t, part, 0.0), axis=0, keepdims=True)
+                jnp.sum(jnp.where(rel == n * 8 + t + 1, part, 0.0), axis=0, keepdims=True)
                 for t in range(8)
             ]
             tab_ref[pl.ds(pl.multiple_of(n * 8, 8), 8), cols] = jnp.concatenate(found, axis=0)
@@ -264,12 +279,73 @@
     out_ref[...] = dot(group_ref[...], tab_ref[...], NT, lax.Precision.HIGHEST)
 
 
-def input_grad_kernel(x_ref, own_ref, recv_ref, dh_ref, gain_ref, gin_ref, sums_ref):
+def input_grad_kernel(
+    x_ref, own_ref, recv_ref, dh_ref, gain_ref, sums_ref, gb1_ref, gb2_ref, tab_ref,
+    gin_ref, small_ref,
+):
+    width = x_ref.shape[1]
     unit, inverse = normed(x_ref[...].astype(F32))
     dn1 = own_ref[...].astype(F32) + recv_ref[...].astype(F32)
-    sums_ref[0:1, :] = jnp.sum(dn1 * unit, axis=0, keepdims=True)
-    sums_ref[1:2, :] = jnp.sum(dn1, axis=0, keepdims=True)
     gin_ref[...] = dh_ref[...] + norm_backward(dn1, unit, inverse, gain_ref[...])
+    small_ref[...] = jnp.zeros_like(small_ref)
+    small_ref[0:1, :] = jnp.sum(dn1 * unit, axis=0, keepdims=True)
+    small_ref[1:2, :] = jnp.sum(dn1, axis=0, keepdims=True)
+    small_ref[2:6, :] = sums_ref[...]
+    small_ref[6:7, :] = gb2_ref[...]
+    at = 7
+    for n in range(gb1_ref.shape[1] // width):
+        small_ref[at : at + 1, :] = gb1_ref[:, n * width : (n + 1) * width]
+        at += 1
+    for h in range(tab_ref.shape[0]):
+        small_ref[at : at + 1, : tab_ref.shape[1]] = tab_ref[h : h + 1, :]
+        at += 1
+
+
+def small_kernel(
+    left_ref, right_ref,
+    gain1_ref, shift1_ref, gain2_ref, shift2_ref, pbias_ref, qvb_ref, gb2_ref, gb1_ref, tab_ref,
+):
+    small = left_ref[...] + right_ref[...]
+    width = small.shape[1]
+    inner = qvb_ref.shape[1]
+    for n, out in enumerate((gain1_ref, shift1_ref, gain2_ref, shift2_ref, pbias_ref)):
+        out[...] = small[n : n + 1, :]
+    qvb_ref[0:1, :] = small[5:6, :inner]
+    qvb_ref[1:2, :] = small[5:6, inner:]
+    gb2_ref[...] = small[6:7, :]
+    at = 7
+    for n in range(gb1_ref.shape[1] // width):
+        gb1_ref[:, n * width : (n + 1) * width] = small[at : at + 1, :]
+        at += 1
+    tab_ref[...] = small[at : at + tab_ref.shape[0], : tab_ref.shape[1]]
+
+
+def mlp_finish_kernel(bit_ref, mine_ref, other_ref, fc2_ref, fc1_ref):
+    half_rows = fc2_ref.shape[0] // 2
+    for src, which in ((mine_ref, bit_ref[0]), (other_ref, 1 - bit_ref[0])):
+        at = pl.ds(pl.multiple_of(which * half_rows, half_rows), half_rows)
+        fc2_ref[at, :] = src[:half_rows, :].astype(F32)
+        fc1_ref[:, at] = src[half_rows:, :].astype(F32)
+
+
+def attn_finish_kernel(bit_ref, mine_ref, other_ref, qkv_ref, proj_ref):
+    inner = qkv_ref.shape[2]
+    half_rows = qkv_ref.shape[1] // 2
+    block = half_rows // 4
+    for src, which in ((mine_ref, bit_ref[0]), (other_ref, 1 - bit_ref[0])):
+        for n in range(3):
+            for a in range(2):
+                for b in range(2):
+                    to = pl.multiple_of(which * half_rows + (b * 2 + a) * block, block)
+                    rows = slice((a * 2 + b) * block, (a * 2 + b + 1) * block)
+                    cols = slice(n * inner, (n + 1) * inner)
+                    qkv_ref[n, pl.ds(to, block), :] = src[rows, cols].astype(F32)
+        at = pl.ds(pl.multiple_of(which * half_rows, half_rows), half_rows)
+        for a in range(2):
+            for b in range(2):
+                rows = slice((a * 2 + b) * block, (a * 2 + b + 1) * block)
+                to = slice((b * 2 + a) * block, (b * 2 + a + 1) * block)
+                proj_ref[to, at] = src[rows, 3 * inner :].astype(F32)
 
 
 def output_kernel(h1_ref, own_ref, recv_ref, bias_ref, out_ref):
@@ -296,7 +372,8 @@
 def reduce_scatter(keep, send, bits, size):
     index = lax.axis_index("dp")
     for n, bit in enumerate(bits):
-        keep = add_pair(keep, swap(send, "dp", size, bit)).astype(BF16)
+        recv = swap(send, "dp", size, bit)
+        keep = add_pair(keep, recv).astype(BF16)
         if n + 1 < len(bits):
             rows = keep.shape[0] // 2
             low, high = keep[:rows], keep[rows:]
@@ -307,15 +384,13 @@
 
 def gather_back(value, bits, size):
     index = lax.axis_index("dp")
-    for bit in reversed(bits[1:]):
+    for bit in bits[:-1]:
         other = swap(value, "dp", size, bit)
         upper = (index & bit) != 0
         value = jnp.concatenate(
             [jnp.where(upper, other, value), jnp.where(upper, value, other)], axis=0
         )
-    other = swap(value, "dp", size, bits[0])
-    upper = (index & bits[0]) != 0
-    return jnp.where(upper, other, value), jnp.where(upper, value, other)
+    return value, swap(value, "dp", size, bits[-1])
 
 
 def local(
@@ -348,25 +423,21 @@
     table_rows = bias_table.shape[0]
     table_pad = -(-table_rows // 8) * 8
     row = lambda v: v.reshape(1, -1)
-    tensor_swap = lambda v: swap(v, "tensor", 2, 1)
+
+    def tensor_swap(value):
+        return swap(value, "tensor", 2, 1)
+
     bits = [1 << n for n in range(dp_size.bit_length() - 1)]
     core_bit = (lax.axis_index("dp") & 1).astype(jnp.int32).reshape(1)
 
-    perm = jnp.asarray(np.kron(np.eye(images, dtype=np.float32), window_order()), BF16)
+    order = window_order()
+    perm = jnp.asarray(np.kron(np.eye(images, dtype=np.float32), order), BF16)
+    shifted = jnp.asarray(window_order(0), BF16)
     hmask = jnp.asarray(
         np.kron(np.eye(heads, dtype=np.float32), np.ones((PAD, HEAD_DIM), np.float32)), BF16
     )
     group = jnp.asarray(np.kron(np.eye(heads, dtype=np.float32), np.ones((1, PAD), np.float32)))
-    rel = jnp.pad(rel_index.T, ((0, PAD - POSITIONS),) * 2, constant_values=-1)
-    rel = jnp.concatenate([rel, rel], axis=1)
-    region_win = (
-        regions.reshape(ACROSS, WIN, ACROSS, WIN).transpose(0, 2, 1, 3).reshape(WINDOWS, POSITIONS)
-    )
-    pad = ((0, 0), (0, PAD - POSITIONS))
-    creg = jnp.pad(region_win, pad, constant_values=-1).T
-    rreg = jnp.tile(jnp.pad(region_win, pad, constant_values=-2), (1, heads))
-    table = jnp.repeat(bias_table, PAD, axis=1)
-    qkv_weight = w_qkv.reshape(width, 3 * inner)
+    qkv_weight = w_qkv.transpose(1, 0, 2)
 
     attn_part, n1, qkvw, prob, otok = pl.pallas_call(
         attn_forward_kernel,
@@ -380,11 +451,12 @@
         scratch_shapes=[
             pltpu.VMEM((WINDOWS * PAD, lanes), F32),
             pltpu.VMEM((wrows, inner), BF16),
+            pltpu.VMEM((table_rows, lanes), F32),
         ],
         name="attn_forward",
     )(
-        inputs, row(ln1_gain), row(ln1_shift), qkv_weight, qv_bias, table, rel, creg, rreg,
-        perm, hmask, w_proj,
+        inputs, row(ln1_gain), row(ln1_shift), qkv_weight, qv_bias, bias_table.T, rel_index,
+        row(regions), shifted, group, perm, hmask, w_proj,
     )
     attn_recv = tensor_swap(attn_part)
 
@@ -475,58 +547,70 @@
         out_shape=shape((heads, table_pad), F32),
         scratch_shapes=[pltpu.VMEM((table_pad, lanes), F32)],
         name="table",
-    )(dsum, rel, group)
+    )(dsum, rel_index, group)
 
     mlp_recv = tensor_swap(mlp_part)
     output = pl.pallas_call(
         output_kernel, out_shape=shape((tokens, width), BF16), name="output"
     )(h1, mlp_part, mlp_recv, row(fc2_bias))
 
-    grad_input, ln1_sums = pl.pallas_call(
+    small_rows = 7 + hidden // width + heads
+    grad_input, small = pl.pallas_call(
         input_grad_kernel,
-        out_shape=(shape((tokens, width), F32), shape((2, width), F32)),
+        out_shape=(shape((tokens, width), F32), shape((small_rows, width), F32)),
         name="input_grad",
-    )(inputs, back_one_part, back_one_recv, dh, row(ln1_gain))
-
-    small = jnp.concatenate(
-        [
-            sums.reshape(-1),
-            ln1_sums.reshape(-1),
-            grad_b2.reshape(-1),
-            grad_b1.reshape(-1),
-            table_sum.reshape(-1),
-        ]
-    )
-    for bit in bits:
-        small = small + swap(small, "dp", dp_size, bit)
-    s = small[: 4 * width].reshape(4, width)
-    rest = small[4 * width :]
-    grad_ln1_gain, grad_ln1_shift, grad_fc2_bias = rest[: 3 * width].reshape(3, width)
-    grad_fc1_bias = rest[3 * width : 3 * width + hidden]
-    grad_table = rest[3 * width + hidden :].reshape(heads, table_pad)[:, :table_rows].T
-    grad_qv_bias = s[3].reshape(2, inner)
-
-    low, high = gather_back(mlp_shard, bits, dp_size)
-    mid = hidden // 2
-    grad_fc2 = jnp.concatenate([low[:mid], high[:mid]], axis=0).astype(F32)
-    grad_fc1 = jnp.concatenate([low[mid:], high[mid:]], axis=1).astype(F32)
-    low, high = gather_back(attn_shard, bits, dp_size)
-    grad_qkv = (
-        jnp.concatenate([low[:, : 3 * inner], high[:, : 3 * inner]], axis=0)
-        .astype(F32)
-        .reshape(width, 3, inner)
-    )
-    grad_proj = jnp.concatenate([low[:, 3 * inner :], high[:, 3 * inner :]], axis=1).astype(F32)
-
+    )(
+        inputs, back_one_part, back_one_recv, dh, row(ln1_gain), sums, grad_b1, grad_b2, table_sum
+    )
+    for n, bit in enumerate(reversed(bits)):
+        recv = swap(small, "dp", dp_size, bit)
+        if n + 1 < len(bits):
+            small = small + recv
+    smalls = pl.pallas_call(
+        small_kernel,
+        out_shape=tuple(shape((1, width), F32) for _ in range(5))
+        + (
+            shape((2, inner), F32),
+            shape((1, width), F32),
+            shape((1, hidden), F32),
+            shape((heads, table_rows), F32),
+        ),
+        name="small",
+    )(small, recv)
+    grad_gain1, grad_shift1, grad_gain2, grad_shift2, grad_pb, grad_qvb, grad_b2, grad_b1 = smalls[:8]
+
+    down = bits[::-1]
+    mine, other = gather_back(mlp_shard, down, dp_size)
+    grad_fc2, grad_fc1 = pl.pallas_call(
+        mlp_finish_kernel,
+        in_specs=[SMEM()] + [VMEM()] * 2,
+        out_shape=(shape((hidden, width), F32), shape((width, hidden), F32)),
+        name="mlp_finish",
+    )(core_bit, mine, other)
+    mine, other = gather_back(attn_shard, down[:-3] + [down[-2], down[-3], down[-1]], dp_size)
+    grad_qkv, grad_proj = pl.pallas_call(
+        attn_finish_kernel,
+        in_specs=[SMEM()] + [VMEM()] * 2,
+        out_shape=(shape((3, width, inner), F32), shape((inner, width), F32)),
+        name="attn_finish",
+    )(core_bit, mine, other)
+
+    flat = lambda v: v.reshape(-1)
     return (
-        output, grad_input, grad_ln1_gain, grad_ln1_shift, grad_qkv, grad_qv_bias, grad_table,
-        grad_proj, s[2], s[0], s[1], grad_fc1, grad_fc1_bias, grad_fc2, grad_fc2_bias,
+        output, grad_input, flat(grad_gain1), flat(grad_shift1), grad_qkv.transpose(1, 0, 2),
+        grad_qvb, smalls[8].T, grad_proj, flat(grad_pb), flat(grad_gain2), flat(grad_shift2),
+        grad_fc1, flat(grad_b1), grad_fc2, flat(grad_b2),
     )
 
 
 def solution(mesh):
+    size = mesh.shape["dp"]
+
+    def body(*args):
+        return local(size, *args)
+
     return jax.shard_map(
-        functools.partial(local, mesh.shape["dp"]),
+        body,
         mesh=mesh,
         in_specs=(
             P("dp", None),

time: 168 us -> 173 us (1.030)
  waiting for transfers between devices: 61.5 us -> 79.4 us
  local copies, waits for them, and re-layouts: 17.3 us -> 4.28 us
  Pallas kernels: 45.5 us -> 54.4 us
  other arithmetic: 10.5 us -> 6.26 us
  starting transfers between devices: 31.3 us -> 27.4 us
    ppermute x24, waiting for transfers between devices: 61.5 us -> 79.4 us  [swap(): return lax.ppermute(value, axis, [(i, i ^ bit) for i in range(size)])]
    pallas_call x0 -> x3, Pallas kernels: none -> 7.85 us  [the longest x1 3.75 us: local(): pl.pallas_call(mlp_finish_kernel, in_specs=[SMEM()] + [VMEM()] * 2, out_s...]
    reshape x7 -> x0, local copies, waits for them, and re-layouts: 3.98 us -> none  [the longest x1 1.16 us: local(): qkv_weight = w_qkv.reshape(width, 3 * inner)]
    ppermute x24, starting transfers between devices: 31.3 us -> 27.4 us  [swap(): return lax.ppermute(value, axis, [(i, i ^ bit) for i in range(size)])]
    unnamed x31 -> x18, local copies, waits for them, and re-layouts: 7.6 us -> 4.28 us
    slice x10 -> x0, local copies, waits for them, and re-layouts: 2.43 us -> none  [the longest x1 0.67 us: local(): high[:, 3 * inner:]]
    convert_element_type x12 -> x8, other arithmetic: 5.28 us -> 3.3 us  [reduce_scatter(): keep = add_pair(keep, recv).astype(BF16)]
    select_n x2 -> x0, other arithmetic: 1.87 us -> none  [gather_back(): return (jnp.where(upper, other, value), jnp.where(upper, value, other))]
  transfers between devices with their start and end apart: 24 -> 24, of which waited for: 13 -> 17; matrix products, arithmetic and copies ran while one was open for 8% -> 3% of each run, Pallas kernels for 17% -> 19%
where the time goes in v2:
time: 173 us
  waiting for transfers between devices  79.4 us (46%)
  Pallas kernels  54.4 us (31%)
  starting transfers between devices  27.4 us (16%)
  other arithmetic  6.26 us (4%)
  local copies, waits for them, and re-layouts  4.28 us (2%)
    ppermute x24, waiting for transfers between devices, swap(): return lax.ppermute(value, axis, [(i, i ^ bit) for i in range(size)])  79.4 us
    ppermute x24, starting transfers between devices, swap(): return lax.ppermute(value, axis, [(i, i ^ bit) for i in range(size)])  27.4 us
    pallas_call x1, Pallas kernels, local(): pl.pallas_call(attn_forward_kernel, out_shape=(shape((tokens, width), BF1...  12 us
    pallas_call x1, Pallas kernels, local(): pl.pallas_call(attn_backward_kernel, out_shape=(shape((tokens, width), BF...  10.1 us
    pallas_call x1, Pallas kernels, local(): pl.pallas_call(mlp_kernel, grid=(steps,), in_specs=[full((tokens, width))...  6.65 us
    pallas_call x1, Pallas kernels, local(): pl.pallas_call(table_kernel, out_shape=shape((heads, table_pad), F32), sc...  5.04 us
    pallas_call x1, Pallas kernels, local(): pl.pallas_call(mlp_grad_kernel, in_specs=[SMEM()] + [VMEM()] * 5, out_sha...  4.43 us
    unnamed x18, local copies, waits for them, and re-layouts  4.28 us
  transfers between devices with their start and end apart: 24, of which 17 were waited for; matrix products, arithmetic and copies ran while one was open for 3% of the time, Pallas kernels for 19%

profile of v2, /device:TPU:0, one launch (start us, length us, event | category | flops | bytes accessed | tf_op | source)
XLA Modules:
  0.0 172.5 jit_solution(13414104491581574799)
XLA Ops:
  0.6 12.0 %attn_forward.1 = (bf16[392,512]{1,0:T(8,128)(2,1)}, bf16[392,512]{1,0:T(8,128)(2,1)}, bf16[512,768]{1,0:T(8,128)(2,1)}, f32[512,512]{1,0:T(8,128)}, bf16[392,256]{1,0:T(8,128)(2,1)}) custom-call(bf16[392,512]{1,0:T(8,128)(2,1)} %x_ref.5, f32[1,512]{1,0:T(1,128)} %bitcast.25, f32[1,512]{1,0:T(1,128)} %bitcast.28, bf16[3,512,256]{2,1,0:T(8,128)(2,1)} %bitcast.20, ...), custom_call_target="tpu_custom_call" | custom-call | tf_op jit(solution)/shard_map/attn_forward/pallas_call | solution.py:442
  12.6 3.0 %collective-permute-start = (bf16[392,512]{1,0:T(8,128)(2,1)}, bf16[392,512]{1,0:T(8,128)(2,1)S(1)}, u32[]{:S(2)}, u32[]{:S(2)}) collective-permute-start(bf16[392,512]{1,0:T(8,128)(2,1)} %get-tuple-element.53.own_ref), channel_id=1, source_target_pairs={{0,1},{1,0},{2,3},{3,2},{4,5},{5,4},{6,7},{7,6},{8,9},{9,8},{10,11... | collective-permute-start | bytes 1204232 | tf_op jit(solution)/shard_map/ppermute | solution.py:365
  15.6 9.5 %collective-permute-done.recv_ref = bf16[392,512]{1,0:T(8,128)(2,1)S(1)} collective-permute-done((bf16[392,512]{1,0:T(8,128)(2,1)}, bf16[392,512]{1,0:T(8,128)(2,1)S(1)}, u32[]{:S(2)}, u32[]{:S(2)}) %collective-permute-start) | collective-permute-done | bytes 401440 | tf_op jit(solution)/shard_map/ppermute | solution.py:365
  25.9 6.7 %mlp.1 = (bf16[392,512]{1,0:T(8,128)(2,1)}, f32[392,512]{1,0:T(8,128)}, bf16[392,512]{1,0:T(8,128)(2,1)}, bf16[392,1024]{1,0:T(8,128)(2,1)}, bf16[392,1024]{1,0:...) custom-call(bf16[392,512]{1,0:T(8,128)(2,1)} %x_ref.5, bf16[392,512]{1,0:T(8,128)(2,1)} %get-tuple-element.53.own_ref, ...), custom_call_target="tpu_custom_call" | custom-call | tf_op jit(solution)/shard_map/mlp/pallas_call | solution.py:466
  32.5 1.8 %collective-permute-start.2 = (bf16[392,512]{1,0:T(8,128)(2,1)}, bf16[392,512]{1,0:T(8,128)(2,1)S(1)}, u32[]{:S(2)}, u32[]{:S(2)}) collective-permute-start(bf16[392,512]{1,0:T(8,128)(2,1)} %get-tuple-element.59.own_ref), channel_id=1, source_target_pairs={{0,1},{1,0},{2,3},{3,2},{4,5},{5,4},{6,7},{7,6},{8,9},{9,8},{10,11... | collective-permute-start | bytes 1204232 | tf_op jit(solution)/shard_map/ppermute | solution.py:365
  34.4 4.4 %mlp_grad.1 = (bf16[1024,512]{1,0:T(8,128)(2,1)}, bf16[1024,512]{1,0:T(8,128)(2,1)}, bf16[392,512]{1,0:T(8,128)(2,1)}) custom-call(s32[1]{0:T(128)} %bitcast.9.bit_ref, bf16[392,1024]{1,0:T(8,128)(2,1)} %get-tuple-element.55.act_ref, bf16[392,1024]{1,0:T(8,128)(2,1)} %get-tuple-element.56.dub_ref, bf16[392,512]{1,0:T(8,128)(2,1)} %get-tuple-element.57.n2_ref, ...), custom_call_target="tpu_custom_call" | custom-call | flops 1233125376 | bytes 8388608 | tf_op jit(solution)/shard_map/mlp_grad/pallas_call | solution.py:495
  38.8 4.5 %collective-permute-done.2.recv_ref = bf16[392,512]{1,0:T(8,128)(2,1)S(1)} collective-permute-done((bf16[392,512]{1,0:T(8,128)(2,1)}, bf16[392,512]{1,0:T(8,128)(2,1)S(1)}, u32[]{:S(2)}, u32[]{:S(2)}) %collective-permute-start.2) | collective-permute-done | bytes 401440 | tf_op jit(solution)/shard_map/ppermute | solution.py:365
  44.0 10.1 %attn_backward.1 = (bf16[392,512]{1,0:T(8,128)(2,1)}, f32[392,512]{1,0:T(8,128)}, bf16[392,512]{1,0:T(8,128)(2,1)}, bf16[392,768]{1,0:T(8,128)(2,1)}, f32[4,512]{1,0:T(4,128)}, /*index=5*/f32[64,512]{1,0:T(8,128)}) custom-call(bf16[392,512]{1,0:T(8,128)(2,1)} %dy_ref.5, bf16[392,512]{1,0:T(8,128)(2,1)} %get-tuple-element.59.own_ref, ...), custom_call_target="tpu_custom_call" | custom-call | tf_op jit(solution)/shard_map/attn_backward/pallas_call | solution.py:510
  54.1 3.0 %attn_grad.1 = (bf16[256,1024]{1,0:T(8,128)(2,1)}, bf16[256,1024]{1,0:T(8,128)(2,1)}) custom-call(s32[1]{0:T(128)} %bitcast.9.bit_ref, bf16[392,512]{1,0:T(8,128)(2,1)} %get-tuple-element.72.n1_ref, bf16[392,768]{1,0:T(8,128)(2,1)} %get-tuple-element.73.dp_ref, bf16[392,256]{1,0:T(8,128)(2,1)} %get-tuple-element.74.otok_ref, ...), custom_call_target="tpu_custom_call" | custom-call | flops 411041792 | bytes 4194304 | tf_op jit(solution)/shard_map/attn_grad/pallas_call | solution.py:531
  57.1 2.1 %collective-permute-done.8 = bf16[256,1024]{1,0:T(8,128)(2,1)S(1)} collective-permute-done((bf16[256,1024]{1,0:T(8,128)(2,1)}, bf16[256,1024]{1,0:T(8,128)(2,1)S(1)}, u32[]{:S(2)}, u32[]{:S(2)}) %collective-permute-start.8) | collective-permute-done | bytes 524320 | tf_op jit(solution)/shard_map/ppermute | solution.py:365
  65.8 4.7 %collective-permute-done.9 = bf16[128,1024]{1,0:T(8,128)(2,1)S(1)} collective-permute-done((bf16[128,1024]{1,0:T(8,128)(2,1)}, bf16[128,1024]{1,0:T(8,128)(2,1)S(1)}, u32[]{:S(2)}, u32[]{:S(2)}) %collective-permute-start.9) | collective-permute-done | bytes 262176 | tf_op jit(solution)/shard_map/ppermute | solution.py:365
  72.3 8.7 %collective-permute-done.17 = bf16[512,512]{1,0:T(8,128)(2,1)S(1)} collective-permute-done((bf16[512,512]{1,0:T(8,128)(2,1)S(1)}, bf16[512,512]{1,0:T(8,128)(2,1)S(1)}, u32[]{:S(2)}, u32[]{:S(2)}) %collective-permute-start.17) | collective-permute-done | bytes 524320 | tf_op jit(solution)/shard_map/ppermute | solution.py:365
  81.2 1.6 collective-permute-start.18
  82.9 5.9 %collective-permute-done.18 = bf16[256,512]{1,0:T(8,128)(2,1)S(1)} collective-permute-done((bf16[256,512]{1,0:T(8,128)(2,1)S(1)}, bf16[256,512]{1,0:T(8,128)(2,1)S(1)}, u32[]{:S(2)}, u32[]{:S(2)}) %collective-permute-start.18) | collective-permute-done | bytes 262176 | tf_op jit(solution)/shard_map/ppermute | solution.py:365
  88.9 2.6 %collective-permute-start.19 = (bf16[128,512]{1,0:T(8,128)(2,1)S(1)}, bf16[128,512]{1,0:T(8,128)(2,1)S(1)}, u32[]{:S(2)}, u32[]{:S(2)}) collective-permute-start(bf16[128,512]{1,0:T(8,128)(2,1)S(1)} %broadcast_select_fusion.11), channel_id=1, source_target_pairs={{0,16},{2,18},{4,20},{6,22},{8,24},{10,26},{12,28},{14,30},{16,0},... | collective-permute-start | bytes 393224 | tf_op jit(solution)/shard_map/ppermute | solution.py:365
  92.0 7.1 %collective-permute-done.19 = bf16[128,512]{1,0:T(8,128)(2,1)S(1)} collective-permute-done((bf16[128,512]{1,0:T(8,128)(2,1)S(1)}, bf16[128,512]{1,0:T(8,128)(2,1)S(1)}, u32[]{:S(2)}, u32[]{:S(2)}) %collective-permute-start.19) | collective-permute-done | bytes 131104 | tf_op jit(solution)/shard_map/ppermute | solution.py:365
  100.5 1.7 collective-permute-start.12
  102.2 6.2 %collective-permute-done.20 = bf16[128,512]{1,0:T(8,128)(2,1)S(1)} collective-permute-done((bf16[128,512]{1,0:T(8,128)(2,1)S(1)}, bf16[128,512]{1,0:T(8,128)(2,1)S(1)}, u32[]{:S(2)}, u32[]{:S(2)}) %collective-permute-start.20) | collective-permute-done | bytes 131104 | tf_op jit(solution)/shard_map/ppermute | solution.py:365
  109.8 5.1 %collective-permute-done.21 = bf16[256,512]{1,0:T(8,128)(2,1)S(1)} collective-permute-done((bf16[256,512]{1,0:T(8,128)(2,1)S(1)}, bf16[256,512]{1,0:T(8,128)(2,1)S(1)}, u32[]{:S(2)}, u32[]{:S(2)}) %collective-permute-start.21) | collective-permute-done | bytes 262176 | tf_op jit(solution)/shard_map/ppermute | solution.py:365
  117.2 9.8 %collective-permute-done.13 = bf16[64,1024]{1,0:T(8,128)(2,1)S(1)} collective-permute-done((bf16[64,1024]{1,0:T(8,128)(2,1)S(1)}, bf16[64,1024]{1,0:T(8,128)(2,1)S(1)}, u32[]{:S(2)}, u32[]{:S(2)}) %collective-permute-start.13) | collective-permute-done | bytes 131104 | tf_op jit(solution)/shard_map/ppermute | solution.py:365
  128.0 1.6 collective-permute-start.3
  129.6 3.9 %collective-permute-done.14 = bf16[128,1024]{1,0:T(8,128)(2,1)S(1)} collective-permute-done((bf16[128,1024]{1,0:T(8,128)(2,1)S(1)}, bf16[128,1024]{1,0:T(8,128)(2,1)S(1)}, u32[]{:S(2)}, u32[]{:S(2)}) %collective-permute-start.14) | collective-permute-done | bytes 262176 | tf_op jit(solution)/shard_map/ppermute | solution.py:365
  133.7 1.6 collective-permute-start.1
  135.3 5.0 %table.1.tab_ref = f32[8,176]{1,0:T(8,128)} custom-call(f32[64,512]{1,0:T(8,128)} %get-tuple-element.67.dsum_ref, s32[49,49]{1,0:T(8,128)} %rel_ref.3, f32[8,512]{1,0:T(8,128)} %constant.27.clone.group_ref), custom_call_target="tpu_custom_call" | custom-call | tf_op jit(solution)/shard_map/table/pallas_call | solution.py:545
  140.5 3.1 %input_grad.1 = (f32[392,512]{1,0:T(8,128)}, f32[17,512]{1,0:T(8,128)}) custom-call(bf16[392,512]{1,0:T(8,128)(2,1)} %x_ref.5, bf16[392,512]{1,0:T(8,128)(2,1)} %get-tuple-element.62.own_ref, bf16[392,512]{1,0:T(8,128)(2,1)} %collective-permute-done.3.recv_ref, f32[392,512]{1,0:T(8,128)} %get-tuple-element.63.dh_ref, f32[1,512]{1,0:T(1,128)} %bitcast.26, ...), custom_call_target="tpu_custom_call" | custom-call | tf_op jit(solution)/shard_map/input_grad/pallas_call | solution.py:558
  143.6 4.7 %collective-permute-start.4 = (f32[17,512]{1,0:T(8,128)}, f32[17,512]{1,0:T(8,128)S(1)}, u32[]{:S(2)}, u32[]{:S(2)}) collective-permute-start(f32[17,512]{1,0:T(8,128)} %get-tuple-element.69), channel_id=1, source_target_pairs={{0,16},{2,18},{4,20},{6,22},{8,24},{10,26},{12,28},{14,30},{16,0},... | collective-permute-start | bytes 104456 | tf_op jit(solution)/shard_map/ppermute | solution.py:365
  148.3 2.6 %collective-permute-done.4 = f32[17,512]{1,0:T(8,128)S(1)} collective-permute-done((f32[17,512]{1,0:T(8,128)}, f32[17,512]{1,0:T(8,128)S(1)}, u32[]{:S(2)}, u32[]{:S(2)}) %collective-permute-start.4) | collective-permute-done | bytes 34848 | tf_op jit(solution)/shard_map/ppermute | solution.py:365
  151.8 4.0 %collective-permute-done.5 = f32[17,512]{1,0:T(8,128)S(1)} collective-permute-done((f32[17,512]{1,0:T(8,128)S(1)}, f32[17,512]{1,0:T(8,128)S(1)}, u32[]{:S(2)}, u32[]{:S(2)}) %collective-permute-start.5) | collective-permute-done | bytes 34848 | tf_op jit(solution)/shard_map/ppermute | solution.py:365
  157.4 2.6 %collective-permute-done.6 = f32[17,512]{1,0:T(8,128)S(1)} collective-permute-done((f32[17,512]{1,0:T(8,128)S(1)}, f32[17,512]{1,0:T(8,128)S(1)}, u32[]{:S(2)}, u32[]{:S(2)}) %collective-permute-start.6) | collective-permute-done | bytes 34848 | tf_op jit(solution)/shard_map/ppermute | solution.py:365
  160.6 2.3 %output.1 = bf16[392,512]{1,0:T(8,128)(2,1)} custom-call(f32[392,512]{1,0:T(8,128)} %get-tuple-element.54.h1_ref, bf16[392,512]{1,0:T(8,128)(2,1)} %get-tuple-element.58.own_ref, bf16[392,512]{1,0:T(8,128)(2,1)} %collective-permute-done.1.recv_ref, f32[1,512]{1,0:T(1,128)} %bitcast.31), custom_call_target="tpu_custom_call" | custom-call | tf_op jit(solution)/shard_map/output/pallas_call | solution.py:553
  165.1 2.6 %attn_finish.1 = (f32[3,512,256]{2,1,0:T(8,128)}, f32[256,512]{1,0:T(8,128)}) custom-call(s32[1]{0:T(128)} %bitcast.9.bit_ref, bf16[256,1024]{1,0:T(8,128)(2,1)} %copy-done.1, bf16[256,1024]{1,0:T(8,128)(2,1)} %copy-done.5), custom_call_target="tpu_custom_call" | custom-call | tf_op jit(solution)/shard_map/attn_finish/pallas_call | solution.py:591
  168.8 3.8 %mlp_finish.1 = (f32[1024,512]{1,0:T(8,128)}, f32[512,1024]{1,0:T(8,128)}) custom-call(s32[1]{0:T(128)} %bitcast.9.bit_ref, bf16[1024,512]{1,0:T(8,128)(2,1)} %copy-done, bf16[1024,512]{1,0:T(8,128)(2,1)} %copy-done.4), custom_call_target="tpu_custom_call" | custom-call | tf_op jit(solution)/shard_map/mlp_finish/pallas_call | solution.py:584
  (74 shorter events, 23.5 us)
Async XLA Ops:
  12.6 12.5 %collective-permute-start = (bf16[392,512]{1,0:T(8,128)(2,1)}, bf16[392,512]{1,0:T(8,128)(2,1)S(1)}, u32[]{:S(2)}, u32[]{:S(2)}) collective-permute-start(bf16[392,512]{1,0:T(8,128)(2,1)} %get-tuple-element.53.own_ref), channel_id=1, source_target_pairs={{0,1},{1,0},{2,3},{3,2},{4,5},{5,4},{6,7},{7,6},{8,9},{9,8},{10,11... | collective-permute-start | bytes 1204232 | tf_op jit(solution)/shard_map/ppermute | solution.py:365
  25.1 0.7 copy-start.6
  32.5 10.7 %collective-permute-start.2 = (bf16[392,512]{1,0:T(8,128)(2,1)}, bf16[392,512]{1,0:T(8,128)(2,1)S(1)}, u32[]{:S(2)}, u32[]{:S(2)}) collective-permute-start(bf16[392,512]{1,0:T(8,128)(2,1)} %get-tuple-element.59.own_ref), channel_id=1, source_target_pairs={{0,1},{1,0},{2,3},{3,2},{4,5},{5,4},{6,7},{7,6},{8,9},{9,8},{10,11... | collective-permute-start | bytes 1204232 | tf_op jit(solution)/shard_map/ppermute | solution.py:365
  38.8 23.8 %collective-permute-start.16 = (bf16[1024,512]{1,0:T(8,128)(2,1)}, bf16[1024,512]{1,0:T(8,128)(2,1)S(1)}, u32[]{:S(2)}, u32[]{:S(2)}) collective-permute-start(bf16[1024,512]{1,0:T(8,128)(2,1)} %get-tuple-element.86), channel_id=1, source_target_pairs={{0,2},{2,0},{4,6},{6,4},{8,10},{10,8},{12,14},{14,12},{16,18},{18,... | collective-permute-start | bytes 3145736 | tf_op jit(solution)/shard_map/ppermute | solution.py:365
  54.1 9.5 %copy-start.2 = (bf16[1024,512]{1,0:T(8,128)(2,1)S(1)}, bf16[1024,512]{1,0:T(8,128)(2,1)}, u32[]{:S(2)}) copy-start(bf16[1024,512]{1,0:T(8,128)(2,1)} %get-tuple-element.85) | copy-start | bytes 3145732
  57.1 2.1 %collective-permute-start.8 = (bf16[256,1024]{1,0:T(8,128)(2,1)}, bf16[256,1024]{1,0:T(8,128)(2,1)S(1)}, u32[]{:S(2)}, u32[]{:S(2)}) collective-permute-start(bf16[256,1024]{1,0:T(8,128)(2,1)} %get-tuple-element.77), channel_id=1, source_target_pairs={{0,2},{2,0},{4,6},{6,4},{8,10},{10,8},{12,14},{14,12},{16,18},{18,... | collective-permute-start | bytes 1572872 | tf_op jit(solution)/shard_map/ppermute | solution.py:365
  61.2 9.4 %collective-permute-start.9 = (bf16[128,1024]{1,0:T(8,128)(2,1)}, bf16[128,1024]{1,0:T(8,128)(2,1)S(1)}, u32[]{:S(2)}, u32[]{:S(2)}) collective-permute-start(bf16[128,1024]{1,0:T(8,128)(2,1)} %broadcast_select_fusion.6), channel_id=1, source_target_pairs={{0,4},{2,6},{4,0},{6,2},{8,12},{10,14},{12,8},{14,10},{16,20},{18,... | collective-permute-start | bytes 786440 | tf_op jit(solution)/shard_map/ppermute | solution.py:365
  62.6 1.0 copy-start.3
  65.2 15.8 %collective-permute-start.17 = (bf16[512,512]{1,0:T(8,128)(2,1)S(1)}, bf16[512,512]{1,0:T(8,128)(2,1)S(1)}, u32[]{:S(2)}, u32[]{:S(2)}) collective-permute-start(bf16[512,512]{1,0:T(8,128)(2,1)S(1)} %broadcast_select_fusion.2), channel_id=1, source_target_pairs={{0,4},{2,6},{4,0},{6,2},{8,12},{10,14},{12,8},{14,10},{16,20},{18,... | collective-permute-start | bytes 1572872 | tf_op jit(solution)/shard_map/ppermute | solution.py:365
  70.7 12.1 %collective-permute-start.10 = (bf16[64,1024]{1,0:T(8,128)(2,1)S(1)}, bf16[64,1024]{1,0:T(8,128)(2,1)S(1)}, u32[]{:S(2)}, u32[]{:S(2)}) collective-permute-start(bf16[64,1024]{1,0:T(8,128)(2,1)S(1)} %broadcast_select_fusion.12), channel_id=1, source_target_pairs={{0,8},{2,10},{4,12},{6,14},{8,0},{10,2},{12,4},{14,6},{16,24},{18,... | collective-permute-start | bytes 393224 | tf_op jit(solution)/shard_map/ppermute | solution.py:365
  81.2 7.6 %collective-permute-start.18 = (bf16[256,512]{1,0:T(8,128)(2,1)S(1)}, bf16[256,512]{1,0:T(8,128)(2,1)S(1)}, u32[]{:S(2)}, u32[]{:S(2)}) collective-permute-start(bf16[256,512]{1,0:T(8,128)(2,1)S(1)} %broadcast_select_fusion.5), channel_id=1, source_target_pairs={{0,8},{2,10},{4,12},{6,14},{8,0},{10,2},{12,4},{14,6},{16,24},{18,... | collective-permute-start | bytes 786440 | tf_op jit(solution)/shard_map/ppermute | solution.py:365
  88.9 10.1 %collective-permute-start.19 = (bf16[128,512]{1,0:T(8,128)(2,1)S(1)}, bf16[128,512]{1,0:T(8,128)(2,1)S(1)}, u32[]{:S(2)}, u32[]{:S(2)}) collective-permute-start(bf16[128,512]{1,0:T(8,128)(2,1)S(1)} %broadcast_select_fusion.11), channel_id=1, source_target_pairs={{0,16},{2,18},{4,20},{6,22},{8,24},{10,26},{12,28},{14,30},{16,0},... | collective-permute-start | bytes 393224 | tf_op jit(solution)/shard_map/ppermute | solution.py:365
  91.5 8.9 %collective-permute-start.11 = (bf16[32,1024]{1,0:T(8,128)(2,1)S(1)}, bf16[32,1024]{1,0:T(8,128)(2,1)S(1)}, u32[]{:S(2)}, u32[]{:S(2)}) collective-permute-start(bf16[32,1024]{1,0:T(8,128)(2,1)S(1)} %broadcast_select_fusion.17), channel_id=1, source_target_pairs={{0,16},{2,18},{4,20},{6,22},{8,24},{10,26},{12,28},{14,30},{16,0},... | collective-permute-start | bytes 196616 | tf_op jit(solution)/shard_map/ppermute | solution.py:365
  99.1 9.3 %collective-permute-start.20 = (bf16[128,512]{1,0:T(8,128)(2,1)S(1)}, bf16[128,512]{1,0:T(8,128)(2,1)S(1)}, u32[]{:S(2)}, u32[]{:S(2)}) collective-permute-start(bf16[128,512]{1,0:T(8,128)(2,1)S(1)} %add_convert_fusion.5), channel_id=1, source_target_pairs={{0,16},{2,18},{4,20},{6,22},{8,24},{10,26},{12,28},{14,30},{16,0},... | collective-permute-start | bytes 393224 | tf_op jit(solution)/shard_map/ppermute | solution.py:365
  100.5 9.3 %collective-permute-start.12 = (bf16[32,1024]{1,0:T(8,128)(2,1)S(1)}, bf16[32,1024]{1,0:T(8,128)(2,1)S(1)}, u32[]{:S(2)}, u32[]{:S(2)}) collective-permute-start(bf16[32,1024]{1,0:T(8,128)(2,1)S(1)} %add_convert_fusion.7), channel_id=1, source_target_pairs={{0,16},{2,18},{4,20},{6,22},{8,24},{10,26},{12,28},{14,30},{16,0},... | collective-permute-start | bytes 196616 | tf_op jit(solution)/shard_map/ppermute | solution.py:365
  108.5 6.4 %collective-permute-start.21 = (bf16[256,512]{1,0:T(8,128)(2,1)S(1)}, bf16[256,512]{1,0:T(8,128)(2,1)S(1)}, u32[]{:S(2)}, u32[]{:S(2)}) collective-permute-start(bf16[256,512]{1,0:T(8,128)(2,1)S(1)} %pad_maximum_fusion.4), channel_id=1, source_target_pairs={{0,8},{2,10},{4,12},{6,14},{8,0},{10,2},{12,4},{14,6},{16,24},{18,... | collective-permute-start | bytes 786440 | tf_op jit(solution)/shard_map/ppermute | solution.py:365
  115.0 12.6 %collective-permute-start.22 = (bf16[512,512]{1,0:T(8,128)(2,1)S(1)}, bf16[512,512]{1,0:T(8,128)(2,1)S(1)}, u32[]{:S(2)}, u32[]{:S(2)}) collective-permute-start(bf16[512,512]{1,0:T(8,128)(2,1)S(1)} %pad_maximum_fusion.2), channel_id=1, source_target_pairs={{0,4},{2,6},{4,0},{6,2},{8,12},{10,14},{12,8},{14,10},{16,20},{18,... | collective-permute-start | bytes 1572872 | tf_op jit(solution)/shard_map/ppermute | solution.py:365
  116.6 10.4 %collective-permute-start.13 = (bf16[64,1024]{1,0:T(8,128)(2,1)S(1)}, bf16[64,1024]{1,0:T(8,128)(2,1)S(1)}, u32[]{:S(2)}, u32[]{:S(2)}) collective-permute-start(bf16[64,1024]{1,0:T(8,128)(2,1)S(1)} %pad_maximum_fusion.5), channel_id=1, source_target_pairs={{0,4},{2,6},{4,0},{6,2},{8,12},{10,14},{12,8},{14,10},{16,20},{18,... | collective-permute-start | bytes 393224 | tf_op jit(solution)/shard_map/ppermute | solution.py:365
  127.1 6.4 %collective-permute-start.14 = (bf16[128,1024]{1,0:T(8,128)(2,1)S(1)}, bf16[128,1024]{1,0:T(8,128)(2,1)S(1)}, u32[]{:S(2)}, u32[]{:S(2)}) collective-permute-start(bf16[128,1024]{1,0:T(8,128)(2,1)S(1)} %pad_maximum_fusion.3), channel_id=1, source_target_pairs={{0,8},{2,10},{4,12},{6,14},{8,0},{10,2},{12,4},{14,6},{16,24},{18,... | collective-permute-start | bytes 786440 | tf_op jit(solution)/shard_map/ppermute | solution.py:365
  127.8 5.9 %copy-start.7 = (bf16[392,512]{1,0:T(8,128)(2,1)S(1)}, bf16[392,512]{1,0:T(8,128)(2,1)}, u32[]{:S(2)}) copy-start(bf16[392,512]{1,0:T(8,128)(2,1)} %get-tuple-element.58.own_ref) | copy-start | bytes 1204228
  127.9 15.7 %copy-start = (bf16[1024,512]{1,0:T(8,128)(2,1)}, bf16[1024,512]{1,0:T(8,128)(2,1)S(1)}, u32[]{:S(2)}) copy-start(bf16[1024,512]{1,0:T(8,128)(2,1)S(1)} %pad_maximum_fusion.mine_ref) | copy-start | bytes 3145732
  127.9 39.9 %collective-permute-start.23 = (bf16[1024,512]{1,0:T(8,128)(2,1)S(1)}, bf16[1024,512]{1,0:T(8,128)(2,1)S(1)}, u32[]{:S(2)}, u32[]{:S(2)}) collective-permute-start(bf16[1024,512]{1,0:T(8,128)(2,1)S(1)} %pad_maximum_fusion.mine_ref), channel_id=1, source_target_pairs={{0,2},{2,0},{4,6},{6,4},{8,10},{10,8},{12,14},{14,12},{16,18},{18,... | collective-permute-start | bytes 3145736 | tf_op jit(solution)/shard_map/ppermute | solution.py:365
  128.0 12.5 %collective-permute-start.3 = (bf16[392,512]{1,0:T(8,128)(2,1)}, bf16[392,512]{1,0:T(8,128)(2,1)}, u32[]{:S(2)}, u32[]{:S(2)}) collective-permute-start(bf16[392,512]{1,0:T(8,128)(2,1)} %get-tuple-element.62.own_ref), channel_id=1, source_target_pairs={{0,1},{1,0},{2,3},{3,2},{4,5},{5,4},{6,7},{7,6},{8,9},{9,8},{10,11... | collective-permute-start | bytes 1204232 | tf_op jit(solution)/shard_map/ppermute | solution.py:365
  133.6 29.2 %copy-start.1 = (bf16[256,1024]{1,0:T(8,128)(2,1)}, bf16[256,1024]{1,0:T(8,128)(2,1)S(1)}, u32[]{:S(2)}) copy-start(bf16[256,1024]{1,0:T(8,128)(2,1)S(1)} %pad_maximum_fusion.1.mine_ref) | copy-start | bytes 1572868
  133.7 30.7 %collective-permute-start.15 = (bf16[256,1024]{1,0:T(8,128)(2,1)S(1)}, bf16[256,1024]{1,0:T(8,128)(2,1)S(1)}, u32[]{:S(2)}, u32[]{:S(2)}) collective-permute-start(bf16[256,1024]{1,0:T(8,128)(2,1)S(1)} %pad_maximum_fusion.1.mine_ref), channel_id=1, source_target_pairs={{0,2},{2,0},{4,6},{6,4},{8,10},{10,8},{12,14},{14,12},{16,18},{18,... | collective-permute-start | bytes 1572872 | tf_op jit(solution)/shard_map/ppermute | solution.py:365
  133.7 26.9 %collective-permute-start.1 = (bf16[392,512]{1,0:T(8,128)(2,1)S(1)}, bf16[392,512]{1,0:T(8,128)(2,1)}, u32[]{:S(2)}, u32[]{:S(2)}) collective-permute-start(bf16[392,512]{1,0:T(8,128)(2,1)S(1)} %copy-done.7), channel_id=1, source_target_pairs={{0,1},{1,0},{2,3},{3,2},{4,5},{5,4},{6,7},{7,6},{8,9},{9,8},{10,11... | collective-permute-start | bytes 1204232 | tf_op jit(solution)/shard_map/ppermute | solution.py:365
  143.6 7.3 %collective-permute-start.4 = (f32[17,512]{1,0:T(8,128)}, f32[17,512]{1,0:T(8,128)S(1)}, u32[]{:S(2)}, u32[]{:S(2)}) collective-permute-start(f32[17,512]{1,0:T(8,128)} %get-tuple-element.69), channel_id=1, source_target_pairs={{0,16},{2,18},{4,20},{6,22},{8,24},{10,26},{12,28},{14,30},{16,0},... | collective-permute-start | bytes 104456 | tf_op jit(solution)/shard_map/ppermute | solution.py:365
  151.7 4.1 %collective-permute-start.5 = (f32[17,512]{1,0:T(8,128)S(1)}, f32[17,512]{1,0:T(8,128)S(1)}, u32[]{:S(2)}, u32[]{:S(2)}) collective-permute-start(f32[17,512]{1,0:T(8,128)S(1)} %add.33), channel_id=1, source_target_pairs={{0,8},{2,10},{4,12},{6,14},{8,0},{10,2},{12,4},{14,6},{16,24},{18,... | collective-permute-start | bytes 104456 | tf_op jit(solution)/shard_map/ppermute | solution.py:365
  155.8 4.2 %collective-permute-start.6 = (f32[17,512]{1,0:T(8,128)S(1)}, f32[17,512]{1,0:T(8,128)S(1)}, u32[]{:S(2)}, u32[]{:S(2)}) collective-permute-start(f32[17,512]{1,0:T(8,128)S(1)} %add.34), channel_id=1, source_target_pairs={{0,4},{2,6},{4,0},{6,2},{8,12},{10,14},{12,8},{14,10},{16,20},{18,... | collective-permute-start | bytes 104456 | tf_op jit(solution)/shard_map/ppermute | solution.py:365
  160.6 2.3 %collective-permute-start.7 = (f32[17,512]{1,0:T(8,128)}, f32[17,512]{1,0:T(8,128)}, u32[]{:S(2)}, u32[]{:S(2)}) collective-permute-start(f32[17,512]{1,0:T(8,128)} %add.35.left_ref), channel_id=1, source_target_pairs={{0,2},{2,0},{4,6},{6,4},{8,10},{10,8},{12,14},{14,12},{16,18},{18,... | collective-permute-start | bytes 104456 | tf_op jit(solution)/shard_map/ppermute | solution.py:365
  164.3 0.8 copy-start.5
  167.8 1.0 copy-start.4
  (1 other events, 0.7 us)

commit v3 on v2

v3 whole, which is shorter than its diff:
```python
import functools

import numpy as np
import jax
import jax.numpy as jnp
from jax import lax
from jax.experimental import pallas as pl
from jax.experimental.pallas import tpu as pltpu
from jax.sharding import PartitionSpec as P

HEAD_DIM = 32
SIDE = 14
WIN = 7
SHIFT = 3
ACROSS = SIDE // WIN
POSITIONS = WIN * WIN
PAD = 64
WINDOWS = ACROSS * ACROSS

NORM_EPS = 1e-05
MASKED = -1e30
F32 = jnp.float32
BF16 = jnp.bfloat16
HIDDEN_BLOCK = 256


def dot(a, b, dims=((1,), (0,)), precision=None):
    return lax.dot_general(a, b, (dims, ((), ())), preferred_element_type=F32, precision=precision)


NT = ((1,), (1,))
TN = ((0,), (0,))


def normed(values):
    centered = values - jnp.mean(values, axis=-1, keepdims=True)
    inverse = lax.rsqrt(jnp.mean(centered * centered, axis=-1, keepdims=True) + NORM_EPS)
    return centered * inverse, inverse


def norm_backward(upstream, unit, inverse, gain):
    weighted = upstream * gain
    return inverse * (
        weighted
        - jnp.mean(weighted, axis=-1, keepdims=True)
        - unit * jnp.mean(weighted * unit, axis=-1, keepdims=True)
    )


def window_order(shift=SHIFT):
    order = np.zeros((WINDOWS * PAD, SIDE * SIDE), np.float32)
    for a in range(ACROSS):
        for b in range(ACROSS):
            for i in range(POSITIONS):
                row = (a * WIN + i // WIN + shift) % SIDE
                col = (b * WIN + i % WIN + shift) % SIDE
                order[(a * ACROSS + b) * PAD + i, row * SIDE + col] = 1.0
    return order


GROUP = 128 // HEAD_DIM


def head_lanes(dtype):
    lane = lax.broadcasted_iota(jnp.int32, (PAD, 128), 1) // HEAD_DIM
    return [(lane == h).astype(dtype) for h in range(GROUP)]


def spread_heads(tile, masks):
    return jnp.concatenate([tile * mask for mask in masks], axis=0)


def gather_heads(full):
    lane = lax.broadcasted_iota(jnp.int32, (PAD, 128), 1) // HEAD_DIM
    total = full[:PAD, :]
    for h in range(1, GROUP):
        total = jnp.where(lane == h, full[h * PAD : (h + 1) * PAD, :], total)
    return total


def slab(image):
    start = image * SIDE * SIDE // 8 * 8
    return start, -(-SIDE * SIDE // 8) * 8, image * SIDE * SIDE - start


def own_rows(image, rows):
    offset = slab(image)[2]
    at = lax.broadcasted_iota(jnp.int32, (rows, 1), 0)
    return ((at >= offset) & (at < offset + SIDE * SIDE)).astype(F32)


def pair_index(rel_ref):
    lane = lax.broadcasted_iota(jnp.int32, (POSITIONS, 2 * PAD), 1)
    sub = lax.broadcasted_iota(jnp.int32, (POSITIONS, 2 * PAD), 0)
    same = (lax.rem(lane, PAD) == sub).astype(BF16)
    spread = dot((rel_ref[...] + 1).astype(F32).astype(BF16), same, TN)
    zero = jnp.zeros((PAD - POSITIONS, 2 * PAD), F32)
    return jnp.concatenate([spread, zero], axis=0).astype(jnp.int32)


def bias_kernel(table_ref, rel_ref, reg_ref, order_ref, bm_ref):
    heads, entries = table_ref.shape
    index = pair_index(rel_ref) - 1
    first = jnp.clip(index, 0, 127)
    second = jnp.clip(index - 128, 0, 127)
    left = lax.broadcasted_iota(jnp.int32, index.shape, 1) < PAD

    def pick(h):
        low = jnp.broadcast_to(table_ref[h : h + 1, :128], index.shape)
        high = jnp.concatenate(
            [table_ref[h : h + 1, 128:], jnp.zeros((1, 256 - entries), F32)], axis=1
        )
        high = jnp.broadcast_to(high, index.shape)
        return jnp.where(
            index < 128,
            jnp.take_along_axis(low, first, axis=1),
            jnp.take_along_axis(high, second, axis=1),
        )

    region = jnp.broadcast_to((reg_ref[...] + 1).astype(F32), (16, reg_ref.shape[1])).astype(BF16)
    order = order_ref[...]
    across = dot(region, order, NT)
    down = dot(order, region, NT)
    hits = []
    for w in range(WINDOWS):
        rows = slice(w * PAD, (w + 1) * PAD)
        hits.append(down[rows, 0:1] == jnp.concatenate([across[0:1, rows]] * 2, axis=1))
    for p in range(heads // 2):
        bias = jnp.where(left, pick(2 * p), pick(2 * p + 1))
        for w in range(WINDOWS):
            rows = slice(w * PAD, (w + 1) * PAD)
            bm_ref[rows, p * 128 : (p + 1) * 128] = jnp.where(hits[w], bias, MASKED)


def attn_forward_kernel(
    image, x_ref, gain_ref, shift_ref, wqkv_ref, qvb_ref, bm_ref, perm_ref, wproj_ref,
    part_ref, n1_ref, qkvw_ref, prob_ref, otok_ref,
    ow_ref,
):
    inner = wproj_ref.shape[0]
    start, size, _ = slab(image)
    unit, _ = normed(x_ref[start : start + size, :].astype(F32))
    n1 = (unit * gain_ref[...] + shift_ref[...]).astype(BF16)
    n1_ref[...] = n1
    q = ((dot(n1, wqkv_ref[0]) + qvb_ref[0:1, :]) * (HEAD_DIM ** (-0.5))).astype(BF16)
    k = dot(n1, wqkv_ref[1]).astype(BF16)
    v = (dot(n1, wqkv_ref[2]) + qvb_ref[1:2, :]).astype(BF16)
    perm = perm_ref[...]
    qkvw_ref[:, :inner] = dot(perm, q).astype(BF16)
    qkvw_ref[:, inner : 2 * inner] = dot(perm, k).astype(BF16)
    qkvw_ref[:, 2 * inner :] = dot(perm, v).astype(BF16)

    def window(i, carry):
        rows = pl.ds(pl.multiple_of(i * PAD, PAD), PAD)
        masks = head_lanes(BF16)
        for g in range(inner // 128):
            cols = slice(g * 128, (g + 1) * 128)
            wide = slice(g * GROUP * PAD, (g + 1) * GROUP * PAD)
            at = lambda n: slice(n * inner + g * 128, n * inner + (g + 1) * 128)
            spread = spread_heads(qkvw_ref[rows, at(0)], masks)
            s = dot(qkvw_ref[rows, at(1)], spread, NT) + bm_ref[rows, wide]
            e = jnp.exp(s - jnp.max(s, axis=0, keepdims=True))
            p = e * (1.0 / jnp.sum(e, axis=0, keepdims=True))
            prob_ref[rows, wide] = p
            full = dot(p.astype(BF16), qkvw_ref[rows, at(2)], TN)
            ow_ref[rows, cols] = gather_heads(full).astype(BF16)
        return carry

    lax.fori_loop(0, WINDOWS, window, 0)
    otok = dot(perm, ow_ref[...], TN).astype(BF16)
    otok_ref[...] = otok
    part_ref[...] = dot(otok, wproj_ref[...]).astype(BF16)


def mlp_kernel(
    x_ref, own0_ref, recv0_ref, own1_ref, recv1_ref, pbias_ref, gain_ref, shift_ref, w1_ref,
    b1_ref, w2_ref, dy_ref,
    back_ref, h1_ref, n2_ref, act_ref, dub_ref, gb1_ref, gb2_ref,
    acc_ref,
):
    step = pl.program_id(0)

    @pl.when(step == 0)
    def _():
        h1_ref[...] = x_ref[...].astype(F32) + pbias_ref[...]
        for image, (own, recv) in enumerate(((own0_ref, recv0_ref), (own1_ref, recv1_ref))):
            start, size, _ = slab(image)
            total = own[...].astype(F32) + recv[...].astype(F32)
            h1_ref[start : start + size, :] += total
        unit, _ = normed(h1_ref[...])
        n2_ref[...] = (unit * gain_ref[...] + shift_ref[...]).astype(BF16)
        gb2_ref[...] = jnp.sum(dy_ref[...].astype(F32), axis=0, keepdims=True)
        acc_ref[...] = jnp.zeros_like(acc_ref)

    u = dot(n2_ref[...], w1_ref[...]) + b1_ref[...]
    cdf = 0.5 * (1.0 + lax.erf(u * 0.7071067811865476))
    act_ref[...] = (u * cdf).astype(BF16)
    slope = cdf + u * jnp.exp(-0.5 * u * u) * 0.3989422804014327
    du = dot(dy_ref[...], w2_ref[...], NT) * slope
    gb1_ref[...] = jnp.sum(du, axis=0, keepdims=True)
    dub = du.astype(BF16)
    dub_ref[...] = dub
    acc_ref[...] += dot(dub, w1_ref[...], NT)

    @pl.when(step == pl.num_programs(0) - 1)
    def _():
        back_ref[...] = acc_ref[...].astype(BF16)


def half(ref, which, size):
    return ref[:, pl.ds(pl.multiple_of(which * size, size), size)]


def mlp_grad_kernel(flip, bit_ref, act_ref, dub_ref, n2_ref, dy_ref, out_ref):
    which = bit_ref[0] if flip == 0 else 1 - bit_ref[0]
    size = act_ref.shape[1] // 2
    width = dy_ref.shape[1]
    out_ref[:, :width] = dot(half(act_ref, which, size), dy_ref[...], TN).astype(BF16)
    out_ref[:, width:] = dot(n2_ref[...], half(dub_ref, which, size), TN).astype(BF16)


def mlp_out_kernel(act_ref, w2_ref, part_ref):
    part_ref[...] = dot(act_ref[...], w2_ref[...]).astype(BF16)


def attn_backward_kernel(
    image, dy_ref, own_ref, recv_ref, h1_ref, gain_ref, wproj_ref, qkvw_ref, prob_ref, perm_ref,
    wqkv_ref,
    part_ref, dh_ref, dhb_ref, dp_ref, sums_ref, dsum_ref,
    dow_ref, dqkv_ref,
):
    inner = wproj_ref.shape[0]
    start, size, _ = slab(image)
    slab_rows = slice(start, start + size)
    mask = own_rows(image, size)
    dn2 = own_ref[slab_rows, :].astype(F32) + recv_ref[slab_rows, :].astype(F32)
    unit, inverse = normed(h1_ref[slab_rows, :])
    mine = dn2 * mask
    sums_ref[0:1, :] = jnp.sum(mine * unit, axis=0, keepdims=True)
    sums_ref[1:2, :] = jnp.sum(mine, axis=0, keepdims=True)
    dh = dy_ref[slab_rows, :].astype(F32) + norm_backward(dn2, unit, inverse, gain_ref[...])
    dh_ref[...] = dh
    sums_ref[2:3, :] = jnp.sum(dh * mask, axis=0, keepdims=True)
    dhb = dh.astype(BF16)
    dhb_ref[...] = dhb
    perm = perm_ref[...]
    dow_ref[...] = dot(perm, dot(dhb, wproj_ref[...], NT).astype(BF16)).astype(BF16)
    dsum_ref[...] = jnp.zeros_like(dsum_ref)
    groups = inner // 128

    def window(i, carry):
        rows = pl.ds(pl.multiple_of(i * PAD, PAD), PAD)
        masks = head_lanes(BF16)
        sums = []
        for g in range(groups):
            wide = slice(g * GROUP * PAD, (g + 1) * GROUP * PAD)
            at = lambda n: slice(n * inner + g * 128, n * inner + (g + 1) * 128)
            qblk = spread_heads(qkvw_ref[rows, at(0)], masks)
            oblk = spread_heads(dow_ref[rows, at(0)], masks)
            p = prob_ref[rows, wide]
            dp = dot(qkvw_ref[rows, at(2)], oblk, NT)
            ds = p * (dp - jnp.sum(p * dp, axis=0, keepdims=True))
            dsum_ref[:, wide] += ds
            dsb = ds.astype(BF16)
            dq = gather_heads(dot(dsb, qkvw_ref[rows, at(1)], TN)) * (HEAD_DIM ** (-0.5))
            dv = dot(p.astype(BF16), oblk)
            dqkv_ref[rows, at(0)] = dq.astype(BF16)
            dqkv_ref[rows, at(1)] = dot(dsb, qblk).astype(BF16)
            dqkv_ref[rows, at(2)] = dv.astype(BF16)
            sums += [jnp.sum(dq, axis=0, keepdims=True), jnp.sum(dv, axis=0, keepdims=True)]
        return tuple(a + b for a, b in zip(carry, sums))

    zero = jnp.zeros((1, 128), F32)
    sums = lax.fori_loop(0, WINDOWS, window, (zero,) * (2 * groups))
    for g in range(groups):
        sums_ref[3:4, g * 128 : (g + 1) * 128] = sums[2 * g]
        sums_ref[3:4, inner + g * 128 : inner + (g + 1) * 128] = sums[2 * g + 1]
    dp_tok = dot(perm, dqkv_ref[...], TN).astype(BF16)
    dp_ref[...] = dp_tok
    part = dot(dp_tok[:, :inner], wqkv_ref[0], NT)
    part = part + dot(dp_tok[:, inner : 2 * inner], wqkv_ref[1], NT)
    part_ref[...] = (part + dot(dp_tok[:, 2 * inner :], wqkv_ref[2], NT)).astype(BF16)


def attn_grad_kernel(
    flip, bit_ref, n1a_ref, n1b_ref, dpa_ref, dpb_ref, oa_ref, ob_ref, dha_ref, dhb_ref, out_ref
):
    which = bit_ref[0] if flip == 0 else 1 - bit_ref[0]
    wide = dpa_ref.shape[1]
    rows = n1a_ref.shape[1] // 2
    qkv = dot(half(n1a_ref, which, rows), dpa_ref[...], TN)
    out_ref[:, :wide] = (qkv + dot(half(n1b_ref, which, rows), dpb_ref[...], TN)).astype(BF16)
    proj = dot(oa_ref[...], half(dha_ref, which, rows), TN)
    out_ref[:, wide:] = (proj + dot(ob_ref[...], half(dhb_ref, which, rows), TN)).astype(BF16)


def table_kernel(dsa_ref, dsb_ref, rel_ref, group_ref, out_ref, tab_ref, dsum_ref):
    rel = pair_index(rel_ref)
    width = rel.shape[1]
    pairs = dsum_ref.shape[1] // width
    dsum_ref[...] = dsa_ref[...] + dsb_ref[...]

    def eight(n, carry):
        for p in range(pairs):
            cols = slice(p * width, (p + 1) * width)
            part = dsum_ref[:, cols]
            found = [
                jnp.sum(jnp.where(rel == n * 8 + t + 1, part, 0.0), axis=0, keepdims=True)
                for t in range(8)
            ]
            tab_ref[pl.ds(pl.multiple_of(n * 8, 8), 8), cols] = jnp.concatenate(found, axis=0)
        return carry

    lax.fori_loop(0, tab_ref.shape[0] // 8, eight, 0)
    out_ref[...] = dot(group_ref[...], tab_ref[...], NT, lax.Precision.HIGHEST)


def input_grad_kernel(
    x_ref, own0_ref, recv0_ref, own1_ref, recv1_ref, dh0_ref, dh1_ref, gain_ref,
    sums0_ref, sums1_ref, gb1_ref, gb2_ref, tab_ref,
    gin_ref, small_ref,
):
    width = x_ref.shape[1]
    small_ref[...] = jnp.zeros_like(small_ref)
    for image, (own, recv, dh) in enumerate(
        ((own0_ref, recv0_ref, dh0_ref), (own1_ref, recv1_ref, dh1_ref))
    ):
        start, size, offset = slab(image)
        unit, inverse = normed(x_ref[start : start + size, :].astype(F32))
        dn1 = own[...].astype(F32) + recv[...].astype(F32)
        small_ref[0:1, :] += jnp.sum(dn1 * unit, axis=0, keepdims=True)
        small_ref[1:2, :] += jnp.sum(dn1, axis=0, keepdims=True)
        gin = dh[...] + norm_backward(dn1, unit, inverse, gain_ref[...])
        if offset == 0:
            gin_ref[start : start + size, :] = gin
        else:
            at = lax.broadcasted_iota(jnp.int32, (8, 1), 0)
            gin_ref[start : start + 8, :] = jnp.where(
                at < offset, gin_ref[start : start + 8, :], gin[:8, :]
            )
            gin_ref[start + 8 : start + size, :] = gin[8:, :]
    small_ref[2:6, :] = sums0_ref[...] + sums1_ref[...]
    small_ref[6:7, :] = gb2_ref[...]
    at = 7
    for n in range(gb1_ref.shape[1] // width):
        small_ref[at : at + 1, :] = gb1_ref[:, n * width : (n + 1) * width]
        at += 1
    for h in range(tab_ref.shape[0]):
        small_ref[at : at + 1, : tab_ref.shape[1]] = tab_ref[h : h + 1, :]
        at += 1


def small_kernel(
    left_ref, right_ref,
    gain1_ref, shift1_ref, gain2_ref, shift2_ref, pbias_ref, qvb_ref, gb2_ref, gb1_ref, tab_ref,
):
    small = left_ref[...] + right_ref[...]
    width = small.shape[1]
    inner = qvb_ref.shape[1]
    for n, out in enumerate((gain1_ref, shift1_ref, gain2_ref, shift2_ref, pbias_ref)):
        out[...] = small[n : n + 1, :]
    qvb_ref[0:1, :] = small[5:6, :inner]
    qvb_ref[1:2, :] = small[5:6, inner:]
    gb2_ref[...] = small[6:7, :]
    at = 7
    for n in range(gb1_ref.shape[1] // width):
        gb1_ref[:, n * width : (n + 1) * width] = small[at : at + 1, :]
        at += 1
    tab_ref[...] = small[at : at + tab_ref.shape[0], : tab_ref.shape[1]]


def mlp_finish_kernel(bits, index_ref, mine_ref, other_ref, fc2_ref, fc1_ref):
    index = index_ref[0]
    total, width = mine_ref.shape[0], fc2_ref.shape[1]
    rows = total >> len(bits)
    for n in range(1 << len(bits)):
        to = 0
        for place, bit in enumerate(bits):
            away = (n >> place) & 1
            set_here = lax.shift_right_logical(index, bit.bit_length() - 1) & 1
            to = to + ((1 - set_here) if away else set_here) * (rows << place)
        for src, away in ((mine_ref, 0), (other_ref, 1)):
            which = (index & 1) if away == 0 else 1 - (index & 1)
            block = src[n * rows : (n + 1) * rows, :]
            at = pl.multiple_of(which * total + to, 8)
            fc2_ref[pl.ds(at, rows), :] = block[:, :width].astype(F32)
            cols = pl.ds(pl.multiple_of(which * total, 128), total)
            fc1_ref[pl.ds(pl.multiple_of(to, 8), rows), cols] = block[:, width:].astype(F32)


def attn_finish_kernel(bit_ref, mine_ref, other_ref, qkv_ref, proj_ref):
    inner = qkv_ref.shape[2]
    half_rows = qkv_ref.shape[1] // 2
    block = half_rows // 4
    for src, which in ((mine_ref, bit_ref[0]), (other_ref, 1 - bit_ref[0])):
        for n in range(3):
            for a in range(2):
                for b in range(2):
                    to = pl.multiple_of(which * half_rows + (b * 2 + a) * block, block)
                    rows = slice((a * 2 + b) * block, (a * 2 + b + 1) * block)
                    cols = slice(n * inner, (n + 1) * inner)
                    qkv_ref[n, pl.ds(to, block), :] = src[rows, cols].astype(F32)
        at = pl.ds(pl.multiple_of(which * half_rows, half_rows), half_rows)
        for a in range(2):
            for b in range(2):
                rows = slice((a * 2 + b) * block, (a * 2 + b + 1) * block)
                to = slice((b * 2 + a) * block, (b * 2 + a + 1) * block)
                proj_ref[to, at] = src[rows, 3 * inner :].astype(F32)


def output_kernel(h1_ref, own_ref, recv_ref, bias_ref, out_ref):
    total = own_ref[...].astype(F32) + recv_ref[...].astype(F32)
    out_ref[...] = (h1_ref[...] + total + bias_ref[...]).astype(BF16)


def shape(dims, dtype):
    return jax.ShapeDtypeStruct(dims, dtype)


VMEM = functools.partial(pl.BlockSpec, memory_space=pltpu.VMEM)
SMEM = functools.partial(pl.BlockSpec, memory_space=pltpu.SMEM)


def swap(value, axis, size, bit):
    return lax.ppermute(value, axis, [(i, i ^ bit) for i in range(size)])


def add_pair(left, right):
    return left.astype(F32) + right.astype(F32)


def reduce_scatter(keep, send, bits, size):
    index = lax.axis_index("dp")
    for n, bit in enumerate(bits):
        recv = swap(send, "dp", size, bit)
        if n + 1 == len(bits):
            return add_pair(keep, recv).astype(BF16)
        rows = keep.shape[0] // 2
        upper = ((index & bits[n + 1]) != 0).astype(jnp.int32)

        def part(which):
            pick = lambda v: lax.dynamic_slice_in_dim(v, which * rows, rows, 0)
            return add_pair(pick(keep), pick(recv)).astype(BF16)

        keep, send = part(upper), part(1 - upper)


def gather_back(value, bits, size, ordered):
    index = lax.axis_index("dp")
    for bit in bits[:-1]:
        other = swap(value, "dp", size, bit)
        low, high = value, other
        if ordered:
            upper = (index & bit) != 0
            low, high = jnp.where(upper, other, value), jnp.where(upper, value, other)
        value = jnp.concatenate([low, high], axis=0)
    return value, swap(value, "dp", size, bits[-1])


def local(
    dp_size,
    inputs,
    ln1_gain,
    ln1_shift,
    w_qkv,
    qv_bias,
    bias_table,
    rel_index,
    regions,
    w_proj,
    proj_bias,
    ln2_gain,
    ln2_shift,
    w_fc1,
    fc1_bias,
    w_fc2,
    fc2_bias,
    grad_output,
):
    tokens, width = inputs.shape
    images = tokens // (SIDE * SIDE)
    inner = w_qkv.shape[2]
    heads = inner // HEAD_DIM
    lanes = heads * PAD
    wrows = WINDOWS * PAD
    srows = slab(0)[1]
    hidden = w_fc1.shape[1]
    table_rows = bias_table.shape[0]
    table_pad = -(-table_rows // 8) * 8
    row = lambda v: v.reshape(1, -1)

    def tensor_swap(value):
        return swap(value, "tensor", 2, 1)

    bits = [1 << n for n in range(dp_size.bit_length() - 1)]
    dp_index = lax.axis_index("dp").astype(jnp.int32).reshape(1)
    core_bit = dp_index & 1

    order = window_order()
    perms = []
    for image in range(images):
        offset = slab(image)[2]
        wide = ((0, 0), (offset, srows - offset - SIDE * SIDE))
        perms.append(jnp.asarray(np.pad(order, wide), BF16))
    shifted = jnp.asarray(window_order(0), BF16)
    group = jnp.asarray(np.kron(np.eye(heads, dtype=np.float32), np.ones((1, PAD), np.float32)))
    qkv_weight = w_qkv.transpose(1, 0, 2)

    masked_bias = pl.pallas_call(
        bias_kernel, out_shape=shape((wrows, lanes), F32), name="bias"
    )(bias_table.T, rel_index, row(regions), shifted)
    forward = []
    for image in range(images):
        outs = pl.pallas_call(
            functools.partial(attn_forward_kernel, image),
            out_shape=(
                shape((srows, width), BF16),
                shape((srows, width), BF16),
                shape((wrows, 3 * inner), BF16),
                shape((wrows, lanes), F32),
                shape((srows, inner), BF16),
            ),
            scratch_shapes=[pltpu.VMEM((wrows, inner), BF16)],
        )(
            inputs, row(ln1_gain), row(ln1_shift), qkv_weight, qv_bias, masked_bias, perms[image],
            w_proj,
        )
        forward.append(outs + (tensor_swap(outs[0]),))
    part0, n1a, qkvw0, prob0, otok0, recv0 = forward[0]
    part1, n1b, qkvw1, prob1, otok1, recv1 = forward[1]

    steps = hidden // HIDDEN_BLOCK
    full = lambda dims: pl.BlockSpec(dims, lambda j: (0, 0))
    cols = lambda rows: pl.BlockSpec((rows, HIDDEN_BLOCK), lambda j: (0, j))
    back_two_part, h1, n2, act, dub, grad_b1, grad_b2 = pl.pallas_call(
        mlp_kernel,
        grid=(steps,),
        in_specs=[
            full((tokens, width)), full((srows, width)), full((srows, width)),
            full((srows, width)), full((srows, width)), full((1, width)),
            full((1, width)), full((1, width)), cols(width), cols(1),
            pl.BlockSpec((HIDDEN_BLOCK, width), lambda j: (j, 0)), full((tokens, width)),
        ],
        out_specs=(
            full((tokens, width)), full((tokens, width)), full((tokens, width)), cols(tokens),
            cols(tokens), cols(1), full((1, width)),
        ),
        out_shape=(
            shape((tokens, width), BF16),
            shape((tokens, width), F32),
            shape((tokens, width), BF16),
            shape((tokens, hidden), BF16),
            shape((tokens, hidden), BF16),
            shape((1, hidden), F32),
            shape((1, width), F32),
        ),
        scratch_shapes=[pltpu.VMEM((tokens, width), F32)],
        name="mlp",
    )(
        inputs, part0, recv0, part1, recv1, row(proj_bias), row(ln2_gain), row(ln2_shift), w_fc1,
        row(fc1_bias), w_fc2, grad_output,
    )
    back_two_recv = tensor_swap(back_two_part)

    def mlp_grad(flip):
        return pl.pallas_call(
            functools.partial(mlp_grad_kernel, flip),
            in_specs=[SMEM()] + [VMEM()] * 4,
            out_shape=shape((hidden // 2, 2 * width), BF16),
        )(core_bit, act, dub, n2, grad_output)

    send = mlp_grad(1)
    keep = mlp_grad(0)
    mlp_shard = reduce_scatter(keep, send, bits, dp_size)
    mlp_part = pl.pallas_call(
        mlp_out_kernel, out_shape=shape((tokens, width), BF16), name="mlp_out"
    )(act, w_fc2)

    backward = []
    for image, (qkvw, prob) in enumerate(((qkvw0, prob0), (qkvw1, prob1))):
        outs = pl.pallas_call(
            functools.partial(attn_backward_kernel, image),
            out_shape=(
                shape((srows, width), BF16),
                shape((srows, width), F32),
                shape((srows, width), BF16),
                shape((srows, 3 * inner), BF16),
                shape((4, width), F32),
                shape((PAD, lanes), F32),
            ),
            scratch_shapes=[
                pltpu.VMEM((wrows, inner), BF16),
                pltpu.VMEM((wrows, 3 * inner), BF16),
            ],
        )(
            grad_output, back_two_part, back_two_recv, h1, row(ln2_gain), w_proj, qkvw, prob,
            perms[image], qkv_weight,
        )
        backward.append(outs + (tensor_swap(outs[0]),))
    back0, dh0, dhb0, dp0, sums0, dsum0, back_recv0 = backward[0]
    back1, dh1, dhb1, dp1, sums1, dsum1, back_recv1 = backward[1]

    def attn_grad(flip):
        return pl.pallas_call(
            functools.partial(attn_grad_kernel, flip),
            in_specs=[SMEM()] + [VMEM()] * 8,
            out_shape=shape((width // 2, 3 * inner + inner), BF16),
        )(core_bit, n1a, n1b, dp0, dp1, otok0, otok1, dhb0, dhb1)

    send = attn_grad(1)
    keep = attn_grad(0)
    attn_shard = reduce_scatter(keep, send, bits, dp_size)

    table_sum = pl.pallas_call(
        table_kernel,
        out_shape=shape((heads, table_pad), F32),
        scratch_shapes=[pltpu.VMEM((table_pad, lanes), F32), pltpu.VMEM((PAD, lanes), F32)],
        name="table",
    )(dsum0, dsum1, rel_index, group)

    mlp_recv = tensor_swap(mlp_part)
    output = pl.pallas_call(
        output_kernel, out_shape=shape((tokens, width), BF16), name="output"
    )(h1, mlp_part, mlp_recv, row(fc2_bias))

    small_rows = 7 + hidden // width + heads
    grad_input, small = pl.pallas_call(
        input_grad_kernel,
        out_shape=(shape((tokens, width), F32), shape((small_rows, width), F32)),
        name="input_grad",
    )(
        inputs, back0, back_recv0, back1, back_recv1, dh0, dh1, row(ln1_gain), sums0, sums1,
        grad_b1, grad_b2, table_sum,
    )
    for n, bit in enumerate(bits):
        recv = swap(small, "dp", dp_size, bit)
        if n + 1 < len(bits):
            small = small + recv
    smalls = pl.pallas_call(
        small_kernel,
        out_shape=tuple(shape((1, width), F32) for _ in range(5))
        + (
            shape((2, inner), F32),
            shape((1, width), F32),
            shape((1, hidden), F32),
            shape((heads, table_rows), F32),
        ),
        name="small",
    )(small, recv)
    grad_gain1, grad_shift1, grad_gain2, grad_shift2, grad_pb, grad_qvb, grad_b2, grad_b1 = smalls[:8]

    down = bits[::-1]
    mine, other = gather_back(mlp_shard, down, dp_size, False)
    grad_fc2, grad_fc1 = pl.pallas_call(
        functools.partial(mlp_finish_kernel, down[:-1]),
        in_specs=[SMEM()] + [VMEM()] * 2,
        out_shape=(shape((hidden, width), F32), shape((width, hidden), F32)),
        name="mlp_finish",
    )(dp_index, mine, other)
    mine, other = gather_back(attn_shard, down[:-3] + [down[-2], down[-3], down[-1]], dp_size, True)
    grad_qkv, grad_proj = pl.pallas_call(
        attn_finish_kernel,
        in_specs=[SMEM()] + [VMEM()] * 2,
        out_shape=(shape((3, width, inner), F32), shape((inner, width), F32)),
        name="attn_finish",
    )(core_bit, mine, other)

    flat = lambda v: v.reshape(-1)
    return (
        output, grad_input, flat(grad_gain1), flat(grad_shift1), grad_qkv.transpose(1, 0, 2),
        grad_qvb, smalls[8].T, grad_proj, flat(grad_pb), flat(grad_gain2), flat(grad_shift2),
        grad_fc1, flat(grad_b1), grad_fc2, flat(grad_b2),
    )


def solution(mesh):
    size = mesh.shape["dp"]

    def body(*args):
        return local(size, *args)

    return jax.shard_map(
        body,
        mesh=mesh,
        in_specs=(
            P("dp", None),
            P(),
            P(),
            P(None, None, "tensor"),
            P(None, "tensor"),
            P(None, "tensor"),
            P(),
            P(),
            P("tensor", None),
            P(),
            P(),
            P(),
            P(None, "tensor"),
            P("tensor"),
            P("tensor", None),
            P(),
            P("dp", None),
        ),
        out_specs=(
            P("dp", None),
            P("dp", None),
            P(),
            P(),
            P(None, None, "tensor"),
            P(None, "tensor"),
            P(None, "tensor"),
            P("tensor", None),
            P(),
            P(),
            P(),
            P(None, "tensor"),
            P("tensor"),
            P("tensor", None),
            P(),
        ),
        check_vma=False,
    )
```

time: 173 us -> 186 us (1.075)
  Pallas kernels: 54.4 us -> 68.2 us
  other arithmetic: 6.26 us -> 3.96 us
    pallas_call x5 -> x11, Pallas kernels: 33.2 us -> 46.9 us  [the longest x2 13.6 us: local(): pl.pallas_call(functools.partial(attn_backward_kernel, image), out_shape=...]
    ppermute x24 -> x26, starting transfers between devices: 27.4 us -> 29 us  [swap(): return lax.ppermute(value, axis, [(i, i ^ bit) for i in range(size)])]
    unnamed x18 -> x20, local copies, waits for them, and re-layouts: 4.28 us -> 3.99 us
    ppermute x24 -> x26, waiting for transfers between devices: 79.4 us -> 79.1 us  [swap(): return lax.ppermute(value, axis, [(i, i ^ bit) for i in range(size)])]
  transfers between devices with their start and end apart: 24 -> 26, of which waited for: 17 -> 18; matrix products, arithmetic and copies ran while one was open for 3% -> 2% of each run, Pallas kernels for 19% -> 25%
where the time goes in v3:
time: 186 us; the launch traced here: 185 us
  waiting for transfers between devices  79.1 us (43%)
  Pallas kernels  68.2 us (37%)
  starting transfers between devices  29 us (16%)
  local copies, waits for them, and re-layouts  3.99 us (2%)
  other arithmetic  3.96 us (2%)
    ppermute x26, waiting for transfers between devices, swap(): return lax.ppermute(value, axis, [(i, i ^ bit) for i in range(size)])  79.1 us
    ppermute x26, starting transfers between devices, swap(): return lax.ppermute(value, axis, [(i, i ^ bit) for i in range(size)])  29 us
    pallas_call x2, Pallas kernels, local(): pl.pallas_call(functools.partial(attn_backward_kernel, image), out_shape=...  13.6 us
    pallas_call x2, Pallas kernels, local(): pl.pallas_call(functools.partial(attn_forward_kernel, image), out_shape=(...  12.1 us
    pallas_call x2, Pallas kernels, mlp_grad(): pl.pallas_call(functools.partial(mlp_grad_kernel, flip), in_specs=[SMEM()...  6.67 us
    pallas_call x1, Pallas kernels, local(): pl.pallas_call(mlp_kernel, grid=(steps,), in_specs=[full((tokens, width))...  6.65 us
    pallas_call x2, Pallas kernels, attn_grad(): pl.pallas_call(functools.partial(attn_grad_kernel, flip), in_specs=[SMEM(...  5.47 us
    pallas_call x1, Pallas kernels, local(): pl.pallas_call(table_kernel, out_shape=shape((heads, table_pad), F32), sc...  5.09 us
  transfers between devices with their start and end apart: 26, of which 18 were waited for; matrix products, arithmetic and copies ran while one was open for 2% of the time, Pallas kernels for 25%

profile of v3, /device:TPU:0, one launch (start us, length us, event | category | flops | bytes accessed | tf_op | source)
XLA Modules:
  0.0 185.1 jit_solution(3678502445387441770)
XLA Ops:
  3.0 6.0 %shard_map.317 = (bf16[200,512]{1,0:T(8,128)(2,1)}, bf16[200,512]{1,0:T(8,128)(2,1)}, bf16[256,768]{1,0:T(8,128)(2,1)}, f32[256,512]{1,0:T(8,128)}, bf16[200,256]{1,0:T(8,128)(2,1)}) custom-call(bf16[392,512]{1,0:T(8,128)(2,1)} %x_ref.7, f32[1,512]{1,0:T(1,128)} %bitcast.27, f32[1,512]{1,0:T(1,128)} %bitcast.31, bf16[3,512,256]{2,1,0:T(8,128)(2,1)} %bitcast.20, ...), custom_call_target="tpu_custom_call" | custom-call | tf_op jit(solution)/shard_map/pallas_call | solution.py:514
  9.0 3.0 %collective-permute-start.1 = (bf16[200,512]{1,0:T(8,128)(2,1)}, bf16[200,512]{1,0:T(8,128)(2,1)S(1)}, u32[]{:S(2)}, u32[]{:S(2)}) collective-permute-start(bf16[200,512]{1,0:T(8,128)(2,1)} %get-tuple-element.60.own1_ref), channel_id=1, source_target_pairs={{0,1},{1,0},{2,3},{3,2},{4,5},{5,4},{6,7},{7,6},{8,9},{9,8},{10,11... | collective-permute-start | bytes 614408 | tf_op jit(solution)/shard_map/ppermute | solution.py:425
  12.0 6.0 %shard_map.316 = (bf16[200,512]{1,0:T(8,128)(2,1)}, bf16[200,512]{1,0:T(8,128)(2,1)}, bf16[256,768]{1,0:T(8,128)(2,1)}, f32[256,512]{1,0:T(8,128)}, bf16[200,256]{1,0:T(8,128)(2,1)}) custom-call(bf16[392,512]{1,0:T(8,128)(2,1)} %x_ref.7, f32[1,512]{1,0:T(1,128)} %bitcast.28, f32[1,512]{1,0:T(1,128)} %bitcast.32, bf16[3,512,256]{2,1,0:T(8,128)(2,1)} %bitcast.21, ...), custom_call_target="tpu_custom_call" | custom-call | tf_op jit(solution)/shard_map/pallas_call | solution.py:514
  18.1 6.7 %collective-permute-done.recv0_ref = bf16[200,512]{1,0:T(8,128)(2,1)S(1)} collective-permute-done((bf16[200,512]{1,0:T(8,128)(2,1)}, bf16[200,512]{1,0:T(8,128)(2,1)S(1)}, u32[]{:S(2)}, u32[]{:S(2)}) %collective-permute-start) | collective-permute-done | bytes 204832 | tf_op jit(solution)/shard_map/ppermute | solution.py:425
  25.5 6.7 %mlp.1 = (bf16[392,512]{1,0:T(8,128)(2,1)}, f32[392,512]{1,0:T(8,128)}, bf16[392,512]{1,0:T(8,128)(2,1)}, bf16[392,1024]{1,0:T(8,128)(2,1)}, bf16[392,1024]{1,0:...) custom-call(bf16[392,512]{1,0:T(8,128)(2,1)} %x_ref.7, bf16[200,512]{1,0:T(8,128)(2,1)} %get-tuple-element.59.own0_ref, ...), custom_call_target="tpu_custom_call" | custom-call | tf_op jit(solution)/shard_map/mlp/pallas_call | solution.py:535
  32.1 3.4 %shard_map.323 = bf16[512,1024]{1,0:T(8,128)(2,1)} custom-call(s32[1]{0:T(128)S(6)} %and.9.bit_ref, bf16[392,1024]{1,0:T(8,128)(2,1)} %get-tuple-element.62.act_ref, bf16[392,1024]{1,0:T(8,128)(2,1)} %get-tuple-element.97.dub_ref, bf16[392,512]{1,0:T(8,128)(2,1)} %get-tuple-element.98.n2_ref, bf16[392,512]{1,0:T(8,128)(2,1)} %dy_ref.9), custom_call_target="tpu_custom_call" | custom-call | tf_op jit(solution)/shard_map/pallas_call | solution.py:566
  35.8 3.3 %shard_map.322 = bf16[512,1024]{1,0:T(8,128)(2,1)} custom-call(s32[1]{0:T(128)S(6)} %and.9.bit_ref, bf16[392,1024]{1,0:T(8,128)(2,1)} %get-tuple-element.62.act_ref, bf16[392,1024]{1,0:T(8,128)(2,1)} %get-tuple-element.97.dub_ref, bf16[392,512]{1,0:T(8,128)(2,1)} %get-tuple-element.98.n2_ref, bf16[392,512]{1,0:T(8,128)(2,1)} %dy_ref.9), custom_call_target="tpu_custom_call" | custom-call | tf_op jit(solution)/shard_map/pallas_call | solution.py:566
  39.1 8.1 %collective-permute-done.3.recv_ref = bf16[392,512]{1,0:T(8,128)(2,1)S(1)} collective-permute-done((bf16[392,512]{1,0:T(8,128)(2,1)S(1)}, bf16[392,512]{1,0:T(8,128)(2,1)S(1)}, u32[]{:S(2)}, u32[]{:S(2)}) %collective-permute-start.3) | collective-permute-done | bytes 401440 | tf_op jit(solution)/shard_map/ppermute | solution.py:425
  47.9 6.8 %shard_map.319 = (bf16[200,512]{1,0:T(8,128)(2,1)}, f32[200,512]{1,0:T(8,128)}, bf16[200,512]{1,0:T(8,128)(2,1)}, bf16[200,768]{1,0:T(8,128)(2,1)}, f32[4,512]{1,0:T(4,128)}, /*index=5*/f32[64,512]{1,0:T(8,128)}) custom-call(bf16[392,512]{1,0:T(8,128)(2,1)} %dy_ref.9, bf16[392,512]{1,0:T(8,128)(2,1)} %get-tuple-element.63.own_ref, ...), custom_call_target="tpu_custom_call" | custom-call | tf_op jit(solution)/shard_map/pallas_call | solution.py:581
  54.8 6.8 %shard_map.318 = (bf16[200,512]{1,0:T(8,128)(2,1)}, f32[200,512]{1,0:T(8,128)}, bf16[200,512]{1,0:T(8,128)(2,1)}, bf16[200,768]{1,0:T(8,128)(2,1)}, f32[4,512]{1,0:T(4,128)}, /*index=5*/f32[64,512]{1,0:T(8,128)}) custom-call(bf16[392,512]{1,0:T(8,128)(2,1)} %dy_ref.9, bf16[392,512]{1,0:T(8,128)(2,1)} %get-tuple-element.63.own_ref, ...), custom_call_target="tpu_custom_call" | custom-call | tf_op jit(solution)/shard_map/pallas_call | solution.py:581
  61.6 2.8 %shard_map.321 = bf16[256,1024]{1,0:T(8,128)(2,1)} custom-call(s32[1]{0:T(128)S(6)} %and.9.bit_ref, bf16[200,512]{1,0:T(8,128)(2,1)} %get-tuple-element.82.n1a_ref, bf16[200,512]{1,0:T(8,128)(2,1)} %get-tuple-element.83.n1b_ref, bf16[200,768]{1,0:T(8,128)(2,1)} %get-tuple-element.84.dpa_ref, bf16[200,768]{1,0:T(8,128)(2,1)} %get-tuple-element.85.dpb_ref, ...), custom_call_target="tpu_custom_call" | custom-call | tf_op jit(solution)/shard_map/pallas_call | solution.py:604
  66.4 2.7 %shard_map.320 = bf16[256,1024]{1,0:T(8,128)(2,1)} custom-call(s32[1]{0:T(128)S(6)} %and.9.bit_ref, bf16[200,512]{1,0:T(8,128)(2,1)} %get-tuple-element.82.n1a_ref, bf16[200,512]{1,0:T(8,128)(2,1)} %get-tuple-element.83.n1b_ref, bf16[200,768]{1,0:T(8,128)(2,1)} %get-tuple-element.84.dpa_ref, bf16[200,768]{1,0:T(8,128)(2,1)} %get-tuple-element.85.dpb_ref, ...), custom_call_target="tpu_custom_call" | custom-call | tf_op jit(solution)/shard_map/pallas_call | solution.py:604
  71.0 8.6 %collective-permute-done.19 = bf16[256,1024]{1,0:T(8,128)(2,1)S(1)} collective-permute-done((bf16[256,1024]{1,0:T(8,128)(2,1)S(1)}, bf16[256,1024]{1,0:T(8,128)(2,1)S(1)}, u32[]{:S(2)}, u32[]{:S(2)}) %collective-permute-start.19) | collective-permute-done | bytes 524320 | tf_op jit(solution)/shard_map/ppermute | solution.py:425
  81.5 3.3 %collective-permute-done.11 = bf16[128,1024]{1,0:T(8,128)(2,1)S(1)} collective-permute-done((bf16[128,1024]{1,0:T(8,128)(2,1)S(1)}, bf16[128,1024]{1,0:T(8,128)(2,1)S(1)}, u32[]{:S(2)}, u32[]{:S(2)}) %collective-permute-start.11) | collective-permute-done | bytes 262176 | tf_op jit(solution)/shard_map/ppermute | solution.py:425
  87.4 2.7 %collective-permute-start.21 = (bf16[64,1024]{1,0:T(8,128)(2,1)S(1)}, bf16[64,1024]{1,0:T(8,128)(2,1)S(1)}, u32[]{:S(2)}, u32[]{:S(2)}) collective-permute-start(bf16[64,1024]{1,0:T(8,128)(2,1)S(1)} %add_convert_fusion.7), channel_id=1, source_target_pairs={{0,16},{2,18},{4,20},{6,22},{8,24},{10,26},{12,28},{14,30},{16,0},... | collective-permute-start | bytes 393224 | tf_op jit(solution)/shard_map/ppermute | solution.py:425
  91.5 2.5 %collective-permute-start.13 = (bf16[32,1024]{1,0:T(8,128)(2,1)S(1)}, bf16[32,1024]{1,0:T(8,128)(2,1)S(1)}, u32[]{:S(2)}, u32[]{:S(2)}) collective-permute-start(bf16[32,1024]{1,0:T(8,128)(2,1)S(1)} %add_convert_fusion.12), channel_id=1, source_target_pairs={{0,16},{2,18},{4,20},{6,22},{8,24},{10,26},{12,28},{14,30},{16,0},... | collective-permute-start | bytes 196616 | tf_op jit(solution)/shard_map/ppermute | solution.py:425
  94.0 4.2 %collective-permute-done.21 = bf16[64,1024]{1,0:T(8,128)(2,1)S(1)} collective-permute-done((bf16[64,1024]{1,0:T(8,128)(2,1)S(1)}, bf16[64,1024]{1,0:T(8,128)(2,1)S(1)}, u32[]{:S(2)}, u32[]{:S(2)}) %collective-permute-start.21) | collective-permute-done | bytes 131104 | tf_op jit(solution)/shard_map/ppermute | solution.py:425
  98.3 2.7 %collective-permute-done.13 = bf16[32,1024]{1,0:T(8,128)(2,1)S(1)} collective-permute-done((bf16[32,1024]{1,0:T(8,128)(2,1)S(1)}, bf16[32,1024]{1,0:T(8,128)(2,1)S(1)}, u32[]{:S(2)}, u32[]{:S(2)}) %collective-permute-start.13) | collective-permute-done | bytes 65568 | tf_op jit(solution)/shard_map/ppermute | solution.py:425
  101.3 3.1 %collective-permute-done.22 = bf16[64,1024]{1,0:T(8,128)(2,1)S(1)} collective-permute-done((bf16[64,1024]{1,0:T(8,128)(2,1)S(1)}, bf16[64,1024]{1,0:T(8,128)(2,1)S(1)}, u32[]{:S(2)}, u32[]{:S(2)}) %collective-permute-start.22) | collective-permute-done | bytes 131104 | tf_op jit(solution)/shard_map/ppermute | solution.py:425
  106.9 4.2 %collective-permute-done.23 = bf16[128,1024]{1,0:T(8,128)(2,1)S(1)} collective-permute-done((bf16[128,1024]{1,0:T(8,128)(2,1)S(1)}, bf16[128,1024]{1,0:T(8,128)(2,1)S(1)}, u32[]{:S(2)}, u32[]{:S(2)}) %collective-permute-start.23) | collective-permute-done | bytes 262176 | tf_op jit(solution)/shard_map/ppermute | solution.py:425
  113.4 11.1 %collective-permute-done.15 = bf16[64,1024]{1,0:T(8,128)(2,1)S(1)} collective-permute-done((bf16[64,1024]{1,0:T(8,128)(2,1)S(1)}, bf16[64,1024]{1,0:T(8,128)(2,1)S(1)}, u32[]{:S(2)}, u32[]{:S(2)}) %collective-permute-start.15) | collective-permute-done | bytes 131104 | tf_op jit(solution)/shard_map/ppermute | solution.py:425
  126.1 4.9 %collective-permute-done.16 = bf16[128,1024]{1,0:T(8,128)(2,1)S(1)} collective-permute-done((bf16[128,1024]{1,0:T(8,128)(2,1)S(1)}, bf16[128,1024]{1,0:T(8,128)(2,1)S(1)}, u32[]{:S(2)}, u32[]{:S(2)}) %collective-permute-start.16) | collective-permute-done | bytes 262176 | tf_op jit(solution)/shard_map/ppermute | solution.py:425
  131.2 2.9 %mlp_out.1.own_ref = bf16[392,512]{1,0:T(8,128)(2,1)} custom-call(bf16[392,1024]{1,0:T(8,128)(2,1)} %get-tuple-element.62.act_ref, bf16[1024,512]{1,0:T(8,128)(2,1)} %w2_ref.3), custom_call_target="tpu_custom_call" | custom-call | tf_op jit(solution)/shard_map/mlp_out/pallas_call | solution.py:575
  136.7 5.1 %table.1.tab_ref = f32[8,176]{1,0:T(8,128)} custom-call(f32[64,512]{1,0:T(8,128)} %get-tuple-element.76.dsa_ref, f32[64,512]{1,0:T(8,128)} %get-tuple-element.77.dsb_ref, s32[49,49]{1,0:T(8,128)} %rel_ref.3, f32[8,512]{1,0:T(8,128)} %constant.51.clone.group_ref), custom_call_target="tpu_custom_call" | custom-call | tf_op jit(solution)/shard_map/table/pallas_call | solution.py:614
  141.8 9.2 %collective-permute-done.5.recv1_ref = bf16[200,512]{1,0:T(8,128)(2,1)} collective-permute-done((bf16[200,512]{1,0:T(8,128)(2,1)}, bf16[200,512]{1,0:T(8,128)(2,1)}, u32[]{:S(2)}, u32[]{:S(2)}) %collective-permute-start.5) | collective-permute-done | bytes 204832 | tf_op jit(solution)/shard_map/ppermute | solution.py:425
  151.0 3.8 %collective-permute-done.4.recv0_ref = bf16[200,512]{1,0:T(8,128)(2,1)} collective-permute-done((bf16[200,512]{1,0:T(8,128)(2,1)}, bf16[200,512]{1,0:T(8,128)(2,1)}, u32[]{:S(2)}, u32[]{:S(2)}) %collective-permute-start.4) | collective-permute-done | bytes 204832 | tf_op jit(solution)/shard_map/ppermute | solution.py:425
  154.8 3.2 %input_grad.1 = (f32[392,512]{1,0:T(8,128)}, f32[17,512]{1,0:T(8,128)}) custom-call(bf16[392,512]{1,0:T(8,128)(2,1)} %x_ref.7, bf16[200,512]{1,0:T(8,128)(2,1)} %get-tuple-element.66.own0_ref, bf16[200,512]{1,0:T(8,128)(2,1)} %collective-permute-done.4.recv0_ref, bf16[200,512]{1,0:T(8,128)(2,1)} %get-tuple-element.69.own1_ref, ...), custom_call_target="tpu_custom_call" | custom-call | tf_op jit(solution)/shard_map/input_grad/pallas_call | solution.py:627
  161.8 2.6 %collective-permute-done.7 = f32[17,512]{1,0:T(8,128)S(1)} collective-permute-done((f32[17,512]{1,0:T(8,128)S(1)}, f32[17,512]{1,0:T(8,128)S(1)}, u32[]{:S(2)}, u32[]{:S(2)}) %collective-permute-start.7) | collective-permute-done | bytes 34848 | tf_op jit(solution)/shard_map/ppermute | solution.py:425
  165.8 2.8 %collective-permute-done.8 = f32[17,512]{1,0:T(8,128)S(1)} collective-permute-done((f32[17,512]{1,0:T(8,128)S(1)}, f32[17,512]{1,0:T(8,128)S(1)}, u32[]{:S(2)}, u32[]{:S(2)}) %collective-permute-start.8) | collective-permute-done | bytes 34848 | tf_op jit(solution)/shard_map/ppermute | solution.py:425
  169.2 3.2 %collective-permute-start.9 = (f32[17,512]{1,0:T(8,128)}, f32[17,512]{1,0:T(8,128)}, u32[]{:S(2)}, u32[]{:S(2)}) collective-permute-start(f32[17,512]{1,0:T(8,128)} %add.89.left_ref), channel_id=1, source_target_pairs={{0,16},{2,18},{4,20},{6,22},{8,24},{10,26},{12,28},{14,30},{16,0},... | collective-permute-start | bytes 104456 | tf_op jit(solution)/shard_map/ppermute | solution.py:425
  177.7 2.6 %attn_finish.1 = (f32[3,512,256]{2,1,0:T(8,128)}, f32[256,512]{1,0:T(8,128)}) custom-call(s32[1]{0:T(128)S(6)} %and.9.bit_ref, bf16[256,1024]{1,0:T(8,128)(2,1)} %copy-done.2, bf16[256,1024]{1,0:T(8,128)(2,1)} %copy-done.6), custom_call_target="tpu_custom_call" | custom-call | tf_op jit(solution)/shard_map/attn_finish/pallas_call | solution.py:661
  181.3 3.8 %mlp_finish.1 = (f32[1024,512]{1,0:T(8,128)}, f32[512,1024]{1,0:T(8,128)}) custom-call(s32[1]{0:T(128)} %bitcast.12.index_ref, bf16[512,1024]{1,0:T(8,128)(2,1)} %copy-done, bf16[512,1024]{1,0:T(8,128)(2,1)} %copy-done.5), custom_call_target="tpu_custom_call" | custom-call | tf_op jit(solution)/shard_map/mlp_finish/pallas_call | solution.py:654
  (77 shorter events, 35.5 us)
Async XLA Ops:
  9.0 9.1 %collective-permute-start.1 = (bf16[200,512]{1,0:T(8,128)(2,1)}, bf16[200,512]{1,0:T(8,128)(2,1)S(1)}, u32[]{:S(2)}, u32[]{:S(2)}) collective-permute-start(bf16[200,512]{1,0:T(8,128)(2,1)} %get-tuple-element.60.own1_ref), channel_id=1, source_target_pairs={{0,1},{1,0},{2,3},{3,2},{4,5},{5,4},{6,7},{7,6},{8,9},{9,8},{10,11... | collective-permute-start | bytes 614408 | tf_op jit(solution)/shard_map/ppermute | solution.py:425
  18.0 6.7 %collective-permute-start = (bf16[200,512]{1,0:T(8,128)(2,1)}, bf16[200,512]{1,0:T(8,128)(2,1)S(1)}, u32[]{:S(2)}, u32[]{:S(2)}) collective-permute-start(bf16[200,512]{1,0:T(8,128)(2,1)} %get-tuple-element.59.own0_ref), channel_id=1, source_target_pairs={{0,1},{1,0},{2,3},{3,2},{4,5},{5,4},{6,7},{7,6},{8,9},{9,8},{10,11... | collective-permute-start | bytes 614408 | tf_op jit(solution)/shard_map/ppermute | solution.py:425
  18.1 6.7 %copy-start.8 = (bf16[200,512]{1,0:T(8,128)(2,1)}, bf16[200,512]{1,0:T(8,128)(2,1)S(1)}, u32[]{:S(2)}) copy-start(bf16[200,512]{1,0:T(8,128)(2,1)S(1)} %collective-permute-done.1.recv1_ref) | copy-start | bytes 614404
  32.1 3.4 %copy-start.3 = (bf16[392,512]{1,0:T(8,128)(2,1)S(1)}, bf16[392,512]{1,0:T(8,128)(2,1)}, u32[]{:S(2)}) copy-start(bf16[392,512]{1,0:T(8,128)(2,1)} %get-tuple-element.63.own_ref) | copy-start | bytes 1204228
  35.5 28.9 %collective-permute-start.18 = (bf16[512,1024]{1,0:T(8,128)(2,1)}, bf16[512,1024]{1,0:T(8,128)(2,1)S(1)}, u32[]{:S(2)}, u32[]{:S(2)}) collective-permute-start(bf16[512,1024]{1,0:T(8,128)(2,1)} %shard_map.323), channel_id=1, source_target_pairs={{0,2},{2,0},{4,6},{6,4},{8,10},{10,8},{12,14},{14,12},{16,18},{18,... | collective-permute-start | bytes 3145736 | tf_op jit(solution)/shard_map/ppermute | solution.py:425
  35.5 11.7 %collective-permute-start.3 = (bf16[392,512]{1,0:T(8,128)(2,1)S(1)}, bf16[392,512]{1,0:T(8,128)(2,1)S(1)}, u32[]{:S(2)}, u32[]{:S(2)}) collective-permute-start(bf16[392,512]{1,0:T(8,128)(2,1)S(1)} %copy-done.3), channel_id=1, source_target_pairs={{0,1},{1,0},{2,3},{3,2},{4,5},{5,4},{6,7},{7,6},{8,9},{9,8},{10,11... | collective-permute-start | bytes 1204232 | tf_op jit(solution)/shard_map/ppermute | solution.py:425
  61.6 2.8 %copy-start.1 = (bf16[512,1024]{1,0:T(8,128)(2,1)S(1)}, bf16[512,1024]{1,0:T(8,128)(2,1)}, u32[]{:S(2)}) copy-start(bf16[512,1024]{1,0:T(8,128)(2,1)} %shard_map.322) | copy-start | bytes 3145732
  64.3 4.7 %collective-permute-start.10 = (bf16[256,1024]{1,0:T(8,128)(2,1)}, bf16[256,1024]{1,0:T(8,128)(2,1)}, u32[]{:S(2)}, u32[]{:S(2)}) collective-permute-start(bf16[256,1024]{1,0:T(8,128)(2,1)} %shard_map.321), channel_id=1, source_target_pairs={{0,2},{2,0},{4,6},{6,4},{8,10},{10,8},{12,14},{14,12},{16,18},{18,... | collective-permute-start | bytes 1572872 | tf_op jit(solution)/shard_map/ppermute | solution.py:425
  64.8 14.9 %collective-permute-start.19 = (bf16[256,1024]{1,0:T(8,128)(2,1)S(1)}, bf16[256,1024]{1,0:T(8,128)(2,1)S(1)}, u32[]{:S(2)}, u32[]{:S(2)}) collective-permute-start(bf16[256,1024]{1,0:T(8,128)(2,1)S(1)} %get-tuple-element.104), channel_id=1, source_target_pairs={{0,4},{2,6},{4,0},{6,2},{8,12},{10,14},{12,8},{14,10},{16,20},{18,... | collective-permute-start | bytes 1572872 | tf_op jit(solution)/shard_map/ppermute | solution.py:425
  70.4 14.3 %collective-permute-start.11 = (bf16[128,1024]{1,0:T(8,128)(2,1)S(1)}, bf16[128,1024]{1,0:T(8,128)(2,1)S(1)}, u32[]{:S(2)}, u32[]{:S(2)}) collective-permute-start(bf16[128,1024]{1,0:T(8,128)(2,1)S(1)} %get-tuple-element.108), channel_id=1, source_target_pairs={{0,4},{2,6},{4,0},{6,2},{8,12},{10,14},{12,8},{14,10},{16,20},{18,... | collective-permute-start | bytes 786440 | tf_op jit(solution)/shard_map/ppermute | solution.py:425
  79.9 7.5 %collective-permute-start.20 = (bf16[128,1024]{1,0:T(8,128)(2,1)S(1)}, bf16[128,1024]{1,0:T(8,128)(2,1)S(1)}, u32[]{:S(2)}, u32[]{:S(2)}) collective-permute-start(bf16[128,1024]{1,0:T(8,128)(2,1)S(1)} %get-tuple-element.106), channel_id=1, source_target_pairs={{0,8},{2,10},{4,12},{6,14},{8,0},{10,2},{12,4},{14,6},{16,24},{18,... | collective-permute-start | bytes 786440 | tf_op jit(solution)/shard_map/ppermute | solution.py:425
  84.9 6.6 %collective-permute-start.12 = (bf16[64,1024]{1,0:T(8,128)(2,1)S(1)}, bf16[64,1024]{1,0:T(8,128)(2,1)S(1)}, u32[]{:S(2)}, u32[]{:S(2)}) collective-permute-start(bf16[64,1024]{1,0:T(8,128)(2,1)S(1)} %get-tuple-element.112), channel_id=1, source_target_pairs={{0,8},{2,10},{4,12},{6,14},{8,0},{10,2},{12,4},{14,6},{16,24},{18,... | collective-permute-start | bytes 393224 | tf_op jit(solution)/shard_map/ppermute | solution.py:425
  87.4 10.7 %collective-permute-start.21 = (bf16[64,1024]{1,0:T(8,128)(2,1)S(1)}, bf16[64,1024]{1,0:T(8,128)(2,1)S(1)}, u32[]{:S(2)}, u32[]{:S(2)}) collective-permute-start(bf16[64,1024]{1,0:T(8,128)(2,1)S(1)} %add_convert_fusion.7), channel_id=1, source_target_pairs={{0,16},{2,18},{4,20},{6,22},{8,24},{10,26},{12,28},{14,30},{16,0},... | collective-permute-start | bytes 393224 | tf_op jit(solution)/shard_map/ppermute | solution.py:425
  91.5 9.4 %collective-permute-start.13 = (bf16[32,1024]{1,0:T(8,128)(2,1)S(1)}, bf16[32,1024]{1,0:T(8,128)(2,1)S(1)}, u32[]{:S(2)}, u32[]{:S(2)}) collective-permute-start(bf16[32,1024]{1,0:T(8,128)(2,1)S(1)} %add_convert_fusion.12), channel_id=1, source_target_pairs={{0,16},{2,18},{4,20},{6,22},{8,24},{10,26},{12,28},{14,30},{16,0},... | collective-permute-start | bytes 196616 | tf_op jit(solution)/shard_map/ppermute | solution.py:425
  98.2 6.2 %collective-permute-start.22 = (bf16[64,1024]{1,0:T(8,128)(2,1)S(1)}, bf16[64,1024]{1,0:T(8,128)(2,1)S(1)}, u32[]{:S(2)}, u32[]{:S(2)}) collective-permute-start(bf16[64,1024]{1,0:T(8,128)(2,1)S(1)} %add_convert_fusion.6), channel_id=1, source_target_pairs={{0,16},{2,18},{4,20},{6,22},{8,24},{10,26},{12,28},{14,30},{16,0},... | collective-permute-start | bytes 393224 | tf_op jit(solution)/shard_map/ppermute | solution.py:425
  101.0 5.9 %collective-permute-start.14 = (bf16[32,1024]{1,0:T(8,128)(2,1)S(1)}, bf16[32,1024]{1,0:T(8,128)(2,1)S(1)}, u32[]{:S(2)}, u32[]{:S(2)}) collective-permute-start(bf16[32,1024]{1,0:T(8,128)(2,1)S(1)} %add_convert_fusion.11), channel_id=1, source_target_pairs={{0,16},{2,18},{4,20},{6,22},{8,24},{10,26},{12,28},{14,30},{16,0},... | collective-permute-start | bytes 196616 | tf_op jit(solution)/shard_map/ppermute | solution.py:425
  104.4 6.8 %collective-permute-start.23 = (bf16[128,1024]{1,0:T(8,128)(2,1)S(1)}, bf16[128,1024]{1,0:T(8,128)(2,1)S(1)}, u32[]{:S(2)}, u32[]{:S(2)}) collective-permute-start(bf16[128,1024]{1,0:T(8,128)(2,1)S(1)} %pad_maximum_fusion.4), channel_id=1, source_target_pairs={{0,8},{2,10},{4,12},{6,14},{8,0},{10,2},{12,4},{14,6},{16,24},{18,... | collective-permute-start | bytes 786440 | tf_op jit(solution)/shard_map/ppermute | solution.py:425
  111.2 14.7 %collective-permute-start.24 = (bf16[256,1024]{1,0:T(8,128)(2,1)S(1)}, bf16[256,1024]{1,0:T(8,128)(2,1)S(1)}, u32[]{:S(2)}, u32[]{:S(2)}) collective-permute-start(bf16[256,1024]{1,0:T(8,128)(2,1)S(1)} %pad_maximum_fusion.2), channel_id=1, source_target_pairs={{0,4},{2,6},{4,0},{6,2},{8,12},{10,14},{12,8},{14,10},{16,20},{18,... | collective-permute-start | bytes 1572872 | tf_op jit(solution)/shard_map/ppermute | solution.py:425
  112.8 11.7 %collective-permute-start.15 = (bf16[64,1024]{1,0:T(8,128)(2,1)S(1)}, bf16[64,1024]{1,0:T(8,128)(2,1)S(1)}, u32[]{:S(2)}, u32[]{:S(2)}) collective-permute-start(bf16[64,1024]{1,0:T(8,128)(2,1)S(1)} %pad_maximum_fusion.5), channel_id=1, source_target_pairs={{0,4},{2,6},{4,0},{6,2},{8,12},{10,14},{12,8},{14,10},{16,20},{18,... | collective-permute-start | bytes 393224 | tf_op jit(solution)/shard_map/ppermute | solution.py:425
  124.5 6.4 %collective-permute-start.16 = (bf16[128,1024]{1,0:T(8,128)(2,1)S(1)}, bf16[128,1024]{1,0:T(8,128)(2,1)S(1)}, u32[]{:S(2)}, u32[]{:S(2)}) collective-permute-start(bf16[128,1024]{1,0:T(8,128)(2,1)S(1)} %pad_maximum_fusion.3), channel_id=1, source_target_pairs={{0,8},{2,10},{4,12},{6,14},{8,0},{10,2},{12,4},{14,6},{16,24},{18,... | collective-permute-start | bytes 786440 | tf_op jit(solution)/shard_map/ppermute | solution.py:425
  126.0 8.2 %copy-start = (bf16[512,1024]{1,0:T(8,128)(2,1)}, bf16[512,1024]{1,0:T(8,128)(2,1)S(1)}, u32[]{:S(2)}) copy-start(bf16[512,1024]{1,0:T(8,128)(2,1)S(1)} %pad_maximum_fusion.mine_ref) | copy-start | bytes 3145732
  126.0 54.3 %collective-permute-start.25 = (bf16[512,1024]{1,0:T(8,128)(2,1)S(1)}, bf16[512,1024]{1,0:T(8,128)(2,1)S(1)}, u32[]{:S(2)}, u32[]{:S(2)}) collective-permute-start(bf16[512,1024]{1,0:T(8,128)(2,1)S(1)} %pad_maximum_fusion.mine_ref), channel_id=1, source_target_pairs={{0,2},{2,0},{4,6},{6,4},{8,10},{10,8},{12,14},{14,12},{16,18},{18,... | collective-permute-start | bytes 3145736 | tf_op jit(solution)/shard_map/ppermute | solution.py:425
  131.1 26.9 %copy-start.2 = (bf16[256,1024]{1,0:T(8,128)(2,1)}, bf16[256,1024]{1,0:T(8,128)(2,1)S(1)}, u32[]{:S(2)}) copy-start(bf16[256,1024]{1,0:T(8,128)(2,1)S(1)} %pad_maximum_fusion.1.mine_ref) | copy-start | bytes 1572868
  131.1 45.7 %collective-permute-start.17 = (bf16[256,1024]{1,0:T(8,128)(2,1)S(1)}, bf16[256,1024]{1,0:T(8,128)(2,1)S(1)}, u32[]{:S(2)}, u32[]{:S(2)}) collective-permute-start(bf16[256,1024]{1,0:T(8,128)(2,1)S(1)} %pad_maximum_fusion.1.mine_ref), channel_id=1, source_target_pairs={{0,2},{2,0},{4,6},{6,4},{8,10},{10,8},{12,14},{14,12},{16,18},{18,... | collective-permute-start | bytes 1572872 | tf_op jit(solution)/shard_map/ppermute | solution.py:425
  134.1 38.3 %collective-permute-start.2 = (bf16[392,512]{1,0:T(8,128)(2,1)}, bf16[392,512]{1,0:T(8,128)(2,1)S(1)}, u32[]{:S(2)}, u32[]{:S(2)}) collective-permute-start(bf16[392,512]{1,0:T(8,128)(2,1)} %mlp_out.1.own_ref), channel_id=1, source_target_pairs={{0,1},{1,0},{2,3},{3,2},{4,5},{5,4},{6,7},{7,6},{8,9},{9,8},{10,11... | collective-permute-start | bytes 1204232 | tf_op jit(solution)/shard_map/ppermute | solution.py:425
  134.7 16.3 %collective-permute-start.5 = (bf16[200,512]{1,0:T(8,128)(2,1)}, bf16[200,512]{1,0:T(8,128)(2,1)}, u32[]{:S(2)}, u32[]{:S(2)}) collective-permute-start(bf16[200,512]{1,0:T(8,128)(2,1)} %get-tuple-element.69.own1_ref), channel_id=1, source_target_pairs={{0,1},{1,0},{2,3},{3,2},{4,5},{5,4},{6,7},{7,6},{8,9},{9,8},{10,11... | collective-permute-start | bytes 614408 | tf_op jit(solution)/shard_map/ppermute | solution.py:425
  136.2 18.6 %collective-permute-start.4 = (bf16[200,512]{1,0:T(8,128)(2,1)}, bf16[200,512]{1,0:T(8,128)(2,1)}, u32[]{:S(2)}, u32[]{:S(2)}) collective-permute-start(bf16[200,512]{1,0:T(8,128)(2,1)} %get-tuple-element.66.own0_ref), channel_id=1, source_target_pairs={{0,1},{1,0},{2,3},{3,2},{4,5},{5,4},{6,7},{7,6},{8,9},{9,8},{10,11... | collective-permute-start | bytes 614408 | tf_op jit(solution)/shard_map/ppermute | solution.py:425
  158.0 1.5 collective-permute-start.6
  160.3 4.1 %collective-permute-start.7 = (f32[17,512]{1,0:T(8,128)S(1)}, f32[17,512]{1,0:T(8,128)S(1)}, u32[]{:S(2)}, u32[]{:S(2)}) collective-permute-start(f32[17,512]{1,0:T(8,128)S(1)} %add.87), channel_id=1, source_target_pairs={{0,4},{2,6},{4,0},{6,2},{8,12},{10,14},{12,8},{14,10},{16,20},{18,... | collective-permute-start | bytes 104456 | tf_op jit(solution)/shard_map/ppermute | solution.py:425
  164.4 4.2 %collective-permute-start.8 = (f32[17,512]{1,0:T(8,128)S(1)}, f32[17,512]{1,0:T(8,128)S(1)}, u32[]{:S(2)}, u32[]{:S(2)}) collective-permute-start(f32[17,512]{1,0:T(8,128)S(1)} %add.88), channel_id=1, source_target_pairs={{0,8},{2,10},{4,12},{6,14},{8,0},{10,2},{12,4},{14,6},{16,24},{18,... | collective-permute-start | bytes 104456 | tf_op jit(solution)/shard_map/ppermute | solution.py:425
  169.2 6.2 %collective-permute-start.9 = (f32[17,512]{1,0:T(8,128)}, f32[17,512]{1,0:T(8,128)}, u32[]{:S(2)}, u32[]{:S(2)}) collective-permute-start(f32[17,512]{1,0:T(8,128)} %add.89.left_ref), channel_id=1, source_target_pairs={{0,16},{2,18},{4,20},{6,22},{8,24},{10,26},{12,28},{14,30},{16,0},... | collective-permute-start | bytes 104456 | tf_op jit(solution)/shard_map/ppermute | solution.py:425
  180.3 1.0 copy-start.5
  (4 other events, 3.0 us)

commit v4 on v3

--- a/solution.py
+++ b/solution.py
@@ -98,7 +98,7 @@
     return jnp.concatenate([spread, zero], axis=0).astype(jnp.int32)
 
 
-def bias_kernel(table_ref, rel_ref, reg_ref, order_ref, bm_ref):
+def bias_kernel(index_ref, table_ref, rel_ref, reg_ref, order_ref, bm_ref):
     heads, entries = table_ref.shape
     index = pair_index(rel_ref) - 1
     first = jnp.clip(index, 0, 127)
@@ -211,8 +211,8 @@
     return ref[:, pl.ds(pl.multiple_of(which * size, size), size)]
 
 
-def mlp_grad_kernel(flip, bit_ref, act_ref, dub_ref, n2_ref, dy_ref, out_ref):
-    which = bit_ref[0] if flip == 0 else 1 - bit_ref[0]
+def mlp_grad_kernel(flip, index_ref, act_ref, dub_ref, n2_ref, dy_ref, out_ref):
+    which = (index_ref[0] & 1) ^ flip
     size = act_ref.shape[1] // 2
     width = dy_ref.shape[1]
     out_ref[:, :width] = dot(half(act_ref, which, size), dy_ref[...], TN).astype(BF16)
@@ -283,9 +283,9 @@
 
 
 def attn_grad_kernel(
-    flip, bit_ref, n1a_ref, n1b_ref, dpa_ref, dpb_ref, oa_ref, ob_ref, dha_ref, dhb_ref, out_ref
+    flip, index_ref, n1a_ref, n1b_ref, dpa_ref, dpb_ref, oa_ref, ob_ref, dha_ref, dhb_ref, out_ref
 ):
-    which = bit_ref[0] if flip == 0 else 1 - bit_ref[0]
+    which = (index_ref[0] & 1) ^ flip
     wide = dpa_ref.shape[1]
     rows = n1a_ref.shape[1] // 2
     qkv = dot(half(n1a_ref, which, rows), dpa_ref[...], TN)
@@ -369,30 +369,38 @@
     tab_ref[...] = small[at : at + tab_ref.shape[0], : tab_ref.shape[1]]
 
 
-def mlp_finish_kernel(bits, index_ref, mine_ref, other_ref, fc2_ref, fc1_ref):
-    index = index_ref[0]
-    total, width = mine_ref.shape[0], fc2_ref.shape[1]
-    rows = total >> len(bits)
-    for n in range(1 << len(bits)):
-        to = 0
-        for place, bit in enumerate(bits):
-            away = (n >> place) & 1
-            set_here = lax.shift_right_logical(index, bit.bit_length() - 1) & 1
-            to = to + ((1 - set_here) if away else set_here) * (rows << place)
-        for src, away in ((mine_ref, 0), (other_ref, 1)):
-            which = (index & 1) if away == 0 else 1 - (index & 1)
-            block = src[n * rows : (n + 1) * rows, :]
-            at = pl.multiple_of(which * total + to, 8)
-            fc2_ref[pl.ds(at, rows), :] = block[:, :width].astype(F32)
-            cols = pl.ds(pl.multiple_of(which * total, 128), total)
-            fc1_ref[pl.ds(pl.multiple_of(to, 8), rows), cols] = block[:, width:].astype(F32)
-
-
-def attn_finish_kernel(bit_ref, mine_ref, other_ref, qkv_ref, proj_ref):
+def mlp_finish_kernel(index_ref, mine_ref, other_ref, fc2_ref, fc1_ref):
+    rows, width = mine_ref.shape[0], fc2_ref.shape[1]
+    for src, which in ((mine_ref, index_ref[0] & 1), (other_ref, 1 - (index_ref[0] & 1))):
+        at = pl.ds(pl.multiple_of(which * rows, rows), rows)
+        fc2_ref[at, :] = src[:, :width].astype(F32)
+        fc1_ref[:, at] = src[:, width:].astype(F32)
+
+
+def split_kernel(place, index_ref, keep_ref, recv_ref, kept_ref, send_ref):
+    rows = kept_ref.shape[0]
+    upper = lax.shift_right_logical(index_ref[0], place) & 1
+    for out, which in ((send_ref, 1 - upper), (kept_ref, upper)):
+        at = pl.ds(pl.multiple_of(which * rows, rows), rows)
+        out[...] = add_pair(keep_ref[at, :], recv_ref[at, :]).astype(BF16)
+
+
+def sum_kernel(left_ref, right_ref, out_ref):
+    out_ref[...] = add_pair(left_ref[...], right_ref[...]).astype(out_ref.dtype)
+
+
+def join_kernel(place, index_ref, mine_ref, other_ref, out_ref):
+    rows = mine_ref.shape[0]
+    upper = lax.shift_right_logical(index_ref[0], place) & 1
+    out_ref[pl.ds(pl.multiple_of(upper * rows, rows), rows), :] = mine_ref[...]
+    out_ref[pl.ds(pl.multiple_of((1 - upper) * rows, rows), rows), :] = other_ref[...]
+
+
+def attn_finish_kernel(index_ref, mine_ref, other_ref, qkv_ref, proj_ref):
     inner = qkv_ref.shape[2]
     half_rows = qkv_ref.shape[1] // 2
     block = half_rows // 4
-    for src, which in ((mine_ref, bit_ref[0]), (other_ref, 1 - bit_ref[0])):
+    for src, which in ((mine_ref, index_ref[0] & 1), (other_ref, 1 - (index_ref[0] & 1))):
         for n in range(3):
             for a in range(2):
                 for b in range(2):
@@ -419,6 +427,20 @@
 
 VMEM = functools.partial(pl.BlockSpec, memory_space=pltpu.VMEM)
 SMEM = functools.partial(pl.BlockSpec, memory_space=pltpu.SMEM)
+PARAMS = pltpu.CompilerParams(vmem_limit_bytes=12 << 20)
+
+
+def call(kernel, out_shape, scratch=(), smem=0):
+    def run(*args):
+        return pl.pallas_call(
+            kernel,
+            in_specs=[SMEM()] * smem + [VMEM()] * (len(args) - smem),
+            out_shape=out_shape,
+            scratch_shapes=list(scratch),
+            compiler_params=PARAMS,
+        )(*args)
+
+    return run
 
 
 def swap(value, axis, size, bit):
@@ -429,31 +451,40 @@
     return left.astype(F32) + right.astype(F32)
 
 
-def reduce_scatter(keep, send, bits, size):
-    index = lax.axis_index("dp")
+def reduce_scatter(keep, send, bits, size, index):
     for n, bit in enumerate(bits):
         recv = swap(send, "dp", size, bit)
         if n + 1 == len(bits):
-            return add_pair(keep, recv).astype(BF16)
+            return call(sum_kernel, shape(keep.shape, BF16))(keep, recv)
         rows = keep.shape[0] // 2
-        upper = ((index & bits[n + 1]) != 0).astype(jnp.int32)
-
-        def part(which):
-            pick = lambda v: lax.dynamic_slice_in_dim(v, which * rows, rows, 0)
-            return add_pair(pick(keep), pick(recv)).astype(BF16)
-
-        keep, send = part(upper), part(1 - upper)
-
-
-def gather_back(value, bits, size, ordered):
-    index = lax.axis_index("dp")
+        place = bits[n + 1].bit_length() - 1
+        half_shape = shape((rows, keep.shape[1]), BF16)
+        if rows % 16 == 0:
+            keep, send = call(
+                functools.partial(split_kernel, place),
+                (half_shape, half_shape), smem=1,
+            )(index, keep, recv)
+        else:
+            upper = ((index[0] >> place) & 1) != 0
+            total = add_pair(keep, recv).astype(BF16)
+            low, high = total[:rows], total[rows:]
+            keep, send = jnp.where(upper, high, low), jnp.where(upper, low, high)
+
+
+def gather_back(value, bits, size, index):
     for bit in bits[:-1]:
         other = swap(value, "dp", size, bit)
-        low, high = value, other
-        if ordered:
-            upper = (index & bit) != 0
+        rows = value.shape[0]
+        place = bit.bit_length() - 1
+        if rows % 16 == 0:
+            value = call(
+                functools.partial(join_kernel, place),
+                shape((2 * rows, value.shape[1]), BF16), smem=1,
+            )(index, value, other)
+        else:
+            upper = ((index[0] >> place) & 1) != 0
             low, high = jnp.where(upper, other, value), jnp.where(upper, value, other)
-        value = jnp.concatenate([low, high], axis=0)
+            value = jnp.concatenate([low, high], axis=0)
     return value, swap(value, "dp", size, bits[-1])
 
 
@@ -494,7 +525,6 @@
 
     bits = [1 << n for n in range(dp_size.bit_length() - 1)]
     dp_index = lax.axis_index("dp").astype(jnp.int32).reshape(1)
-    core_bit = dp_index & 1
 
     order = window_order()
     perms = []
@@ -506,9 +536,9 @@
     group = jnp.asarray(np.kron(np.eye(heads, dtype=np.float32), np.ones((1, PAD), np.float32)))
     qkv_weight = w_qkv.transpose(1, 0, 2)
 
-    masked_bias = pl.pallas_call(
-        bias_kernel, out_shape=shape((wrows, lanes), F32), name="bias"
-    )(bias_table.T, rel_index, row(regions), shifted)
+    masked_bias = call(bias_kernel, shape((wrows, lanes), F32), smem=1)(
+        dp_index, bias_table.T, rel_index, row(regions), shifted
+    )
     forward = []
     for image in range(images):
         outs = pl.pallas_call(
@@ -521,6 +551,7 @@
                 shape((srows, inner), BF16),
             ),
             scratch_shapes=[pltpu.VMEM((wrows, inner), BF16)],
+            compiler_params=PARAMS,
         )(
             inputs, row(ln1_gain), row(ln1_shift), qkv_weight, qv_bias, masked_bias, perms[image],
             w_proj,
@@ -555,6 +586,7 @@
             shape((1, width), F32),
         ),
         scratch_shapes=[pltpu.VMEM((tokens, width), F32)],
+        compiler_params=PARAMS,
         name="mlp",
     )(
         inputs, part0, recv0, part1, recv1, row(proj_bias), row(ln2_gain), row(ln2_shift), w_fc1,
@@ -567,13 +599,14 @@
             functools.partial(mlp_grad_kernel, flip),
             in_specs=[SMEM()] + [VMEM()] * 4,
             out_shape=shape((hidden // 2, 2 * width), BF16),
-        )(core_bit, act, dub, n2, grad_output)
+            compiler_params=PARAMS,
+        )(dp_index, act, dub, n2, grad_output)
 
     send = mlp_grad(1)
     keep = mlp_grad(0)
-    mlp_shard = reduce_scatter(keep, send, bits, dp_size)
+    mlp_shard = reduce_scatter(keep, send, bits, dp_size, dp_index)
     mlp_part = pl.pallas_call(
-        mlp_out_kernel, out_shape=shape((tokens, width), BF16), name="mlp_out"
+        mlp_out_kernel, out_shape=shape((tokens, width), BF16), compiler_params=PARAMS, name="mlp_out"
     )(act, w_fc2)
 
     backward = []
@@ -592,6 +625,7 @@
                 pltpu.VMEM((wrows, inner), BF16),
                 pltpu.VMEM((wrows, 3 * inner), BF16),
             ],
+            compiler_params=PARAMS,
         )(
             grad_output, back_two_part, back_two_recv, h1, row(ln2_gain), w_proj, qkvw, prob,
             perms[image], qkv_weight,
@@ -605,28 +639,31 @@
             functools.partial(attn_grad_kernel, flip),
             in_specs=[SMEM()] + [VMEM()] * 8,
             out_shape=shape((width // 2, 3 * inner + inner), BF16),
-        )(core_bit, n1a, n1b, dp0, dp1, otok0, otok1, dhb0, dhb1)
+            compiler_params=PARAMS,
+        )(dp_index, n1a, n1b, dp0, dp1, otok0, otok1, dhb0, dhb1)
 
     send = attn_grad(1)
     keep = attn_grad(0)
-    attn_shard = reduce_scatter(keep, send, bits, dp_size)
+    attn_shard = reduce_scatter(keep, send, bits, dp_size, dp_index)
 
     table_sum = pl.pallas_call(
         table_kernel,
         out_shape=shape((heads, table_pad), F32),
         scratch_shapes=[pltpu.VMEM((table_pad, lanes), F32), pltpu.VMEM((PAD, lanes), F32)],
+        compiler_params=PARAMS,
         name="table",
     )(dsum0, dsum1, rel_index, group)
 
     mlp_recv = tensor_swap(mlp_part)
     output = pl.pallas_call(
-        output_kernel, out_shape=shape((tokens, width), BF16), name="output"
+        output_kernel, out_shape=shape((tokens, width), BF16), compiler_params=PARAMS, name="output"
     )(h1, mlp_part, mlp_recv, row(fc2_bias))
 
     small_rows = 7 + hidden // width + heads
     grad_input, small = pl.pallas_call(
         input_grad_kernel,
         out_shape=(shape((tokens, width), F32), shape((small_rows, width), F32)),
+        compiler_params=PARAMS,
         name="input_grad",
     )(
         inputs, back0, back_recv0, back1, back_recv1, dh0, dh1, row(ln1_gain), sums0, sums1,
@@ -645,25 +682,30 @@
             shape((1, hidden), F32),
             shape((heads, table_rows), F32),
         ),
+        compiler_params=PARAMS,
         name="small",
     )(small, recv)
     grad_gain1, grad_shift1, grad_gain2, grad_shift2, grad_pb, grad_qvb, grad_b2, grad_b1 = smalls[:8]
 
     down = bits[::-1]
-    mine, other = gather_back(mlp_shard, down, dp_size, False)
+    mine, other = gather_back(mlp_shard, down, dp_size, dp_index)
     grad_fc2, grad_fc1 = pl.pallas_call(
-        functools.partial(mlp_finish_kernel, down[:-1]),
+        mlp_finish_kernel,
         in_specs=[SMEM()] + [VMEM()] * 2,
         out_shape=(shape((hidden, width), F32), shape((width, hidden), F32)),
+        compiler_params=PARAMS,
         name="mlp_finish",
     )(dp_index, mine, other)
-    mine, other = gather_back(attn_shard, down[:-3] + [down[-2], down[-3], down[-1]], dp_size, True)
+    mine, other = gather_back(
+        attn_shard, down[:-3] + [down[-2], down[-3], down[-1]], dp_size, dp_index
+    )
     grad_qkv, grad_proj = pl.pallas_call(
         attn_finish_kernel,
         in_specs=[SMEM()] + [VMEM()] * 2,
         out_shape=(shape((3, width, inner), F32), shape((inner, width), F32)),
+        compiler_params=PARAMS,
         name="attn_finish",
-    )(core_bit, mine, other)
+    )(dp_index, mine, other)
 
     flat = lambda v: v.reshape(-1)
     return (

time: 186 us -> 175 us (0.941)
  Pallas kernels: 68.2 us -> 33.9 us
  waiting for transfers between devices: 79.1 us -> 108 us
  starting transfers between devices: 29 us -> 22 us
  local copies, waits for them, and re-layouts: 3.99 us -> 9.18 us
  other arithmetic: 3.96 us -> 0.03 us
    ppermute x26, waiting for transfers between devices: 79.1 us -> 108 us  [swap(): return lax.ppermute(value, axis, [(i, i ^ bit) for i in range(size)])]
    ppermute x26, starting transfers between devices: 29 us -> 22 us  [swap(): return lax.ppermute(value, axis, [(i, i ^ bit) for i in range(size)])]
    pallas_call x4 -> x18, Pallas kernels: 11.3 us -> 5.18 us  [the longest x1 2.22 us: local(): pl.pallas_call(mlp_finish_kernel, in_specs=[SMEM()] + [VMEM()] * 2, out_s...]
    pallas_call x2, Pallas kernels: 13.6 us -> 7.96 us  [local(): pl.pallas_call(functools.partial(attn_backward_kernel, image), out_shape=...]
    unnamed x20 -> x54, local copies, waits for them, and re-layouts: 3.99 us -> 9.18 us
    pallas_call x2, Pallas kernels: 6.67 us -> 1.49 us  [mlp_grad(): pl.pallas_call(functools.partial(mlp_grad_kernel, flip), in_specs=[SMEM()...]
    pallas_call x2, Pallas kernels: 5.47 us -> 0.95 us  [attn_grad(): pl.pallas_call(functools.partial(attn_grad_kernel, flip), in_specs=[SMEM(...]
    pallas_call x2, Pallas kernels: 12.1 us -> 7.6 us  [local(): pl.pallas_call(functools.partial(attn_forward_kernel, image), out_shape=(...]
  transfers between devices with their start and end apart: 26 -> 26, of which waited for: 18 -> 19; matrix products, arithmetic and copies ran while one was open for 2% -> 0% of each run, Pallas kernels for 25% -> 13%
where the time goes in v4:
time: 175 us
  waiting for transfers between devices  108 us (62%)
  Pallas kernels  33.9 us (19%)
  starting transfers between devices  22 us (13%)
  local copies, waits for them, and re-layouts  9.18 us (5%)
    ppermute x26, waiting for transfers between devices, swap(): return lax.ppermute(value, axis, [(i, i ^ bit) for i in range(size)])  108 us
    ppermute x26, starting transfers between devices, swap(): return lax.ppermute(value, axis, [(i, i ^ bit) for i in range(size)])  22 us
    unnamed x54, local copies, waits for them, and re-layouts  9.18 us
    pallas_call x2, Pallas kernels, local(): pl.pallas_call(functools.partial(attn_backward_kernel, image), out_shape=...  7.96 us
    pallas_call x2, Pallas kernels, local(): pl.pallas_call(functools.partial(attn_forward_kernel, image), out_shape=(...  7.6 us
    pallas_call x1, Pallas kernels, local(): pl.pallas_call(mlp_kernel, grid=(steps,), in_specs=[full((tokens, width))...  3.56 us
    pallas_call x1, Pallas kernels, local(): pl.pallas_call(table_kernel, out_shape=shape((heads, table_pad), F32), sc...  3.5 us
  transfers between devices with their start and end apart: 26, of which 19 were waited for; matrix products, arithmetic and copies ran while one was open for 0% of the time, Pallas kernels for 13%

profile of v4, /device:TPU:0, one launch (start us, length us, event | category | flops | bytes accessed | tf_op | source)
XLA Modules:
  0.0 174.6 jit_solution(14708204729153856995)
XLA Ops:
  10.4 3.8 %shard_map.318 = (bf16[200,512]{1,0:T(8,128)(2,1)S(1)}, bf16[200,512]{1,0:T(8,128)(2,1)S(1)}, bf16[256,768]{1,0:T(8,128)(2,1)S(1)}, f32[256,512]{1,0:T(8,128)S(1)}, bf16[200,256]{1,0:T(8,128)(2,1)S(1)}) custom-call(bf16[392,512]{1,0:T(8,128)(2,1)S(1)} %copy-done.3, f32[1,512]{1,0:T(1,128)S(1)} %bitcast.27, f32[1,512]{1,0:T(1,128)S(1)} %bitcast.31, ...), custom_call_target="tpu_custom_call" | custom-call | tf_op jit(solution)/shard_map/pallas_call | solution.py:544
  14.2 3.1 %collective-permute-start.1 = (bf16[200,512]{1,0:T(8,128)(2,1)S(1)}, bf16[200,512]{1,0:T(8,128)(2,1)S(1)}, u32[]{:S(2)}, u32[]{:S(2)}) collective-permute-start(bf16[200,512]{1,0:T(8,128)(2,1)S(1)} %get-tuple-element.72.own1_ref), channel_id=1, source_target_pairs={{0,1},{1,0},{2,3},{3,2},{4,5},{5,4},{6,7},{7,6},{8,9},{9,8},{10,11... | collective-permute-start | bytes 614408 | tf_op jit(solution)/shard_map/ppermute | solution.py:447
  17.3 3.8 %shard_map.317 = (bf16[200,512]{1,0:T(8,128)(2,1)S(1)}, bf16[200,512]{1,0:T(8,128)(2,1)S(1)}, bf16[256,768]{1,0:T(8,128)(2,1)S(1)}, f32[256,512]{1,0:T(8,128)S(1)}, bf16[200,256]{1,0:T(8,128)(2,1)S(1)}) custom-call(bf16[392,512]{1,0:T(8,128)(2,1)S(1)} %copy-done.3, f32[1,512]{1,0:T(1,128)S(1)} %bitcast.28, f32[1,512]{1,0:T(1,128)S(1)} %bitcast.32, ...), custom_call_target="tpu_custom_call" | custom-call | tf_op jit(solution)/shard_map/pallas_call | solution.py:544
  22.4 5.3 %collective-permute-done.recv0_ref = bf16[200,512]{1,0:T(8,128)(2,1)S(1)} collective-permute-done((bf16[200,512]{1,0:T(8,128)(2,1)S(1)}, bf16[200,512]{1,0:T(8,128)(2,1)S(1)}, u32[]{:S(2)}, u32[]{:S(2)}) %collective-permute-start) | collective-permute-done | bytes 204832 | tf_op jit(solution)/shard_map/ppermute | solution.py:447
  27.8 3.6 %mlp.1 = (bf16[392,512]{1,0:T(8,128)(2,1)S(1)}, f32[392,512]{1,0:T(8,128)S(1)}, bf16[392,512]{1,0:T(8,128)(2,1)S(1)}, bf16[392,1024]{1,0:T(8,128)(2,1)S(1)}, bf1...) custom-call(bf16[392,512]{1,0:T(8,128)(2,1)S(1)} %copy-done.4, ...), custom_call_target="tpu_custom_call" | custom-call | tf_op jit(solution)/shard_map/mlp/pallas_call | solution.py:566
  32.9 1.9 %collective-permute-done.18.recv_ref = bf16[512,1024]{1,0:T(8,128)(2,1)S(1)} collective-permute-done((bf16[512,1024]{1,0:T(8,128)(2,1)S(1)}, bf16[512,1024]{1,0:T(8,128)(2,1)S(1)}, u32[]{:S(2)}, u32[]{:S(2)}) %collective-permute-start.18) | collective-permute-done | bytes 1048608 | tf_op jit(solution)/shard_map/ppermute | solution.py:447
  35.0 1.6 collective-permute-start.19
  37.4 11.7 %collective-permute-done.19.recv_ref = bf16[256,1024]{1,0:T(8,128)(2,1)S(1)} collective-permute-done((bf16[256,1024]{1,0:T(8,128)(2,1)S(1)}, bf16[256,1024]{1,0:T(8,128)(2,1)S(1)}, u32[]{:S(2)}, u32[]{:S(2)}) %collective-permute-start.19) | collective-permute-done | bytes 524320 | tf_op jit(solution)/shard_map/ppermute | solution.py:447
  49.2 1.6 collective-permute-start.20
  50.8 5.9 %collective-permute-done.20.recv_ref = bf16[128,1024]{1,0:T(8,128)(2,1)S(1)} collective-permute-done((bf16[128,1024]{1,0:T(8,128)(2,1)S(1)}, bf16[128,1024]{1,0:T(8,128)(2,1)S(1)}, u32[]{:S(2)}, u32[]{:S(2)}) %collective-permute-start.20) | collective-permute-done | bytes 262176 | tf_op jit(solution)/shard_map/ppermute | solution.py:447
  56.8 2.7 %collective-permute-start.21 = (bf16[64,1024]{1,0:T(8,128)(2,1)S(1)}, bf16[64,1024]{1,0:T(8,128)(2,1)S(1)}, u32[]{:S(2)}, u32[]{:S(2)}) collective-permute-start(bf16[64,1024]{1,0:T(8,128)(2,1)S(1)} %get-tuple-element.122), channel_id=1, source_target_pairs={{0,16},{2,18},{4,20},{6,22},{8,24},{10,26},{12,28},{14,30},{16,0},... | collective-permute-start | bytes 393224 | tf_op jit(solution)/shard_map/ppermute | solution.py:447
  59.5 4.0 %shard_map.320 = (bf16[200,512]{1,0:T(8,128)(2,1)S(1)}, f32[200,512]{1,0:T(8,128)S(1)}, bf16[200,512]{1,0:T(8,128)(2,1)S(1)}, bf16[200,768]{1,0:T(8,128)(2,1)S(1...) custom-call(bf16[392,512]{1,0:T(8,128)(2,1)S(1)} %copy-done.2, bf16[392,512]{1,0:T(8,128)(2,1)S(1)} %get-tuple-element.75.own_ref, ...), custom_call_target="tpu_custom_call" | custom-call | tf_op jit(solution)/shard_map/pallas_call | solution.py:614
  63.5 4.0 %shard_map.319 = (bf16[200,512]{1,0:T(8,128)(2,1)S(1)}, f32[200,512]{1,0:T(8,128)S(1)}, bf16[200,512]{1,0:T(8,128)(2,1)S(1)}, bf16[200,768]{1,0:T(8,128)(2,1)S(1...) custom-call(bf16[392,512]{1,0:T(8,128)(2,1)S(1)} %copy-done.2, bf16[392,512]{1,0:T(8,128)(2,1)S(1)} %get-tuple-element.75.own_ref, ...), custom_call_target="tpu_custom_call" | custom-call | tf_op jit(solution)/shard_map/pallas_call | solution.py:614
  68.5 9.3 %collective-permute-done.22.other_ref = bf16[64,1024]{1,0:T(8,128)(2,1)S(1)} collective-permute-done((bf16[64,1024]{1,0:T(8,128)(2,1)S(1)}, bf16[64,1024]{1,0:T(8,128)(2,1)S(1)}, u32[]{:S(2)}, u32[]{:S(2)}) %collective-permute-start.22) | collective-permute-done | bytes 131104 | tf_op jit(solution)/shard_map/ppermute | solution.py:447
  77.9 7.8 %collective-permute-done.23.other_ref = bf16[128,1024]{1,0:T(8,128)(2,1)S(1)} collective-permute-done((bf16[128,1024]{1,0:T(8,128)(2,1)S(1)}, bf16[128,1024]{1,0:T(8,128)(2,1)S(1)}, u32[]{:S(2)}, u32[]{:S(2)}) %collective-permute-start.23) | collective-permute-done | bytes 262176 | tf_op jit(solution)/shard_map/ppermute | solution.py:447
  85.7 1.6 collective-permute-start.24
  88.5 15.5 %collective-permute-done.11.recv_ref = bf16[128,1024]{1,0:T(8,128)(2,1)S(1)} collective-permute-done((bf16[128,1024]{1,0:T(8,128)(2,1)S(1)}, bf16[128,1024]{1,0:T(8,128)(2,1)S(1)}, u32[]{:S(2)}, u32[]{:S(2)}) %collective-permute-start.11) | collective-permute-done | bytes 262176 | tf_op jit(solution)/shard_map/ppermute | solution.py:447
  104.7 4.4 %collective-permute-done.12.recv_ref = bf16[64,1024]{1,0:T(8,128)(2,1)S(1)} collective-permute-done((bf16[64,1024]{1,0:T(8,128)(2,1)S(1)}, bf16[64,1024]{1,0:T(8,128)(2,1)S(1)}, u32[]{:S(2)}, u32[]{:S(2)}) %collective-permute-start.12) | collective-permute-done | bytes 131104 | tf_op jit(solution)/shard_map/ppermute | solution.py:447
  110.6 4.8 %collective-permute-done.13.right_ref = bf16[32,1024]{1,0:T(8,128)(2,1)S(1)} collective-permute-done((bf16[32,1024]{1,0:T(8,128)(2,1)S(1)}, bf16[32,1024]{1,0:T(8,128)(2,1)S(1)}, u32[]{:S(2)}, u32[]{:S(2)}) %collective-permute-start.13) | collective-permute-done | bytes 65568 | tf_op jit(solution)/shard_map/ppermute | solution.py:447
  115.8 5.5 %collective-permute-done.14.other_ref = bf16[32,1024]{1,0:T(8,128)(2,1)S(1)} collective-permute-done((bf16[32,1024]{1,0:T(8,128)(2,1)S(1)}, bf16[32,1024]{1,0:T(8,128)(2,1)S(1)}, u32[]{:S(2)}, u32[]{:S(2)}) %collective-permute-start.14) | collective-permute-done | bytes 65568 | tf_op jit(solution)/shard_map/ppermute | solution.py:447
  121.3 1.6 collective-permute-start.15
  122.9 3.5 %collective-permute-done.15.other_ref = bf16[64,1024]{1,0:T(8,128)(2,1)S(1)} collective-permute-done((bf16[64,1024]{1,0:T(8,128)(2,1)S(1)}, bf16[64,1024]{1,0:T(8,128)(2,1)S(1)}, u32[]{:S(2)}, u32[]{:S(2)}) %collective-permute-start.15) | collective-permute-done | bytes 131104 | tf_op jit(solution)/shard_map/ppermute | solution.py:447
  126.5 6.4 %collective-permute-done.16.other_ref = bf16[128,1024]{1,0:T(8,128)(2,1)S(1)} collective-permute-done((bf16[128,1024]{1,0:T(8,128)(2,1)S(1)}, bf16[128,1024]{1,0:T(8,128)(2,1)S(1)}, u32[]{:S(2)}, u32[]{:S(2)}) %collective-permute-start.16) | collective-permute-done | bytes 262176 | tf_op jit(solution)/shard_map/ppermute | solution.py:447
  136.4 3.5 %table.1.tab_ref = f32[8,176]{1,0:T(8,128)S(1)} custom-call(f32[64,512]{1,0:T(8,128)S(1)} %get-tuple-element.88.dsa_ref, f32[64,512]{1,0:T(8,128)S(1)} %get-tuple-element.89.dsb_ref, s32[49,49]{1,0:T(8,128)S(1)} %copy-done.14, f32[8,512]{1,0:T(8,128)S(1)} %copy-done.18), custom_call_target="tpu_custom_call" | custom-call | tf_op jit(solution)/shard_map/table/pallas_call | solution.py:649
  139.9 10.2 %collective-permute-done.5.recv1_ref = bf16[200,512]{1,0:T(8,128)(2,1)S(1)} collective-permute-done((bf16[200,512]{1,0:T(8,128)(2,1)S(1)}, bf16[200,512]{1,0:T(8,128)(2,1)S(1)}, u32[]{:S(2)}, u32[]{:S(2)}) %collective-permute-start.5) | collective-permute-done | bytes 204832 | tf_op jit(solution)/shard_map/ppermute | solution.py:447
  150.2 3.9 %collective-permute-done.4.recv0_ref = bf16[200,512]{1,0:T(8,128)(2,1)S(1)} collective-permute-done((bf16[200,512]{1,0:T(8,128)(2,1)S(1)}, bf16[200,512]{1,0:T(8,128)(2,1)S(1)}, u32[]{:S(2)}, u32[]{:S(2)}) %collective-permute-start.4) | collective-permute-done | bytes 204832 | tf_op jit(solution)/shard_map/ppermute | solution.py:447
  154.1 1.6 input_grad.1
  156.9 1.6 collective-permute-start.7
  158.5 2.6 %collective-permute-done.7 = f32[17,512]{1,0:T(8,128)S(1)} collective-permute-done((f32[17,512]{1,0:T(8,128)S(1)}, f32[17,512]{1,0:T(8,128)S(1)}, u32[]{:S(2)}, u32[]{:S(2)}) %collective-permute-start.7) | collective-permute-done | bytes 34848 | tf_op jit(solution)/shard_map/ppermute | solution.py:447
  161.2 4.1 %collective-permute-done.8 = f32[17,512]{1,0:T(8,128)S(1)} collective-permute-done((f32[17,512]{1,0:T(8,128)S(1)}, f32[17,512]{1,0:T(8,128)S(1)}, u32[]{:S(2)}, u32[]{:S(2)}) %collective-permute-start.8) | collective-permute-done | bytes 34848 | tf_op jit(solution)/shard_map/ppermute | solution.py:447
  167.0 3.3 %collective-permute-done.9.right_ref = f32[17,512]{1,0:T(8,128)S(1)} collective-permute-done((f32[17,512]{1,0:T(8,128)S(1)}, f32[17,512]{1,0:T(8,128)S(1)}, u32[]{:S(2)}, u32[]{:S(2)}) %collective-permute-start.9) | collective-permute-done | bytes 34848 | tf_op jit(solution)/shard_map/ppermute | solution.py:447
  172.4 2.2 %mlp_finish.1 = (f32[1024,512]{1,0:T(8,128)}, f32[512,1024]{1,0:T(8,128)}) custom-call(s32[1]{0:T(128)} %bitcast.3.index_ref, bf16[512,1024]{1,0:T(8,128)(2,1)S(1)} %shard_map.338.mine_ref, bf16[512,1024]{1,0:T(8,128)(2,1)S(1)} %collective-permute-done.25.other_ref), custom_call_target="tpu_custom_call" | custom-call | tf_op jit(solution)/shard_map/mlp_finish/pallas_call | solution.py:692
  (108 shorter events, 27.5 us)
Async XLA Ops:
  14.2 8.1 %collective-permute-start.1 = (bf16[200,512]{1,0:T(8,128)(2,1)S(1)}, bf16[200,512]{1,0:T(8,128)(2,1)S(1)}, u32[]{:S(2)}, u32[]{:S(2)}) collective-permute-start(bf16[200,512]{1,0:T(8,128)(2,1)S(1)} %get-tuple-element.72.own1_ref), channel_id=1, source_target_pairs={{0,1},{1,0},{2,3},{3,2},{4,5},{5,4},{6,7},{7,6},{8,9},{9,8},{10,11... | collective-permute-start | bytes 614408 | tf_op jit(solution)/shard_map/ppermute | solution.py:447
  21.1 6.6 %collective-permute-start = (bf16[200,512]{1,0:T(8,128)(2,1)S(1)}, bf16[200,512]{1,0:T(8,128)(2,1)S(1)}, u32[]{:S(2)}, u32[]{:S(2)}) collective-permute-start(bf16[200,512]{1,0:T(8,128)(2,1)S(1)} %get-tuple-element.71.own0_ref), channel_id=1, source_target_pairs={{0,1},{1,0},{2,3},{3,2},{4,5},{5,4},{6,7},{7,6},{8,9},{9,8},{10,11... | collective-permute-start | bytes 614408 | tf_op jit(solution)/shard_map/ppermute | solution.py:447
  32.1 2.7 %collective-permute-start.18 = (bf16[512,1024]{1,0:T(8,128)(2,1)S(1)}, bf16[512,1024]{1,0:T(8,128)(2,1)S(1)}, u32[]{:S(2)}, u32[]{:S(2)}) collective-permute-start(bf16[512,1024]{1,0:T(8,128)(2,1)S(1)} %shard_map.331), channel_id=1, source_target_pairs={{0,2},{2,0},{4,6},{6,4},{8,10},{10,8},{12,14},{14,12},{16,18},{18,... | collective-permute-start | bytes 3145736 | tf_op jit(solution)/shard_map/ppermute | solution.py:447
  32.9 26.6 %copy-start.1 = (bf16[512,3,256]{2,0,1:T(8,128)(2,1)S(1)}, bf16[512,3,256]{2,0,1:T(8,128)(2,1)}, u32[]{:S(2)}) copy-start(bf16[512,3,256]{2,0,1:T(8,128)(2,1)} %param.24) | copy-start | bytes 2359300
  32.9 26.6 %copy-start.11 = (bf16[256,200]{1,0:T(8,128)(2,1)S(1)}, bf16[256,200]{1,0:T(8,128)(2,1)}, u32[]{:S(2)}) copy-start(bf16[256,200]{1,0:T(8,128)(2,1)} %constant.15.clone.perm_ref) | copy-start | bytes 307204
  35.0 14.0 %collective-permute-start.19 = (bf16[256,1024]{1,0:T(8,128)(2,1)S(1)}, bf16[256,1024]{1,0:T(8,128)(2,1)S(1)}, u32[]{:S(2)}, u32[]{:S(2)}) collective-permute-start(bf16[256,1024]{1,0:T(8,128)(2,1)S(1)} %get-tuple-element.118), channel_id=1, source_target_pairs={{0,4},{2,6},{4,0},{6,2},{8,12},{10,14},{12,8},{14,10},{16,20},{18,... | collective-permute-start | bytes 1572872 | tf_op jit(solution)/shard_map/ppermute | solution.py:447
  36.6 22.9 %collective-permute-start.3 = (bf16[392,512]{1,0:T(8,128)(2,1)S(1)}, bf16[392,512]{1,0:T(8,128)(2,1)S(1)}, u32[]{:S(2)}, u32[]{:S(2)}) collective-permute-start(bf16[392,512]{1,0:T(8,128)(2,1)S(1)} %get-tuple-element.75.own_ref), channel_id=1, source_target_pairs={{0,1},{1,0},{2,3},{3,2},{4,5},{5,4},{6,7},{7,6},{8,9},{9,8},{10,11... | collective-permute-start | bytes 1204232 | tf_op jit(solution)/shard_map/ppermute | solution.py:447
  49.2 7.6 %collective-permute-start.20 = (bf16[128,1024]{1,0:T(8,128)(2,1)S(1)}, bf16[128,1024]{1,0:T(8,128)(2,1)S(1)}, u32[]{:S(2)}, u32[]{:S(2)}) collective-permute-start(bf16[128,1024]{1,0:T(8,128)(2,1)S(1)} %get-tuple-element.120), channel_id=1, source_target_pairs={{0,8},{2,10},{4,12},{6,14},{8,0},{10,2},{12,4},{14,6},{16,24},{18,... | collective-permute-start | bytes 786440 | tf_op jit(solution)/shard_map/ppermute | solution.py:447
  56.8 11.2 %collective-permute-start.21 = (bf16[64,1024]{1,0:T(8,128)(2,1)S(1)}, bf16[64,1024]{1,0:T(8,128)(2,1)S(1)}, u32[]{:S(2)}, u32[]{:S(2)}) collective-permute-start(bf16[64,1024]{1,0:T(8,128)(2,1)S(1)} %get-tuple-element.122), channel_id=1, source_target_pairs={{0,16},{2,18},{4,20},{6,22},{8,24},{10,26},{12,28},{14,30},{16,0},... | collective-permute-start | bytes 393224 | tf_op jit(solution)/shard_map/ppermute | solution.py:447
  68.0 19.8 %collective-permute-start.10 = (bf16[256,1024]{1,0:T(8,128)(2,1)S(1)}, bf16[256,1024]{1,0:T(8,128)(2,1)S(1)}, u32[]{:S(2)}, u32[]{:S(2)}) collective-permute-start(bf16[256,1024]{1,0:T(8,128)(2,1)S(1)} %shard_map.322), channel_id=1, source_target_pairs={{0,2},{2,0},{4,6},{6,4},{8,10},{10,8},{12,14},{14,12},{16,18},{18,... | collective-permute-start | bytes 1572872 | tf_op jit(solution)/shard_map/ppermute | solution.py:447
  68.1 9.7 %collective-permute-start.22 = (bf16[64,1024]{1,0:T(8,128)(2,1)S(1)}, bf16[64,1024]{1,0:T(8,128)(2,1)S(1)}, u32[]{:S(2)}, u32[]{:S(2)}) collective-permute-start(bf16[64,1024]{1,0:T(8,128)(2,1)S(1)} %shard_map.335.mine_ref), channel_id=1, source_target_pairs={{0,16},{2,18},{4,20},{6,22},{8,24},{10,26},{12,28},{14,30},{16,0},... | collective-permute-start | bytes 393224 | tf_op jit(solution)/shard_map/ppermute | solution.py:447
  77.8 7.9 %collective-permute-start.23 = (bf16[128,1024]{1,0:T(8,128)(2,1)S(1)}, bf16[128,1024]{1,0:T(8,128)(2,1)S(1)}, u32[]{:S(2)}, u32[]{:S(2)}) collective-permute-start(bf16[128,1024]{1,0:T(8,128)(2,1)S(1)} %shard_map.336.mine_ref), channel_id=1, source_target_pairs={{0,8},{2,10},{4,12},{6,14},{8,0},{10,2},{12,4},{14,6},{16,24},{18,... | collective-permute-start | bytes 786440 | tf_op jit(solution)/shard_map/ppermute | solution.py:447
  85.7 24.7 %collective-permute-start.24 = (bf16[256,1024]{1,0:T(8,128)(2,1)S(1)}, bf16[256,1024]{1,0:T(8,128)(2,1)S(1)}, u32[]{:S(2)}, u32[]{:S(2)}) collective-permute-start(bf16[256,1024]{1,0:T(8,128)(2,1)S(1)} %shard_map.337.mine_ref), channel_id=1, source_target_pairs={{0,4},{2,6},{4,0},{6,2},{8,12},{10,14},{12,8},{14,10},{16,20},{18,... | collective-permute-start | bytes 1572872 | tf_op jit(solution)/shard_map/ppermute | solution.py:447
  87.9 16.1 %collective-permute-start.11 = (bf16[128,1024]{1,0:T(8,128)(2,1)S(1)}, bf16[128,1024]{1,0:T(8,128)(2,1)S(1)}, u32[]{:S(2)}, u32[]{:S(2)}) collective-permute-start(bf16[128,1024]{1,0:T(8,128)(2,1)S(1)} %get-tuple-element.103), channel_id=1, source_target_pairs={{0,4},{2,6},{4,0},{6,2},{8,12},{10,14},{12,8},{14,10},{16,20},{18,... | collective-permute-start | bytes 786440 | tf_op jit(solution)/shard_map/ppermute | solution.py:447
  104.1 5.0 %collective-permute-start.12 = (bf16[64,1024]{1,0:T(8,128)(2,1)S(1)}, bf16[64,1024]{1,0:T(8,128)(2,1)S(1)}, u32[]{:S(2)}, u32[]{:S(2)}) collective-permute-start(bf16[64,1024]{1,0:T(8,128)(2,1)S(1)} %get-tuple-element.105), channel_id=1, source_target_pairs={{0,8},{2,10},{4,12},{6,14},{8,0},{10,2},{12,4},{14,6},{16,24},{18,... | collective-permute-start | bytes 393224 | tf_op jit(solution)/shard_map/ppermute | solution.py:447
  109.1 6.3 %collective-permute-start.13 = (bf16[32,1024]{1,0:T(8,128)(2,1)S(1)}, bf16[32,1024]{1,0:T(8,128)(2,1)S(1)}, u32[]{:S(2)}, u32[]{:S(2)}) collective-permute-start(bf16[32,1024]{1,0:T(8,128)(2,1)S(1)} %get-tuple-element.107), channel_id=1, source_target_pairs={{0,16},{2,18},{4,20},{6,22},{8,24},{10,26},{12,28},{14,30},{16,0},... | collective-permute-start | bytes 196616 | tf_op jit(solution)/shard_map/ppermute | solution.py:447
  110.5 61.9 %collective-permute-start.25 = (bf16[512,1024]{1,0:T(8,128)(2,1)S(1)}, bf16[512,1024]{1,0:T(8,128)(2,1)S(1)}, u32[]{:S(2)}, u32[]{:S(2)}) collective-permute-start(bf16[512,1024]{1,0:T(8,128)(2,1)S(1)} %shard_map.338.mine_ref), channel_id=1, source_target_pairs={{0,2},{2,0},{4,6},{6,4},{8,10},{10,8},{12,14},{14,12},{16,18},{18,... | collective-permute-start | bytes 3145736 | tf_op jit(solution)/shard_map/ppermute | solution.py:447
  115.5 21.0 %copy-start.14 = (s32[49,49]{1,0:T(8,128)S(1)}, s32[49,49]{1,0:T(8,128)}, u32[]{:S(2)}) copy-start(s32[49,49]{1,0:T(8,128)} %rel_ref.3) | copy-start | bytes 28816
  115.5 21.0 %copy-start.18 = (f32[8,512]{1,0:T(8,128)S(1)}, f32[8,512]{1,0:T(8,128)}, u32[]{:S(2)}) copy-start(f32[8,512]{1,0:T(8,128)} %constant.17.clone.group_ref) | copy-start | bytes 49156
  115.5 5.8 %collective-permute-start.14 = (bf16[32,1024]{1,0:T(8,128)(2,1)S(1)}, bf16[32,1024]{1,0:T(8,128)(2,1)S(1)}, u32[]{:S(2)}, u32[]{:S(2)}) collective-permute-start(bf16[32,1024]{1,0:T(8,128)(2,1)S(1)} %shard_map.326.mine_ref), channel_id=1, source_target_pairs={{0,16},{2,18},{4,20},{6,22},{8,24},{10,26},{12,28},{14,30},{16,0},... | collective-permute-start | bytes 196616 | tf_op jit(solution)/shard_map/ppermute | solution.py:447
  121.3 32.8 %copy-start.17 = (f32[512]{0:T(512)S(1)}, f32[512]{0:T(512)}, u32[]{:S(2)}) copy-start(f32[512]{0:T(512)} %param.22) | copy-start | bytes 6148
  121.3 5.0 %collective-permute-start.15 = (bf16[64,1024]{1,0:T(8,128)(2,1)S(1)}, bf16[64,1024]{1,0:T(8,128)(2,1)S(1)}, u32[]{:S(2)}, u32[]{:S(2)}) collective-permute-start(bf16[64,1024]{1,0:T(8,128)(2,1)S(1)} %shard_map.327.mine_ref), channel_id=1, source_target_pairs={{0,4},{2,6},{4,0},{6,2},{8,12},{10,14},{12,8},{14,10},{16,20},{18,... | collective-permute-start | bytes 393224 | tf_op jit(solution)/shard_map/ppermute | solution.py:447
  126.4 6.4 %collective-permute-start.16 = (bf16[128,1024]{1,0:T(8,128)(2,1)S(1)}, bf16[128,1024]{1,0:T(8,128)(2,1)S(1)}, u32[]{:S(2)}, u32[]{:S(2)}) collective-permute-start(bf16[128,1024]{1,0:T(8,128)(2,1)S(1)} %shard_map.328.mine_ref), channel_id=1, source_target_pairs={{0,8},{2,10},{4,12},{6,14},{8,0},{10,2},{12,4},{14,6},{16,24},{18,... | collective-permute-start | bytes 786440 | tf_op jit(solution)/shard_map/ppermute | solution.py:447
  132.9 33.2 %copy-start.25 = (f32[512]{0:T(512)S(1)}, f32[512]{0:T(512)}, u32[]{:S(2)}) copy-start(f32[512]{0:T(512)} %param.36) | copy-start | bytes 6148
  132.9 38.1 %collective-permute-start.17 = (bf16[256,1024]{1,0:T(8,128)(2,1)S(1)}, bf16[256,1024]{1,0:T(8,128)(2,1)S(1)}, u32[]{:S(2)}, u32[]{:S(2)}) collective-permute-start(bf16[256,1024]{1,0:T(8,128)(2,1)S(1)} %shard_map.329.mine_ref), channel_id=1, source_target_pairs={{0,2},{2,0},{4,6},{6,4},{8,10},{10,8},{12,14},{14,12},{16,18},{18,... | collective-permute-start | bytes 1572872 | tf_op jit(solution)/shard_map/ppermute | solution.py:447
  133.5 32.6 %collective-permute-start.2 = (bf16[392,512]{1,0:T(8,128)(2,1)S(1)}, bf16[392,512]{1,0:T(8,128)(2,1)S(1)}, u32[]{:S(2)}, u32[]{:S(2)}) collective-permute-start(bf16[392,512]{1,0:T(8,128)(2,1)S(1)} %mlp_out.1.own_ref), channel_id=1, source_target_pairs={{0,1},{1,0},{2,3},{3,2},{4,5},{5,4},{6,7},{7,6},{8,9},{9,8},{10,11... | collective-permute-start | bytes 1204232 | tf_op jit(solution)/shard_map/ppermute | solution.py:447
  134.4 15.8 %collective-permute-start.5 = (bf16[200,512]{1,0:T(8,128)(2,1)S(1)}, bf16[200,512]{1,0:T(8,128)(2,1)S(1)}, u32[]{:S(2)}, u32[]{:S(2)}) collective-permute-start(bf16[200,512]{1,0:T(8,128)(2,1)S(1)} %get-tuple-element.81.own1_ref), channel_id=1, source_target_pairs={{0,1},{1,0},{2,3},{3,2},{4,5},{5,4},{6,7},{7,6},{8,9},{9,8},{10,11... | collective-permute-start | bytes 614408 | tf_op jit(solution)/shard_map/ppermute | solution.py:447
  135.6 18.4 %collective-permute-start.4 = (bf16[200,512]{1,0:T(8,128)(2,1)S(1)}, bf16[200,512]{1,0:T(8,128)(2,1)S(1)}, u32[]{:S(2)}, u32[]{:S(2)}) collective-permute-start(bf16[200,512]{1,0:T(8,128)(2,1)S(1)} %get-tuple-element.78.own0_ref), channel_id=1, source_target_pairs={{0,1},{1,0},{2,3},{3,2},{4,5},{5,4},{6,7},{7,6},{8,9},{9,8},{10,11... | collective-permute-start | bytes 614408 | tf_op jit(solution)/shard_map/ppermute | solution.py:447
  155.7 1.2 collective-permute-start.6
  156.9 4.2 %collective-permute-start.7 = (f32[17,512]{1,0:T(8,128)S(1)}, f32[17,512]{1,0:T(8,128)S(1)}, u32[]{:S(2)}, u32[]{:S(2)}) collective-permute-start(f32[17,512]{1,0:T(8,128)S(1)} %add.9), channel_id=1, source_target_pairs={{0,4},{2,6},{4,0},{6,2},{8,12},{10,14},{12,8},{14,10},{16,20},{18,... | collective-permute-start | bytes 104456 | tf_op jit(solution)/shard_map/ppermute | solution.py:447
  161.1 4.2 %collective-permute-start.8 = (f32[17,512]{1,0:T(8,128)S(1)}, f32[17,512]{1,0:T(8,128)S(1)}, u32[]{:S(2)}, u32[]{:S(2)}) collective-permute-start(f32[17,512]{1,0:T(8,128)S(1)} %add.10), channel_id=1, source_target_pairs={{0,8},{2,10},{4,12},{6,14},{8,0},{10,2},{12,4},{14,6},{16,24},{18,... | collective-permute-start | bytes 104456 | tf_op jit(solution)/shard_map/ppermute | solution.py:447
  165.3 5.1 %collective-permute-start.9 = (f32[17,512]{1,0:T(8,128)S(1)}, f32[17,512]{1,0:T(8,128)S(1)}, u32[]{:S(2)}, u32[]{:S(2)}) collective-permute-start(f32[17,512]{1,0:T(8,128)S(1)} %add.11.left_ref), channel_id=1, source_target_pairs={{0,16},{2,18},{4,20},{6,22},{8,24},{10,26},{12,28},{14,30},{16,0},... | collective-permute-start | bytes 104456 | tf_op jit(solution)/shard_map/ppermute | solution.py:447
  (21 other events, 181.2 us)
